TPU v7x, 256 devices: a whole 4x4x8 slice. The times are simulated.
256 devices in a mesh: seq: 16 (over x_hi, y, core), tp: 16 (over x_lo, z).
Axes of the slice: x: 4 (x_hi: 2, x_lo: 2; x = x_hi * 2 + x_lo), y: 4, z: 8, core: 2. Of those that a mesh axis runs over, the one named last changes fastest.
Arguments:
- hidden: bfloat16 [4096, 4096], P('seq', 'tp'), may hold values from -6 to 6
- norm_gain: float32 [4096], replicated, may hold values from 0.25 to 1.75
- value_weight: bfloat16 [4096, 4096], P(None, 'tp'), may hold values from -0.09375 to 0.09375
- gate_weight: bfloat16 [4096, 4096], P(None, 'tp'), may hold values from -0.09375 to 0.09375
- value_taps: float32 [3, 4096], P(None, 'tp'), may hold values from -3 to 3
- gate_taps: float32 [3, 4096], P(None, 'tp'), may hold values from -3 to 3
- rates: float32 [16, 4096], P(None, 'tp'), may hold values from 1.2207031e-05 to 0.05, as said below
- residues: float32 [16, 4096], P(None, 'tp'), may hold values from -1.5 to 1.5
- out_weight: bfloat16 [4096, 4096], P('tp'), may hold values from -0.125 to 0.125
Outputs:
- mixed: bfloat16 [4096, 4096], P('seq', 'tp')
Inputs may be any that keep to these rules, and one draw needn't show every extreme that they name: Decay rates are positive.
All inputs are finite; a program needn't handle non-finite values.
Results may differ from a plain program's by a relative error of at most 0.0076.
Values may be sent and summed in bfloat16 or wider, within the bound.
No kernel may reach another device: no remote copies, remote signals or barrier semaphores. Data moves between devices by JAX's collectives and lax.ppermute only.
A program may use at most 128 MiB of HBM per device.

v0:
```python
import functools
import jax
import jax.numpy as jnp
from jax import lax
from jax.experimental import pallas as pl
from jax.experimental.pallas import tpu as pltpu
from jax.sharding import PartitionSpec as P

eps = 1e-05
f32 = jnp.float32
bf16 = jnp.bfloat16
T = 16


def tables_kernel(rates_ref, residues_ref, pow_ref, near_ref, fore_ref, back_ref):
    rates = rates_ref[...]
    modes, chans = rates.shape
    strength = residues_ref[...] * jnp.sqrt(rates)
    for k in range(T):
        pow_ref[k] = jnp.exp(-rates * float(k))
    pow_ref[T] = jnp.exp(-rates * float(T))
    pow_ref[T + 1] = jnp.exp(rates)
    steps = lax.broadcasted_iota(jnp.int32, (T, chans), 0).astype(f32)
    total = jnp.zeros((T, chans), f32)
    for m in range(modes):
        rate = rates[m : m + 1, :]
        weight = strength[m : m + 1, :]
        fore = weight * jnp.exp(-rate * (steps + 1.0))
        fore_ref[m] = fore
        back_ref[m] = weight * jnp.exp(-rate * (float(T) - steps))
        total = total + fore
    near_ref[pl.ds(T + 1, T), :] = total
    near_ref[pl.ds(T, 1), :] = jnp.sum(strength, axis=0, keepdims=True)
    for k in range(1, T + 1):
        near_ref[pl.ds(T - k, 1), :] = total[k - 1 : k, :]


def project_kernel(
    x_ref, gain_ref, wv_ref, wg_ref, vt_ref, gt_ref, pow_ref, near_ref,
    send_ref, fore_ref, back_ref, local_ref, gates_ref,
    acc_ref, scale_ref, pad_ref, sv_ref,
):
    k = pl.program_id(0)
    blocks, rows, chans = x_ref.shape
    place = lax.axis_index("seq")
    places = lax.axis_size("seq")

    @pl.when(k == 0)
    def _():
        total = jnp.zeros((rows, chans), f32)
        for b in range(blocks):
            part = x_ref[b].astype(f32)
            total = total + part * part
        mean = jnp.sum(total, axis=1, keepdims=True) * (1.0 / (blocks * chans))
        scale_ref[...] = jnp.broadcast_to(lax.rsqrt(mean + eps), scale_ref.shape)
        acc_ref[...] = jnp.zeros_like(acc_ref)

    scale = scale_ref[:, 0:1]
    gain = gain_ref[0]
    i0 = lax.broadcasted_iota(jnp.int32, (chans, chans), 0)
    i1 = lax.broadcasted_iota(jnp.int32, (chans, chans), 1)
    flip = (i0 + i1 == chans - 1).astype(f32).astype(bf16)
    own = (x_ref[k].astype(f32) * scale * gain).astype(bf16)
    far = jnp.dot(x_ref[blocks - 1 - k], flip, preferred_element_type=f32)
    far = (far * scale * gain).astype(bf16)
    both = jnp.concatenate([own, far], axis=0)
    weight = jnp.concatenate([wv_ref[...], wg_ref[...]], axis=1)
    acc_ref[...] += jnp.dot(both, weight, preferred_element_type=f32)

    @pl.when(k == blocks - 1)
    def _():
        low_ok = (place > 0).astype(f32)
        high_ok = (place < places - 1).astype(f32)
        zeros8 = jnp.zeros((8, chans), f32)
        edges = []
        for s in range(2):
            v = acc_ref[s * rows : (s + 1) * rows, :chans].astype(bf16).astype(f32)
            pad_ref[0:8, :] = zeros8
            pad_ref[8 : 8 + rows, :] = v
            pad_ref[8 + rows : 16 + rows, :] = zeros8
            a, c = (0, 2) if s == 0 else (2, 0)
            ta, tb, tc = vt_ref[a : a + 1, :], vt_ref[1:2, :], vt_ref[c : c + 1, :]
            sv = ta * pad_ref[7 : 7 + rows, :] + tb * v + tc * pad_ref[9 : 9 + rows, :]
            sv_ref[s] = sv.reshape(rows // T, T, chans)
            low = tc * v[0:1, :] * low_ok
            high = ta * v[rows - 1 : rows, :] * high_ok
            edges.append((low, high))
            gates_ref[s] = acc_ref[s * rows : (s + 1) * rows, chans:].astype(bf16)
        tiles = rows // T
        for s in range(2):
            for g in range(chans // 128):
                lanes = slice(g * 128, (g + 1) * 128)
                low, high = edges[s][0][:, lanes], edges[s][1][:, lanes]
                inner = jnp.zeros((tiles, T, 128), f32)
                for j in range(T):
                    inner = inner + near_ref[T - j : 2 * T - j, lanes][None] * sv_ref[s, :, j : j + 1, lanes]
                local_ref[s, :, :, lanes] = inner
                fold = jnp.zeros((tiles, 16, 128), f32)
                for j in range(T):
                    fold = fold + pow_ref[T - 1 - j, :, lanes][None] * sv_ref[s, :, j : j + 1, lanes]
                jump = pow_ref[T, :, lanes]
                inverse = pow_ref[T + 1, :, lanes]
                state = jnp.broadcast_to(low, (16, 128))
                for n in range(tiles):
                    fore_ref[s, n, :, lanes] = state
                    state = jump * state + fold[n]
                ahead = state + inverse * high
                fold = jnp.zeros((tiles, 16, 128), f32)
                for j in range(T):
                    fold = fold + pow_ref[j, :, lanes][None] * sv_ref[s, :, j : j + 1, lanes]
                state = jnp.broadcast_to(high, (16, 128))
                for n in reversed(range(tiles)):
                    back_ref[s, n, :, lanes] = state
                    state = jump * state + fold[n]
                behind = state + inverse * low
                wide = slice(s * chans + g * 128, s * chans + (g + 1) * 128)
                first = jnp.broadcast_to(gates_ref[s, 0:1, lanes].astype(f32), (8, 128))
                last = jnp.broadcast_to(gates_ref[s, rows - 1 : rows, lanes].astype(f32), (8, 128))

                for i in range(places):
                    later = i > place
                    send_ref[i, 0:16, wide] = jnp.where(later, ahead, behind)
                    send_ref[i, 16:24, wide] = jnp.where(later, last, first)


def output_kernel(
    recv_ref, fore_ref, back_ref, local_ref, gates_ref, gt_ref, rates_ref, spread_f_ref, spread_b_ref,
    near_w_ref, far_w_ref, out_ref, z_ref, pad_ref, st_ref,
):
    k = pl.program_id(0)
    rows = gates_ref.shape[1]
    chans = gates_ref.shape[2]
    tiles = rows // T
    place = lax.axis_index("seq")
    places = lax.axis_size("seq")

    @pl.when(k == 0)
    def _():
        low_ok = (place > 0).astype(f32)
        high_ok = (place < places - 1).astype(f32)
        below = jnp.maximum(place - 1, 0)
        above = jnp.minimum(place + 1, places - 1)
        for s in range(2):
            wide = slice(s * chans, (s + 1) * chans)
            g = gates_ref[s].astype(f32)
            pad_ref[0:8, :] = recv_ref[below, 16:24, wide] * low_ok
            pad_ref[8 : 8 + rows, :] = g
            pad_ref[8 + rows : 16 + rows, :] = recv_ref[above, 16:24, wide] * high_ok
            a, c = (0, 2) if s == 0 else (2, 0)
            ta, tb, tc = gt_ref[a : a + 1, :], gt_ref[1:2, :], gt_ref[c : c + 1, :]
            sg = ta * pad_ref[7 : 7 + rows, :] + tb * g + tc * pad_ref[9 : 9 + rows, :]
            for g2 in range(chans // 128):
                lanes = slice(g2 * 128, (g2 + 1) * 128)
                wide = slice(s * chans + g2 * 128, s * chans + (g2 + 1) * 128)
                rates = rates_ref[:, lanes]
                hop = jnp.exp(-rates * float(rows))
                jump = jnp.exp(-rates * float(T))
                carry_f = jnp.zeros((16, 128), f32)
                carry_b = jnp.zeros((16, 128), f32)
                for j in range(places):
                    r = places - 1 - j
                    carry_f = jnp.where(j < place, carry_f * hop + recv_ref[j, 0:16, wide], carry_f)
                    carry_b = jnp.where(r > place, carry_b * hop + recv_ref[r, 0:16, wide], carry_b)
                for n in range(tiles):
                    m = tiles - 1 - n
                    st_ref[0, n] = fore_ref[s, n, :, lanes] + carry_f
                    st_ref[1, m] = back_ref[s, m, :, lanes] + carry_b
                    carry_f = carry_f * jump
                    carry_b = carry_b * jump
                conv = local_ref[s, :, :, lanes]
                for m in range(16):
                    conv = conv + spread_f_ref[m, :, lanes][None] * st_ref[0, :, m : m + 1, :]
                for m in range(16):
                    conv = conv + spread_b_ref[m, :, lanes][None] * st_ref[1, :, m : m + 1, :]
                z_ref[:, wide] = (sg[:, lanes] * conv.reshape(rows, 128)).astype(bf16)

    i0 = lax.broadcasted_iota(jnp.int32, (chans, chans), 0)
    i1 = lax.broadcasted_iota(jnp.int32, (chans, chans), 1)
    flip = (i0 + i1 == chans - 1).astype(f32).astype(bf16)
    far = jnp.dot(far_w_ref[...], flip, preferred_element_type=f32).astype(bf16)
    weight = jnp.concatenate([near_w_ref[...], far], axis=0)
    out_ref[0] = jnp.dot(z_ref[...], weight, preferred_element_type=f32).astype(bf16)


def whole(shape):
    return pl.BlockSpec(shape, lambda *_: (0,) * len(shape))


def body(
    hidden, norm_gain, value_weight, gate_weight, value_taps, gate_taps, rates, residues, out_weight
):
    rows, chans = hidden.shape
    tp = lax.axis_size("tp")
    places = lax.axis_size("seq")
    modes = rates.shape[0]
    tiles = rows // T
    shape = jax.ShapeDtypeStruct
    params = pltpu.CompilerParams(vmem_limit_bytes=48 << 20)

    powers, near, spread_f, spread_b = pl.pallas_call(
        tables_kernel,
        out_shape=(
            shape((T + 2, modes, chans), f32),
            shape((2 * T + 8, chans), f32),
            shape((modes, T, chans), f32),
            shape((modes, T, chans), f32),
        ),
        compiler_params=params,
        name="tables",
    )(rates, residues)

    blocks = lax.all_to_all(
        jnp.broadcast_to(hidden[None], (tp, rows, chans)), "tp", split_axis=0, concat_axis=0
    )
    gain = norm_gain.reshape(tp, 1, chans)
    send, fore, back, local, gates = pl.pallas_call(
        project_kernel,
        grid=(tp,),
        in_specs=[
            whole((tp, rows, chans)),
            pl.BlockSpec((1, 1, chans), lambda k: (k, 0, 0)),
            pl.BlockSpec((chans, chans), lambda k: (k, 0)),
            pl.BlockSpec((chans, chans), lambda k: (k, 0)),
            whole(value_taps.shape),
            whole(gate_taps.shape),
            whole(powers.shape),
            whole(near.shape),
        ],
        out_specs=[
            whole((places, 24, 2 * chans)),
            whole((2, tiles, modes, chans)),
            whole((2, tiles, modes, chans)),
            whole((2, tiles, T, chans)),
            whole((2, rows, chans)),
        ],
        out_shape=(
            shape((places, 24, 2 * chans), f32),
            shape((2, tiles, modes, chans), f32),
            shape((2, tiles, modes, chans), f32),
            shape((2, tiles, T, chans), f32),
            shape((2, rows, chans), bf16),
        ),
        scratch_shapes=[
            pltpu.VMEM((2 * rows, 2 * chans), f32),
            pltpu.VMEM((rows, 128), f32),
            pltpu.VMEM((rows + 16, chans), f32),
            pltpu.VMEM((2, tiles, T, chans), f32),
        ],
        compiler_params=params,
        name="project",
    )(blocks, gain, value_weight, gate_weight, value_taps, gate_taps, powers, near)

    recv = lax.all_to_all(send, "seq", split_axis=0, concat_axis=0)

    partial = pl.pallas_call(
        output_kernel,
        grid=(tp,),
        in_specs=[
            whole(recv.shape),
            whole(fore.shape),
            whole(back.shape),
            whole(local.shape),
            whole(gates.shape),
            whole(gate_taps.shape),
            whole(rates.shape),
            whole(spread_f.shape),
            whole(spread_b.shape),
            pl.BlockSpec((chans, chans), lambda k: (0, k)),
            pl.BlockSpec((chans, chans), lambda k: (0, tp - 1 - k)),
        ],
        out_specs=pl.BlockSpec((1, rows, chans), lambda k: (k, 0, 0)),
        out_shape=shape((tp, rows, chans), bf16),
        scratch_shapes=[
            pltpu.VMEM((rows, 2 * chans), bf16),
            pltpu.VMEM((rows + 16, chans), f32),
            pltpu.VMEM((2, tiles, modes, 128), f32),
        ],
        compiler_params=params,
        name="output",
    )(recv, fore, back, local, gates, gate_taps, rates, spread_f, spread_b, out_weight, out_weight)

    parts = lax.all_to_all(partial, "tp", split_axis=0, concat_axis=0)
    return jnp.sum(parts.astype(f32), axis=0).astype(bf16)


def solution(mesh):
    in_specs = (
        P("seq", "tp"),
        P(),
        P(None, "tp"),
        P(None, "tp"),
        P(None, "tp"),
        P(None, "tp"),
        P(None, "tp"),
        P(None, "tp"),
        P("tp", None),
    )
    out_specs = P("seq", "tp")
    return jax.shard_map(body, mesh=mesh, in_specs=in_specs, out_specs=out_specs, check_vma=False)
```

profile of v0, /device:TPU:4, one launch (start us, length us, event | category | flops | bytes accessed | tf_op | source)
XLA Modules:
  0.0 165.2 jit_solution(8575151140237146220)
XLA Ops:
  0.0 2.5 %broadcast_in_dim.2 = bf16[16,256,256]{2,1,0:T(8,128)(2,1)} broadcast(bf16[256,256]{1,0:T(8,128)(2,1)} %param.9), dimensions={1,2} | broadcast | bytes 2228224 | tf_op jit(solution)/shard_map/broadcast_in_dim | solution.py:213
  2.5 0.0 copy-start
  2.5 0.0 copy-start.3
  2.5 0.0 copy-start.1
  2.5 0.0 copy-start.2
  2.5 0.0 copy-start.4
  2.5 9.3 %all-to-all-start = ((bf16[16,256,256]{2,1,0:T(8,128)(2,1)}), bf16[16,256,256]{2,1,0:T(8,128)(2,1)S(1)}, u32[]{:S(2)}, u32[]{:S(2)}) async-start(bf16[16,256,256]{2,1,0:T(8,128)(2,1)} %broadcast_in_dim.2), calls=%async_computation | async-start | bytes 4194304 | tf_op jit(solution)/shard_map/all_to_all | solution.py:212
  11.8 0.0 copy-done
  11.8 0.0 copy-done.3
  11.9 0.1 tables.1
  12.0 48.8 %all-to-all-done.x_ref = bf16[16,256,256]{2,1,0:T(8,128)(2,1)S(1)} async-done(((bf16[16,256,256]{2,1,0:T(8,128)(2,1)}), bf16[16,256,256]{2,1,0:T(8,128)(2,1)S(1)}, u32[]{:S(2)}, u32[]{:S(2)}) %all-to-all-start) | async-done | bytes 2097184 | tf_op jit(solution)/shard_map/all_to_all | solution.py:212
  60.8 0.0 copy-done.1
  60.8 0.0 copy-done.2
  60.8 0.0 copy-done.4
  60.8 15.1 %project.1 = (f32[16,24,512]{2,1,0:T(8,128)S(1)}, f32[2,16,16,256]{3,2,1,0:T(8,128)S(1)}, f32[2,16,16,256]{3,2,1,0:T(8,128)S(1)}, f32[2,16,16,256]{3,2,1,0:T(8,128)S(1)}, bf16[2,256,256]{2,1,0:T(8,128)(2,1)S(1)}) custom-call(bf16[16,256,256]{2,1,0:T(8,128)(2,1)S(1)} %all-to-all-done.x_ref, f32[16,1,256]{2,1,0:T(1,128)S(1)} %bitcast.1, ...), custom_call_target="tpu_custom_call" | custom-call | tf_op jit(solution)/shard_map/project/pallas_call | solution.py:216
  75.9 19.6 %all_to_all.15.recv_ref = f32[16,24,512]{2,1,0:T(8,128)S(1)} all-to-all(f32[16,24,512]{2,1,0:T(8,128)S(1)} %get-tuple-element.16), channel_id=1, replica_groups=mesh['seq'=16,'tp'=16] {'seq'}, dimensions={0} | all-to-all | bytes 1572864 | tf_op jit(solution)/shard_map/all_to_all | solution.py:253
  95.6 13.9 %output.1 = bf16[16,256,256]{2,1,0:T(8,128)(2,1)S(1)} custom-call(f32[16,24,512]{2,1,0:T(8,128)S(1)} %all_to_all.15.recv_ref, f32[2,16,16,256]{3,2,1,0:T(8,128)S(1)} %get-tuple-element.17.fore_ref, f32[2,16,16,256]{3,2,1,0:T(8,128)S(1)} %get-tuple-element.18.back_ref, f32[2,16,16,256]{3,2,1,0:T(8,128)S(1)} %get-tuple-element.19.local_ref, ...), custom_call_target="tpu_custom_call" | custom-call | tf_op jit(solution)/shard_map/output/pallas_call | solution.py:255
  109.4 54.8 %all_to_all.16 = bf16[16,256,256]{2,1,0:T(8,128)(2,1)S(1)} all-to-all(bf16[16,256,256]{2,1,0:T(8,128)(2,1)S(1)} %output.1), channel_id=1, replica_groups=mesh['seq'=16,'tp'=16] {'tp'}, dimensions={0} | all-to-all | bytes 4194304 | tf_op jit(solution)/shard_map/all_to_all | solution.py:282
  164.2 1.0 reduce_sum.12
Async XLA Ops:
  2.5 9.4 %copy-start = (f32[16,256]{1,0:T(8,128)S(1)}, f32[16,256]{1,0:T(8,128)}, u32[]{:S(2)}) copy-start(f32[16,256]{1,0:T(8,128)} %rates_ref.3) | copy-start | bytes 49156
  2.5 9.4 %copy-start.3 = (f32[16,256]{1,0:T(8,128)S(1)}, f32[16,256]{1,0:T(8,128)}, u32[]{:S(2)}) copy-start(f32[16,256]{1,0:T(8,128)} %residues_ref.1) | copy-start | bytes 49156
  2.5 58.4 %copy-start.1 = (f32[4096]{0:T(1024)S(1)}, f32[4096]{0:T(1024)}, u32[]{:S(2)}) copy-start(f32[4096]{0:T(1024)} %param.10) | copy-start | bytes 49156
  2.5 58.4 %copy-start.2 = (f32[3,256]{1,0:T(4,128)S(1)}, f32[3,256]{1,0:T(4,128)}, u32[]{:S(2)}) copy-start(f32[3,256]{1,0:T(4,128)} %gt_ref.3) | copy-start | bytes 9220
  2.5 58.4 %copy-start.4 = (f32[3,256]{1,0:T(4,128)S(1)}, f32[3,256]{1,0:T(4,128)}, u32[]{:S(2)}) copy-start(f32[3,256]{1,0:T(4,128)} %vt_ref.1) | copy-start | bytes 9220
  2.5 58.3 %all-to-all-start = ((bf16[16,256,256]{2,1,0:T(8,128)(2,1)}), bf16[16,256,256]{2,1,0:T(8,128)(2,1)S(1)}, u32[]{:S(2)}, u32[]{:S(2)}) async-start(bf16[16,256,256]{2,1,0:T(8,128)(2,1)} %broadcast_in_dim.2), calls=%async_computation | async-start | bytes 4194304 | tf_op jit(solution)/shard_map/all_to_all | solution.py:212
where the time goes:
time: 167 us; the launch traced here: 165 us
  blocking collectives  74.4 us (45%)
  waiting for transfers between devices  48.8 us (29%)
  Pallas kernels  29.1 us (17%)
  starting transfers between devices  9.35 us (6%)
  local copies, waits for them, and re-layouts  2.48 us (1%)
    all_to_all x1, blocking collectives, body(): parts = lax.all_to_all(partial, 'tp', split_axis=0, concat_axis=0)  54.8 us
    all_to_all x1, waiting for transfers between devices, body(): lax.all_to_all(jnp.broadcast_to(hidden[None], (tp, rows, chans)), 'tp', s...  48.8 us
    all_to_all x1, blocking collectives, body(): recv = lax.all_to_all(send, 'seq', split_axis=0, concat_axis=0)  19.6 us
    pallas_call x1, Pallas kernels, body(): pl.pallas_call(project_kernel, grid=(tp,), in_specs=[whole((tp, rows, cha...  15.1 us
    pallas_call x1, Pallas kernels, body(): pl.pallas_call(output_kernel, grid=(tp,), in_specs=[whole(recv.shape), wh...  13.9 us
    all_to_all x1, starting transfers between devices, body(): lax.all_to_all(jnp.broadcast_to(hidden[None], (tp, rows, chans)), 'tp', s...  9.35 us
  transfers between devices with their start and end apart: 1, of which 1 were waited for; matrix products, arithmetic and copies ran while one was open for 0% of the time, Pallas kernels for 0%

commit v1 on v0

v1 whole, which is shorter than its diff:
```python
import functools
import jax
import jax.numpy as jnp
from jax import lax
from jax.experimental import pallas as pl
from jax.experimental.pallas import tpu as pltpu
from jax.sharding import PartitionSpec as P

eps = 1e-05
f32 = jnp.float32
bf16 = jnp.bfloat16
T = 16


def tables_kernel(rates_ref, residues_ref, pow_ref, near_ref, fore_ref, back_ref):
    rates = rates_ref[...]
    modes, chans = rates.shape
    strength = residues_ref[...] * jnp.sqrt(rates)
    for k in range(T):
        pow_ref[k] = jnp.exp(-rates * float(k))
    pow_ref[T] = jnp.exp(-rates * float(T))
    pow_ref[T + 1] = jnp.exp(rates)
    steps = lax.broadcasted_iota(jnp.int32, (T, chans), 0).astype(f32)
    total = jnp.zeros((T, chans), f32)
    for m in range(modes):
        rate = rates[m : m + 1, :]
        weight = strength[m : m + 1, :]
        fore = weight * jnp.exp(-rate * (steps + 1.0))
        fore_ref[m] = fore
        back_ref[m] = weight * jnp.exp(-rate * (float(T) - steps))
        total = total + fore
    near_ref[pl.ds(T + 1, T), :] = total
    near_ref[pl.ds(T, 1), :] = jnp.sum(strength, axis=0, keepdims=True)
    for k in range(1, T + 1):
        near_ref[pl.ds(T - k, 1), :] = total[k - 1 : k, :]


def prepare_kernel(wv_ref, wg_ref, gain_ref, wo_ref, own_ref, far_ref, back_ref):
    chans = wo_ref.shape[0]
    i0 = lax.broadcasted_iota(jnp.int32, (chans, chans), 0)
    i1 = lax.broadcasted_iota(jnp.int32, (chans, chans), 1)
    flip = (i0 + i1 == chans - 1).astype(f32).astype(bf16)
    rows = jnp.broadcast_to(gain_ref[0], (chans, chans))
    gain = jnp.sum(jnp.where(i0 == i1, rows, 0.0), axis=1, keepdims=True)
    for n, ref in enumerate((wv_ref, wg_ref)):
        scaled = (ref[...].astype(f32) * gain).astype(bf16)
        own_ref[n] = scaled
        far_ref[n] = jnp.dot(flip, scaled, preferred_element_type=f32).astype(bf16)
    back_ref[...] = jnp.dot(wo_ref[...], flip, preferred_element_type=f32).astype(bf16)


def matmul_step(x_ref, own_ref, far_ref, acc_ref):
    blocks, rows, chans = x_ref.shape
    x = jnp.concatenate([x_ref[b] for b in range(blocks)], axis=1)
    first = jnp.dot(x, own_ref[0], preferred_element_type=f32)
    second = jnp.dot(x, far_ref[0], preferred_element_type=f32)
    k = pl.program_id(0)

    @pl.when(k == 0)
    def _():
        acc_ref[:, :chans] = first
        acc_ref[:, chans:] = second

    @pl.when(k > 0)
    def _():
        acc_ref[:, :chans] += first
        acc_ref[:, chans:] += second


def values_kernel(
    x_ref, own_ref, far_ref, vt_ref, pow_ref,
    send_ref, fore_ref, back_ref, sv_ref, scale_ref,
    acc_ref, sq_ref, pad_ref,
):
    k = pl.program_id(0)
    steps = pl.num_programs(0)
    blocks, rows, chans = x_ref.shape
    place = lax.axis_index("seq")
    places = lax.axis_size("seq")
    matmul_step(x_ref, own_ref, far_ref, acc_ref)
    total = jnp.zeros((rows, chans), f32)
    for b in range(blocks):
        part = x_ref[b].astype(f32)
        total = total + part * part

    @pl.when(k == 0)
    def _():
        sq_ref[...] = total

    @pl.when(k > 0)
    def _():
        sq_ref[...] += total

    @pl.when(k == steps - 1)
    def _():
        mean = jnp.sum(sq_ref[...], axis=1, keepdims=True) * (1.0 / (steps * blocks * chans))
        scale = lax.rsqrt(mean + eps)
        scale_ref[...] = jnp.broadcast_to(scale, scale_ref.shape)
        low_ok = (place > 0).astype(f32)
        high_ok = (place < places - 1).astype(f32)
        zeros8 = jnp.zeros((8, chans), f32)
        tiles = rows // T
        for s in range(2):
            v = acc_ref[:, s * chans : (s + 1) * chans] * scale
            pad_ref[0:8, :] = zeros8
            pad_ref[8 : 8 + rows, :] = v
            pad_ref[8 + rows : 16 + rows, :] = zeros8
            a, c = (0, 2) if s == 0 else (2, 0)
            ta, tb, tc = vt_ref[a : a + 1, :], vt_ref[1:2, :], vt_ref[c : c + 1, :]
            sv = ta * pad_ref[7 : 7 + rows, :] + tb * v + tc * pad_ref[9 : 9 + rows, :]
            sv_ref[s] = sv.reshape(tiles, T, chans)
            all_low = tc * v[0:1, :] * low_ok
            all_high = ta * v[rows - 1 : rows, :] * high_ok
            for g in range(chans // 128):
                lanes = slice(g * 128, (g + 1) * 128)
                low, high = all_low[:, lanes], all_high[:, lanes]
                jump = pow_ref[T, :, lanes]
                inverse = pow_ref[T + 1, :, lanes]
                fold = jnp.zeros((tiles, 16, 128), f32)
                for j in range(T):
                    fold = fold + pow_ref[T - 1 - j, :, lanes][None] * sv_ref[s, :, j : j + 1, lanes]
                state = jnp.broadcast_to(low, (16, 128))
                for n in range(tiles):
                    fore_ref[s, n, :, lanes] = state
                    state = jump * state + fold[n]
                ahead = state + inverse * high
                fold = jnp.zeros((tiles, 16, 128), f32)
                for j in range(T):
                    fold = fold + pow_ref[j, :, lanes][None] * sv_ref[s, :, j : j + 1, lanes]
                state = jnp.broadcast_to(high, (16, 128))
                for n in reversed(range(tiles)):
                    back_ref[s, n, :, lanes] = state
                    state = jump * state + fold[n]
                behind = state + inverse * low
                wide = slice(s * chans + g * 128, s * chans + (g + 1) * 128)
                for i in range(places):
                    send_ref[i, :, wide] = jnp.where(i > place, ahead, behind)


def gates_kernel(x_ref, own_ref, far_ref, scale_ref, gates_ref, first_ref, last_ref, acc_ref):
    k = pl.program_id(0)
    steps = pl.num_programs(0)
    rows = x_ref.shape[1]
    matmul_step(x_ref, own_ref, far_ref, acc_ref)

    @pl.when(k == steps - 1)
    def _():
        gates = acc_ref[...] * scale_ref[:, 0:1]
        gates_ref[...] = gates
        first_ref[...] = gates[0:8, :]
        last_ref[...] = gates[rows - 8 : rows, :]


def near_kernel(sv_ref, near_ref, local_ref):
    tiles = sv_ref.shape[1]
    chans = sv_ref.shape[3]
    for s in range(2):
        for g in range(chans // 128):
            lanes = slice(g * 128, (g + 1) * 128)
            inner = jnp.zeros((tiles, T, 128), f32)
            for j in range(T):
                inner = inner + near_ref[T - j : 2 * T - j, lanes][None] * sv_ref[s, :, j : j + 1, lanes]
            local_ref[s, :, :, lanes] = inner


def output_kernel(
    recv_ref, fore_ref, back_ref, local_ref, gates_ref, above_ref, below_ref, gt_ref, rates_ref,
    spread_f_ref, spread_b_ref, near_w_ref, far_w_ref, out_ref, z_ref, pad_ref, st_ref,
):
    k = pl.program_id(0)
    rows = gates_ref.shape[0]
    chans = gates_ref.shape[1] // 2
    tiles = rows // T
    place = lax.axis_index("seq")
    places = lax.axis_size("seq")

    @pl.when(k == 0)
    def _():
        for s in range(2):
            wide = slice(s * chans, (s + 1) * chans)
            g = gates_ref[:, wide]
            pad_ref[0:8, :] = below_ref[:, wide]
            pad_ref[8 : 8 + rows, :] = g
            pad_ref[8 + rows : 16 + rows, :] = above_ref[:, wide]
            a, c = (0, 2) if s == 0 else (2, 0)
            ta, tb, tc = gt_ref[a : a + 1, :], gt_ref[1:2, :], gt_ref[c : c + 1, :]
            sg = ta * pad_ref[7 : 7 + rows, :] + tb * g + tc * pad_ref[9 : 9 + rows, :]
            for g2 in range(chans // 128):
                lanes = slice(g2 * 128, (g2 + 1) * 128)
                wide = slice(s * chans + g2 * 128, s * chans + (g2 + 1) * 128)
                rates = rates_ref[:, lanes]
                hop = jnp.exp(-rates * float(rows))
                jump = jnp.exp(-rates * float(T))
                carry_f = jnp.zeros((16, 128), f32)
                carry_b = jnp.zeros((16, 128), f32)
                for j in range(places):
                    r = places - 1 - j
                    carry_f = jnp.where(j < place, carry_f * hop + recv_ref[j, :, wide], carry_f)
                    carry_b = jnp.where(r > place, carry_b * hop + recv_ref[r, :, wide], carry_b)
                for n in range(tiles):
                    m = tiles - 1 - n
                    st_ref[0, n] = fore_ref[s, n, :, lanes] + carry_f
                    st_ref[1, m] = back_ref[s, m, :, lanes] + carry_b
                    carry_f = carry_f * jump
                    carry_b = carry_b * jump
                conv = local_ref[s, :, :, lanes]
                for m in range(16):
                    conv = conv + spread_f_ref[m, :, lanes][None] * st_ref[0, :, m : m + 1, :]
                for m in range(16):
                    conv = conv + spread_b_ref[m, :, lanes][None] * st_ref[1, :, m : m + 1, :]
                z_ref[:, wide] = (sg[:, lanes] * conv.reshape(rows, 128)).astype(bf16)

    out = jnp.dot(z_ref[:, :chans], near_w_ref[...], preferred_element_type=f32)
    out = out + jnp.dot(z_ref[:, chans:], far_w_ref[...], preferred_element_type=f32)
    for b in range(out_ref.shape[0]):
        out_ref[b] = out[:, b * chans : (b + 1) * chans].astype(bf16)


def far_memory(*arrays):
    return [pltpu.with_memory_space_constraint(a, pltpu.HBM) for a in arrays]


def whole(shape):
    return pl.BlockSpec(shape, lambda *_: (0,) * len(shape))


def body(
    hidden, norm_gain, value_weight, gate_weight, value_taps, gate_taps, rates, residues, out_weight
):
    rows, chans = hidden.shape
    tp = lax.axis_size("tp")
    places = lax.axis_size("seq")
    modes = rates.shape[0]
    tiles = rows // T
    width = value_weight.shape[0]
    shape = pltpu.HBM
    params = pltpu.CompilerParams(vmem_limit_bytes=14 << 20)
    square = pl.BlockSpec((chans, chans), lambda k: (k, 0))

    blocks = lax.all_to_all(
        jnp.broadcast_to(hidden[None], (tp, rows, chans)), "tp", split_axis=0, concat_axis=0
    )

    powers, near, spread_f, spread_b = pl.pallas_call(
        tables_kernel,
        out_shape=(
            shape((T + 2, modes, chans), f32),
            shape((2 * T + 8, chans), f32),
            shape((modes, T, chans), f32),
            shape((modes, T, chans), f32),
        ),
        compiler_params=params,
        name="tables",
    )(rates, residues)
    own_w, far_w, back_w = pl.pallas_call(
        prepare_kernel,
        grid=(tp,),
        in_specs=[
            square,
            square,
            pl.BlockSpec((1, 1, chans), lambda k: (k, 0, 0)),
            pl.BlockSpec((chans, chans), lambda k: (0, k)),
        ],
        out_specs=[
            pl.BlockSpec((2, chans, chans), lambda k: (0, k, 0)),
            pl.BlockSpec((2, chans, chans), lambda k: (0, tp - 1 - k, 0)),
            pl.BlockSpec((chans, chans), lambda k: (0, tp - 1 - k)),
        ],
        out_shape=(
            shape((2, width, chans), bf16),
            shape((2, width, chans), bf16),
            shape((chans, width), bf16),
        ),
        compiler_params=params,
        name="prepare",
    )(*far_memory(value_weight, gate_weight), norm_gain.reshape(tp, 1, chans), *far_memory(out_weight))

    group = 4
    steps = tp // group
    x_spec = pl.BlockSpec((group, rows, chans), lambda k: (k, 0, 0))

    def w_spec(n):
        return pl.BlockSpec((1, group * chans, chans), lambda k: (n, k, 0))

    send, fore, back, sv, scale = pl.pallas_call(
        values_kernel,
        grid=(steps,),
        in_specs=[x_spec, w_spec(0), w_spec(0), whole(value_taps.shape), whole(powers.shape)],
        out_specs=[
            whole((places, modes, 2 * chans)),
            whole((2, tiles, modes, chans)),
            whole((2, tiles, modes, chans)),
            whole((2, tiles, T, chans)),
            whole((rows, 128)),
        ],
        out_shape=(
            shape((places, modes, 2 * chans), f32),
            shape((2, tiles, modes, chans), f32),
            shape((2, tiles, modes, chans), f32),
            shape((2, tiles, T, chans), f32),
            shape((rows, 128), f32),
        ),
        scratch_shapes=[
            pltpu.VMEM((rows, 2 * chans), f32),
            pltpu.VMEM((rows, chans), f32),
            pltpu.VMEM((rows + 16, chans), f32),
        ],
        compiler_params=params,
        name="values",
    )(blocks, *far_memory(own_w, far_w), value_taps, *far_memory(powers))

    recv = lax.all_to_all(send, "seq", split_axis=0, concat_axis=0)

    gates, first, last = pl.pallas_call(
        gates_kernel,
        grid=(steps,),
        in_specs=[x_spec, w_spec(1), w_spec(1), whole((rows, 128))],
        out_specs=[whole((rows, 2 * chans)), whole((8, 2 * chans)), whole((8, 2 * chans))],
        out_shape=(
            shape((rows, 2 * chans), f32),
            shape((8, 2 * chans), f32),
            shape((8, 2 * chans), f32),
        ),
        scratch_shapes=[pltpu.VMEM((rows, 2 * chans), f32)],
        compiler_params=params,
        name="gates",
    )(blocks, *far_memory(own_w, far_w, scale))
    up = [(i, i + 1) for i in range(places - 1)]
    below = lax.ppermute(last, "seq", up)
    above = lax.ppermute(first, "seq", [(b, a) for a, b in up])

    local = pl.pallas_call(
        near_kernel,
        out_shape=shape((2, tiles, T, chans), f32),
        compiler_params=params,
        name="near",
    )(*far_memory(sv, near))

    partial = pl.pallas_call(
        output_kernel,
        grid=(steps,),
        in_specs=[
            whole(recv.shape),
            whole(fore.shape),
            whole(back.shape),
            whole(local.shape),
            whole(gates.shape),
            whole(above.shape),
            whole(below.shape),
            whole(gate_taps.shape),
            whole(rates.shape),
            whole(spread_f.shape),
            whole(spread_b.shape),
            pl.BlockSpec((chans, group * chans), lambda k: (0, k)),
            pl.BlockSpec((chans, group * chans), lambda k: (0, k)),
        ],
        out_specs=pl.BlockSpec((group, rows, chans), lambda k: (k, 0, 0)),
        out_shape=jax.ShapeDtypeStruct((tp, rows, chans), bf16),
        scratch_shapes=[
            pltpu.VMEM((rows, 2 * chans), bf16),
            pltpu.VMEM((rows + 16, chans), f32),
            pltpu.VMEM((2, tiles, modes, 128), f32),
        ],
        compiler_params=params,
        name="output",
    )(
        recv, *far_memory(fore, back, local, gates), above, below, gate_taps, rates,
        *far_memory(spread_f, spread_b, out_weight, back_w),
    )

    parts = lax.all_to_all(partial, "tp", split_axis=0, concat_axis=0)
    return jnp.sum(parts.astype(f32), axis=0).astype(bf16)


def solution(mesh):
    in_specs = (
        P("seq", "tp"),
        P(),
        P(None, "tp"),
        P(None, "tp"),
        P(None, "tp"),
        P(None, "tp"),
        P(None, "tp"),
        P(None, "tp"),
        P("tp", None),
    )
    out_specs = P("seq", "tp")
    return jax.shard_map(body, mesh=mesh, in_specs=in_specs, out_specs=out_specs, check_vma=False)
```

time: 167 us -> 153 us (0.916)
  blocking collectives: 74.4 us -> 50.7 us
  starting transfers between devices: 9.35 us -> 23 us
  waiting for transfers between devices: 48.8 us -> 37.2 us
  Pallas kernels: 29.1 us -> 38 us
    all_to_all x1 -> x0, blocking collectives: 19.6 us -> none  [body(): recv = lax.all_to_all(send, 'seq', split_axis=0, concat_axis=0)]
    all_to_all x1, waiting for transfers between devices: 48.8 us -> 33.4 us  [body(): lax.all_to_all(jnp.broadcast_to(hidden[None], (tp, rows, chans)), 'tp', s...]
    pallas_call x2 -> x5, Pallas kernels: 29 us -> 37 us  [the longest x1 14.5 us: body(): pl.pallas_call(prepare_kernel, grid=(tp,), in_specs=[square, square, pl.B...]
    all_to_all x0 -> x1, starting transfers between devices: none -> 7.45 us  [body(): recv = lax.all_to_all(send, 'seq', split_axis=0, concat_axis=0)]
    ppermute x0 -> x2, starting transfers between devices: none -> 6.24 us  [the longest x1 4.32 us: body(): above = lax.ppermute(first, 'seq', [(b, a) for a, b in up])]
    all_to_all x1, blocking collectives: 54.8 us -> 50.7 us  [body(): parts = lax.all_to_all(partial, 'tp', split_axis=0, concat_axis=0)]
    ppermute x0 -> x2, waiting for transfers between devices: none -> 3.75 us  [the longest x1 3.75 us: body(): below = lax.ppermute(last, 'seq', up)]
  transfers between devices with their start and end apart: 1 -> 4, of which waited for: 1 -> 2; matrix products, arithmetic and copies ran while one was open for 0% -> 0% of each run, Pallas kernels for 0% -> 16%
where the time goes in v1:
time: 153 us; the launch traced here: 152 us
  blocking collectives  50.7 us (33%)
  Pallas kernels  38 us (25%)
  waiting for transfers between devices  37.2 us (24%)
  starting transfers between devices  23 us (15%)
  local copies, waits for them, and re-layouts  2.44 us (2%)
    all_to_all x1, blocking collectives, body(): parts = lax.all_to_all(partial, 'tp', split_axis=0, concat_axis=0)  50.7 us
    all_to_all x1, waiting for transfers between devices, body(): lax.all_to_all(jnp.broadcast_to(hidden[None], (tp, rows, chans)), 'tp', s...  33.4 us
    pallas_call x1, Pallas kernels, body(): pl.pallas_call(prepare_kernel, grid=(tp,), in_specs=[square, square, pl.B...  14.5 us
    all_to_all x1, starting transfers between devices, body(): lax.all_to_all(jnp.broadcast_to(hidden[None], (tp, rows, chans)), 'tp', s...  9.33 us
    pallas_call x1, Pallas kernels, body(): pl.pallas_call(values_kernel, grid=(steps,), in_specs=[x_spec, w_spec(0),...  7.7 us
    all_to_all x1, starting transfers between devices, body(): recv = lax.all_to_all(send, 'seq', split_axis=0, concat_axis=0)  7.45 us
    pallas_call x1, Pallas kernels, body(): pl.pallas_call(output_kernel, grid=(steps,), in_specs=[whole(recv.shape),...  6.65 us
    pallas_call x1, Pallas kernels, body(): pl.pallas_call(gates_kernel, grid=(steps,), in_specs=[x_spec, w_spec(1),...  4.92 us
  transfers between devices with their start and end apart: 4, of which 2 were waited for; matrix products, arithmetic and copies ran while one was open for 0% of the time, Pallas kernels for 16%

profile of v1, /device:TPU:4, one launch (start us, length us, event | category | flops | bytes accessed | tf_op | source)
XLA Modules:
  0.0 152.4 jit_solution(14350389184717320986)
XLA Ops:
  0.0 2.4 %broadcast_in_dim.2 = bf16[16,256,256]{2,1,0:T(8,128)(2,1)} broadcast(bf16[256,256]{1,0:T(8,128)(2,1)} %param.9), dimensions={1,2} | broadcast | bytes 2228224 | tf_op jit(solution)/shard_map/broadcast_in_dim | solution.py:241
  2.4 0.0 copy-start
  2.4 0.0 copy-start.2
  2.4 0.0 copy-start.1
  2.4 9.3 %all-to-all-start = ((bf16[16,256,256]{2,1,0:T(8,128)(2,1)}), bf16[16,256,256]{2,1,0:T(8,128)(2,1)S(1)}, u32[]{:S(2)}, u32[]{:S(2)}) async-start(bf16[16,256,256]{2,1,0:T(8,128)(2,1)} %broadcast_in_dim.2), calls=%async_computation | async-start | bytes 4194304 | tf_op jit(solution)/shard_map/all_to_all | solution.py:240
  11.8 0.0 copy-done
  11.8 0.0 copy-done.2
  11.8 1.0 tables.1
  12.8 0.0 copy-done.1
  12.8 0.0 copy-start.3
  12.8 14.5 %prepare.1 = (bf16[2,4096,256]{2,1,0:T(8,128)(2,1)}, bf16[2,4096,256]{2,1,0:T(8,128)(2,1)}, bf16[256,4096]{1,0:T(8,128)(2,1)}) custom-call(bf16[4096,256]{1,0:T(8,128)(2,1)} %wv_ref.1, bf16[4096,256]{1,0:T(8,128)(2,1)} %wg_ref.1, f32[16,1,256]{2,1,0:T(1,128)S(1)} %bitcast.1, bf16[256,4096]{1,0:T(8,128)(2,1)} %near_w_ref.1), custom_call_target="tpu_custom_call" | custom-call | tf_op jit(solution)/shard_map/prepare/pallas_call | solution.py:255
  27.3 33.4 %all-to-all-done.x_ref = bf16[16,256,256]{2,1,0:T(8,128)(2,1)S(1)} async-done(((bf16[16,256,256]{2,1,0:T(8,128)(2,1)}), bf16[16,256,256]{2,1,0:T(8,128)(2,1)S(1)}, u32[]{:S(2)}, u32[]{:S(2)}) %all-to-all-start) | async-done | bytes 2097184 | tf_op jit(solution)/shard_map/all_to_all | solution.py:240
  60.8 0.0 copy-done.3
  60.8 7.7 %values.1 = (f32[16,16,512]{2,1,0:T(8,128)}, f32[2,16,16,256]{3,2,1,0:T(8,128)}, f32[2,16,16,256]{3,2,1,0:T(8,128)}, f32[2,16,16,256]{3,2,1,0:T(8,128)}, f32[256,128]{1,0:T(8,128)}) custom-call(bf16[16,256,256]{2,1,0:T(8,128)(2,1)S(1)} %all-to-all-done.x_ref, bf16[2,4096,256]{2,1,0:T(8,128)(2,1)} %get-tuple-element.20.own_ref, ...), custom_call_target="tpu_custom_call" | custom-call | tf_op jit(solution)/shard_map/values/pallas_call | solution.py:285
  68.5 7.5 %all-to-all-start.1 = ((f32[16,16,512]{2,1,0:T(8,128)}), f32[16,16,512]{2,1,0:T(8,128)S(1)}, u32[]{:S(2)}, u32[]{:S(2)}) async-start(f32[16,16,512]{2,1,0:T(8,128)} %get-tuple-element.23), calls=%async_computation.1 | async-start | bytes 1048576 | tf_op jit(solution)/shard_map/all_to_all | solution.py:312
  75.9 0.0 copy-start.4
  75.9 4.9 %gates.1 = (f32[256,512]{1,0:T(8,128)}, f32[8,512]{1,0:T(8,128)}, f32[8,512]{1,0:T(8,128)}) custom-call(bf16[16,256,256]{2,1,0:T(8,128)(2,1)S(1)} %all-to-all-done.x_ref, bf16[2,4096,256]{2,1,0:T(8,128)(2,1)} %get-tuple-element.20.own_ref, bf16[2,4096,256]{2,1,0:T(8,128)(2,1)} %get-tuple-element.21.far_ref, f32[256,128]{1,0:T(8,128)} %get-tuple-element.28.scale_ref), custom_call_target="tpu_custom_call" | custom-call | tf_op jit(solution)/shard_map/gates/pallas_call | solution.py:314
  80.8 4.3 %collective-permute-start = (f32[8,512]{1,0:T(8,128)}, f32[8,512]{1,0:T(8,128)S(1)}, u32[]{:S(2)}, u32[]{:S(2)}) collective-permute-start(f32[8,512]{1,0:T(8,128)} %get-tuple-element.30), channel_id=1, source_target_pairs={{16,0},{32,16},{48,32},{64,48},{80,64},{96,80},{112,96},{128,112},... | collective-permute-start | bytes 49160 | tf_op jit(solution)/shard_map/ppermute | solution.py:330
  85.2 1.9 %collective-permute-start.1 = (f32[8,512]{1,0:T(8,128)}, f32[8,512]{1,0:T(8,128)S(1)}, u32[]{:S(2)}, u32[]{:S(2)}) collective-permute-start(f32[8,512]{1,0:T(8,128)} %get-tuple-element.31), channel_id=1, source_target_pairs={{0,16},{16,32},{32,48},{48,64},{64,80},{80,96},{96,112},{112,128},... | collective-permute-start | bytes 49160 | tf_op jit(solution)/shard_map/ppermute | solution.py:329
  87.1 3.2 %near.1.local_ref = f32[2,16,16,256]{3,2,1,0:T(8,128)} custom-call(f32[2,16,16,256]{3,2,1,0:T(8,128)} %get-tuple-element.26.sv_ref, f32[40,256]{1,0:T(8,128)} %get-tuple-element.27.near_ref), custom_call_target="tpu_custom_call" | custom-call | tf_op jit(solution)/shard_map/near/pallas_call | solution.py:332
  90.3 0.0 collective-permute-done.above_ref
  90.3 3.7 %collective-permute-done.1.below_ref = f32[8,512]{1,0:T(8,128)S(1)} collective-permute-done((f32[8,512]{1,0:T(8,128)}, f32[8,512]{1,0:T(8,128)S(1)}, u32[]{:S(2)}, u32[]{:S(2)}) %collective-permute-start.1) | collective-permute-done | bytes 16416 | tf_op jit(solution)/shard_map/ppermute | solution.py:329
  94.0 0.0 all-to-all-done.1.recv_ref
  94.0 0.0 copy-done.4
  94.1 6.6 %output.1 = bf16[16,256,256]{2,1,0:T(8,128)(2,1)S(1)} custom-call(f32[16,16,512]{2,1,0:T(8,128)S(1)} %all-to-all-done.1.recv_ref, f32[2,16,16,256]{3,2,1,0:T(8,128)} %get-tuple-element.24.fore_ref, f32[2,16,16,256]{3,2,1,0:T(8,128)} %get-tuple-element.25.back_ref, f32[2,16,16,256]{3,2,1,0:T(8,128)} %near.1.local_ref, ...), custom_call_target="tpu_custom_call" | custom-call | tf_op jit(solution)/shard_map/output/pallas_call | solution.py:339
  100.7 50.7 %all_to_all.15 = bf16[16,256,256]{2,1,0:T(8,128)(2,1)S(1)} all-to-all(bf16[16,256,256]{2,1,0:T(8,128)(2,1)S(1)} %output.1), channel_id=1, replica_groups=mesh['seq'=16,'tp'=16] {'tp'}, dimensions={0} | all-to-all | bytes 4194304 | tf_op jit(solution)/shard_map/all_to_all | solution.py:371
  151.4 1.0 reduce_sum.12
Async XLA Ops:
  2.4 9.4 %copy-start = (f32[16,256]{1,0:T(8,128)S(1)}, f32[16,256]{1,0:T(8,128)}, u32[]{:S(2)}) copy-start(f32[16,256]{1,0:T(8,128)} %rates_ref.3) | copy-start | bytes 49156
  2.4 9.4 %copy-start.2 = (f32[16,256]{1,0:T(8,128)S(1)}, f32[16,256]{1,0:T(8,128)}, u32[]{:S(2)}) copy-start(f32[16,256]{1,0:T(8,128)} %residues_ref.1) | copy-start | bytes 49156
  2.4 10.4 %copy-start.1 = (f32[4096]{0:T(1024)S(1)}, f32[4096]{0:T(1024)}, u32[]{:S(2)}) copy-start(f32[4096]{0:T(1024)} %param.10) | copy-start | bytes 49156
  2.4 58.3 %all-to-all-start = ((bf16[16,256,256]{2,1,0:T(8,128)(2,1)}), bf16[16,256,256]{2,1,0:T(8,128)(2,1)S(1)}, u32[]{:S(2)}, u32[]{:S(2)}) async-start(bf16[16,256,256]{2,1,0:T(8,128)(2,1)} %broadcast_in_dim.2), calls=%async_computation | async-start | bytes 4194304 | tf_op jit(solution)/shard_map/all_to_all | solution.py:240
  12.8 48.0 %copy-start.3 = (f32[3,256]{1,0:T(4,128)S(1)}, f32[3,256]{1,0:T(4,128)}, u32[]{:S(2)}) copy-start(f32[3,256]{1,0:T(4,128)} %vt_ref.1) | copy-start | bytes 9220
  68.5 25.6 %all-to-all-start.1 = ((f32[16,16,512]{2,1,0:T(8,128)}), f32[16,16,512]{2,1,0:T(8,128)S(1)}, u32[]{:S(2)}, u32[]{:S(2)}) async-start(f32[16,16,512]{2,1,0:T(8,128)} %get-tuple-element.23), calls=%async_computation.1 | async-start | bytes 1048576 | tf_op jit(solution)/shard_map/all_to_all | solution.py:312
  75.9 18.1 %copy-start.4 = (f32[3,256]{1,0:T(4,128)S(1)}, f32[3,256]{1,0:T(4,128)}, u32[]{:S(2)}) copy-start(f32[3,256]{1,0:T(4,128)} %gt_ref.1) | copy-start | bytes 9220
  80.8 9.5 %collective-permute-start = (f32[8,512]{1,0:T(8,128)}, f32[8,512]{1,0:T(8,128)S(1)}, u32[]{:S(2)}, u32[]{:S(2)}) collective-permute-start(f32[8,512]{1,0:T(8,128)} %get-tuple-element.30), channel_id=1, source_target_pairs={{16,0},{32,16},{48,32},{64,48},{80,64},{96,80},{112,96},{128,112},... | collective-permute-start | bytes 49160 | tf_op jit(solution)/shard_map/ppermute | solution.py:330
  85.2 8.9 %collective-permute-start.1 = (f32[8,512]{1,0:T(8,128)}, f32[8,512]{1,0:T(8,128)S(1)}, u32[]{:S(2)}, u32[]{:S(2)}) collective-permute-start(f32[8,512]{1,0:T(8,128)} %get-tuple-element.31), channel_id=1, source_target_pairs={{0,16},{16,32},{32,48},{48,64},{64,80},{80,96},{96,112},{112,128},... | collective-permute-start | bytes 49160 | tf_op jit(solution)/shard_map/ppermute | solution.py:329

commit v2 on v0

v2 whole, which is shorter than its diff:
```python
import functools
import jax
import jax.numpy as jnp
from jax import lax
from jax.experimental import pallas as pl
from jax.experimental.pallas import tpu as pltpu
from jax.sharding import PartitionSpec as P

eps = 1e-05
f32 = jnp.float32
bf16 = jnp.bfloat16
T = 16


def tables_kernel(rates_ref, residues_ref, pow_ref, near_ref, fore_ref, back_ref):
    rates = rates_ref[...]
    modes, chans = rates.shape
    strength = residues_ref[...] * jnp.sqrt(rates)
    for k in range(T):
        pow_ref[k] = jnp.exp(-rates * float(k))
    pow_ref[T] = jnp.exp(-rates * float(T))
    pow_ref[T + 1] = jnp.exp(rates)
    steps = lax.broadcasted_iota(jnp.int32, (T, chans), 0).astype(f32)
    total = jnp.zeros((T, chans), f32)
    for m in range(modes):
        rate = rates[m : m + 1, :]
        weight = strength[m : m + 1, :]
        fore = weight * jnp.exp(-rate * (steps + 1.0))
        fore_ref[m] = fore
        back_ref[m] = weight * jnp.exp(-rate * (float(T) - steps))
        total = total + fore
    near_ref[pl.ds(T + 1, T), :] = total
    near_ref[pl.ds(T, 1), :] = jnp.sum(strength, axis=0, keepdims=True)
    for k in range(1, T + 1):
        near_ref[pl.ds(T - k, 1), :] = total[k - 1 : k, :]


def reversal(n):
    i0 = lax.broadcasted_iota(jnp.int32, (n, n), 0)
    i1 = lax.broadcasted_iota(jnp.int32, (n, n), 1)
    return (i0 + i1 == n - 1).astype(f32).astype(bf16)


def shard_at(place, column, hop, tp):
    ring = tp // 2
    return ((place // ring + column) % 2) * ring + (place % ring + hop + ring) % ring


def rows_of(block, size):
    return pl.ds(pl.multiple_of(block * size, size), size)


def accumulate(slots, x_refs, gain_ref, weights, x_buf, w_buf, sems, acc_ref, sq_ref, fresh):
    tp = lax.axis_size("tp")
    place = lax.axis_index("tp")
    rows, chans = x_buf.shape[1:]
    copies = []
    for n, (array, entry, column, hop) in enumerate(slots):
        block = shard_at(place, column, hop, tp)
        source = x_refs[array] if entry is None else x_refs[array].at[entry]
        group = [pltpu.make_async_copy(source, x_buf.at[n], sems.at[n, 0])]
        for w, ref in enumerate(weights):
            lanes = pl.ds(w * chans, chans)
            group.append(
                pltpu.make_async_copy(ref.at[rows_of(block, chans), :], w_buf.at[n, 0, :, lanes], sems.at[n, 1 + w])
            )
            group.append(
                pltpu.make_async_copy(
                    ref.at[rows_of(tp - 1 - block, chans), :], w_buf.at[n, 1, :, lanes], sems.at[n, 3 + w]
                )
            )
        for copy in group:
            copy.start()
        copies.append(group)
    flip = reversal(chans)
    wide = w_buf.shape[3]
    for n, (array, entry, column, hop) in enumerate(slots):
        block = shard_at(place, column, hop, tp)
        for copy in copies[n]:
            copy.wait()
        x = x_buf[n]
        part = x.astype(f32)
        mirrored = jnp.dot(x, flip, preferred_element_type=f32)
        own = (part * gain_ref[block]).astype(bf16)
        far = (mirrored * gain_ref[tp - 1 - block]).astype(bf16)
        first = jnp.dot(own, w_buf[n, 0], preferred_element_type=f32)
        second = jnp.dot(far, w_buf[n, 1], preferred_element_type=f32)
        if fresh and n == 0:
            sq_ref[...] = part * part
            acc_ref[0] = first
            acc_ref[1] = second
        else:
            sq_ref[...] += part * part
            acc_ref[0] += first
            acc_ref[1] += second


def early_kernel(slots, arrays, fresh, *refs):
    x_refs, refs = refs[:arrays], refs[arrays:]
    gain_ref, wv_ref, wg_ref, refs = refs[0], refs[1], refs[2], refs[3:]
    if not fresh:
        acc_in, sq_in, refs = refs[0], refs[1], refs[2:]
    acc_ref, sq_ref, x_buf, w_buf, sems = refs
    if not fresh:
        acc_ref[...] = acc_in[...]
        sq_ref[...] = sq_in[...]
    accumulate(slots, x_refs, gain_ref, (wv_ref, wg_ref), x_buf, w_buf, sems, acc_ref, sq_ref, fresh)


def states_kernel(slots, arrays, *refs):
    x_refs, refs = refs[:arrays], refs[arrays:]
    gain_ref, wv_ref, wg_ref, acc_in, sq_in, vt_ref, pow_ref, refs = *refs[:7], refs[7:]
    send_ref, fore_ref, back_ref, sv_ref, gates_ref, first_ref, last_ref, refs = *refs[:7], refs[7:]
    acc_ref, sq_ref, pad_ref, x_buf, w_buf, sems = refs
    acc_ref[...] = acc_in[...]
    sq_ref[...] = sq_in[...]
    accumulate(slots, x_refs, gain_ref, (wv_ref, wg_ref), x_buf, w_buf, sems, acc_ref, sq_ref, False)
    rows, chans = sq_ref.shape
    place = lax.axis_index("seq")
    places = lax.axis_size("seq")
    mean = jnp.sum(sq_ref[...], axis=1, keepdims=True) * (1.0 / (lax.axis_size("tp") * chans))
    scale = lax.rsqrt(mean + eps)
    low_ok = (place > 0).astype(f32)
    high_ok = (place < places - 1).astype(f32)
    zeros8 = jnp.zeros((8, chans), f32)
    tiles = rows // T
    for s in range(2):
        strand = slice(s * chans, (s + 1) * chans)
        gates = acc_ref[s, :, chans:] * scale
        gates_ref[:, strand] = gates
        first_ref[:, strand] = gates[0:8, :]
        last_ref[:, strand] = gates[rows - 8 : rows, :]
        v = acc_ref[s, :, :chans] * scale
        pad_ref[0:8, :] = zeros8
        pad_ref[8 : 8 + rows, :] = v
        pad_ref[8 + rows : 16 + rows, :] = zeros8
        a, c = (0, 2) if s == 0 else (2, 0)
        ta, tb, tc = vt_ref[a : a + 1, :], vt_ref[1:2, :], vt_ref[c : c + 1, :]
        sv = ta * pad_ref[7 : 7 + rows, :] + tb * v + tc * pad_ref[9 : 9 + rows, :]
        sv_ref[s] = sv.reshape(tiles, T, chans)
        all_low = tc * v[0:1, :] * low_ok
        all_high = ta * v[rows - 1 : rows, :] * high_ok
        for g in range(chans // 128):
            lanes = slice(g * 128, (g + 1) * 128)
            low, high = all_low[:, lanes], all_high[:, lanes]
            jump = pow_ref[T, :, lanes]
            inverse = pow_ref[T + 1, :, lanes]
            fold = jnp.zeros((tiles, 16, 128), f32)
            for j in range(T):
                fold = fold + pow_ref[T - 1 - j, :, lanes][None] * sv_ref[s, :, j : j + 1, lanes]
            state = jnp.broadcast_to(low, (16, 128))
            for n in range(tiles):
                fore_ref[s, n, :, lanes] = state
                state = jump * state + fold[n]
            ahead = state + inverse * high
            fold = jnp.zeros((tiles, 16, 128), f32)
            for j in range(T):
                fold = fold + pow_ref[j, :, lanes][None] * sv_ref[s, :, j : j + 1, lanes]
            state = jnp.broadcast_to(high, (16, 128))
            for n in reversed(range(tiles)):
                back_ref[s, n, :, lanes] = state
                state = jump * state + fold[n]
            behind = state + inverse * low
            wide = slice(s * chans + g * 128, s * chans + (g + 1) * 128)
            for i in range(places):
                send_ref[i, :, wide] = jnp.where(i > place, ahead, behind)


def near_kernel(sv_ref, near_ref, local_ref):
    tiles = sv_ref.shape[1]
    chans = sv_ref.shape[3]
    for s in range(2):
        for g in range(chans // 128):
            lanes = slice(g * 128, (g + 1) * 128)
            inner = jnp.zeros((tiles, T, 128), f32)
            for j in range(T):
                inner = inner + near_ref[T - j : 2 * T - j, lanes][None] * sv_ref[s, :, j : j + 1, lanes]
            local_ref[s, :, :, lanes] = inner


def fetch_columns(chunks, wo_ref, w_buf, sems):
    tp = lax.axis_size("tp")
    place = lax.axis_index("tp")
    chans = w_buf.shape[2]
    copies = []
    for n, (column, hop) in enumerate(chunks):
        block = shard_at(place, column, hop, tp)
        pair = (
            pltpu.make_async_copy(wo_ref.at[:, rows_of(block, chans)], w_buf.at[n, 0], sems.at[n, 0]),
            pltpu.make_async_copy(wo_ref.at[:, rows_of(tp - 1 - block, chans)], w_buf.at[n, 1], sems.at[n, 1]),
        )
        for copy in pair:
            copy.start()
        copies.append(pair)
    return copies


def partial_chunk(n, copies, z_ref, w_buf, flip):
    chans = w_buf.shape[2]
    for copy in copies[n]:
        copy.wait()
    far = jnp.dot(w_buf[n, 1], flip, preferred_element_type=f32).astype(bf16)
    out = jnp.dot(z_ref[:, :chans], w_buf[n, 0], preferred_element_type=f32)
    return out + jnp.dot(z_ref[:, chans:], far, preferred_element_type=f32)


def gated_kernel(
    chunks, recv_ref, fore_ref, back_ref, local_ref, gates_ref, above_ref, below_ref, gt_ref, rates_ref,
    spread_f_ref, spread_b_ref, wo_ref, z_ref, *refs,
):
    outs, (pad_ref, st_ref, w_buf, sems) = refs[: len(chunks)], refs[len(chunks) :]
    rows = gates_ref.shape[0]
    chans = gates_ref.shape[1] // 2
    tiles = rows // T
    place = lax.axis_index("seq")
    places = lax.axis_size("seq")
    copies = fetch_columns(chunks, wo_ref, w_buf, sems)
    for s in range(2):
        wide = slice(s * chans, (s + 1) * chans)
        g = gates_ref[:, wide]
        pad_ref[0:8, :] = below_ref[:, wide]
        pad_ref[8 : 8 + rows, :] = g
        pad_ref[8 + rows : 16 + rows, :] = above_ref[:, wide]
        a, c = (0, 2) if s == 0 else (2, 0)
        ta, tb, tc = gt_ref[a : a + 1, :], gt_ref[1:2, :], gt_ref[c : c + 1, :]
        sg = ta * pad_ref[7 : 7 + rows, :] + tb * g + tc * pad_ref[9 : 9 + rows, :]
        for g2 in range(chans // 128):
            lanes = slice(g2 * 128, (g2 + 1) * 128)
            wide = slice(s * chans + g2 * 128, s * chans + (g2 + 1) * 128)
            rates = rates_ref[:, lanes]
            hop = jnp.exp(-rates * float(rows))
            jump = jnp.exp(-rates * float(T))
            carry_f = jnp.zeros((16, 128), f32)
            carry_b = jnp.zeros((16, 128), f32)
            for j in range(places):
                r = places - 1 - j
                carry_f = jnp.where(j < place, carry_f * hop + recv_ref[j, :, wide], carry_f)
                carry_b = jnp.where(r > place, carry_b * hop + recv_ref[r, :, wide], carry_b)
            for n in range(tiles):
                m = tiles - 1 - n
                st_ref[0, n] = fore_ref[s, n, :, lanes] + carry_f
                st_ref[1, m] = back_ref[s, m, :, lanes] + carry_b
                carry_f = carry_f * jump
                carry_b = carry_b * jump
            conv = local_ref[s, :, :, lanes]
            for m in range(16):
                conv = conv + spread_f_ref[m, :, lanes][None] * st_ref[0, :, m : m + 1, :]
            for m in range(16):
                conv = conv + spread_b_ref[m, :, lanes][None] * st_ref[1, :, m : m + 1, :]
            z_ref[:, wide] = (sg[:, lanes] * conv.reshape(rows, 128)).astype(bf16)
    flip = reversal(chans)
    for n, ref in enumerate(outs):
        ref[...] = partial_chunk(n, copies, z_ref, w_buf, flip).astype(bf16)


def rest_kernel(chunks, z_ref, wo_ref, *refs):
    outs, (w_buf, sems) = refs[:-2], refs[-2:]
    copies = fetch_columns(chunks, wo_ref, w_buf, sems)
    flip = reversal(w_buf.shape[2])
    for n in range(len(chunks)):
        outs[n // 2][n % 2] = partial_chunk(n, copies, z_ref, w_buf, flip).astype(bf16)


def far_memory(*arrays):
    return [pltpu.with_memory_space_constraint(a, pltpu.HBM) for a in arrays]


def whole(shape):
    return pl.BlockSpec(shape, lambda *_: (0,) * len(shape))


remote = pl.BlockSpec(memory_space=pl.ANY)


def body(
    hidden, norm_gain, value_weight, gate_weight, value_taps, gate_taps, rates, residues, out_weight
):
    rows, chans = hidden.shape
    tp = lax.axis_size("tp")
    ring = tp // 2
    places = lax.axis_size("seq")
    modes = rates.shape[0]
    tiles = rows // T
    shape = pltpu.HBM
    params = pltpu.CompilerParams(vmem_limit_bytes=24 << 20)

    def turn(a, hop):
        return lax.ppermute(
            a, "tp", [(c * ring + i, c * ring + (i + hop) % ring) for c in range(2) for i in range(ring)]
        )

    def across(a):
        return lax.ppermute(a, "tp", [(i, (i + ring) % tp) for i in range(tp)])

    powers, near, spread_f, spread_b = pl.pallas_call(
        tables_kernel,
        out_shape=(
            shape((T + 2, modes, chans), f32),
            shape((2 * T + 8, chans), f32),
            shape((modes, T, chans), f32),
            shape((modes, T, chans), f32),
        ),
        compiler_params=params,
        name="tables",
    )(rates, residues)
    gain = norm_gain.reshape(tp, 1, chans)
    value_weight, gate_weight, out_weight = far_memory(value_weight, gate_weight, out_weight)

    ups, downs = [], []
    ahead = behind = jnp.stack([hidden, across(hidden)])
    start = ahead
    for _ in range(3):
        ahead, behind = turn(ahead, 1), turn(behind, -1)
        ups.append(ahead)
        downs.append(behind)
    last_up, last_down = turn(ahead[0], 1), turn(behind[1], -1)

    def project(arrays, slots, carried):
        return pl.pallas_call(
            functools.partial(early_kernel, slots, len(arrays), not carried),
            in_specs=[remote] * len(arrays)
            + [whole(gain.shape), remote, remote]
            + [whole(a.shape) for a in carried],
            out_specs=[whole((2, rows, 2 * chans)), whole((rows, chans))],
            out_shape=(shape((2, rows, 2 * chans), f32), shape((rows, chans), f32)),
            scratch_shapes=[
                pltpu.VMEM((len(slots), rows, chans), bf16),
                pltpu.VMEM((len(slots), 2, chans, 2 * chans), bf16),
                pltpu.SemaphoreType.DMA((len(slots), 5)),
            ],
            compiler_params=params,
            cost_estimate=pl.CostEstimate(
                flops=len(slots) * 10 * chans**3, transcendentals=0, bytes_accessed=len(slots) * 10 * chans**2
            ),
            name="project",
        )(*arrays, gain, value_weight, gate_weight, *carried)

    def pair_slots(hops):
        return tuple((n, c, c, hop) for n, hop in enumerate(hops) for c in range(2))

    carried = project([start, ups[0], downs[0], ups[1], downs[1]], pair_slots((0, -1, 1, -2, 2)), ())
    carried = project([ups[2], downs[2]], pair_slots((-3, 3)), far_memory(*carried))

    slots = ((0, None, 0, -4), (1, None, 1, 4))
    send, fore, back, sv, gates, first, last = pl.pallas_call(
        functools.partial(states_kernel, slots, 2),
        in_specs=[remote, remote, whole(gain.shape), remote, remote]
        + [whole(a.shape) for a in carried]
        + [whole(value_taps.shape), whole(powers.shape)],
        out_specs=[
            whole((places, modes, 2 * chans)),
            whole((2, tiles, modes, chans)),
            whole((2, tiles, modes, chans)),
            whole((2, tiles, T, chans)),
            whole((rows, 2 * chans)),
            whole((8, 2 * chans)),
            whole((8, 2 * chans)),
        ],
        out_shape=(
            shape((places, modes, 2 * chans), f32),
            shape((2, tiles, modes, chans), f32),
            shape((2, tiles, modes, chans), f32),
            shape((2, tiles, T, chans), f32),
            shape((rows, 2 * chans), f32),
            shape((8, 2 * chans), f32),
            shape((8, 2 * chans), f32),
        ),
        scratch_shapes=[
            pltpu.VMEM((2, rows, 2 * chans), f32),
            pltpu.VMEM((rows, chans), f32),
            pltpu.VMEM((rows + 16, chans), f32),
            pltpu.VMEM((2, rows, chans), bf16),
            pltpu.VMEM((2, 2, chans, 2 * chans), bf16),
            pltpu.SemaphoreType.DMA((2, 5)),
        ],
        compiler_params=params,
        name="states",
    )(
        last_up, last_down, gain, value_weight, gate_weight, *far_memory(*carried), value_taps,
        *far_memory(powers),
    )

    recv = lax.all_to_all(send, "seq", split_axis=0, concat_axis=0)
    up = [(i, i + 1) for i in range(places - 1)]
    below = lax.ppermute(last, "seq", up)
    above = lax.ppermute(first, "seq", [(b, a) for a, b in up])

    local = pl.pallas_call(
        near_kernel,
        out_shape=shape((2, tiles, T, chans), f32),
        compiler_params=params,
        name="near",
    )(*far_memory(sv, near))

    chunks = ((0, 4), (1, 4))
    square = shape((rows, chans), bf16)
    pair = shape((2, rows, chans), bf16)
    inputs = (
        recv, *far_memory(fore, back, local, gates), above, below, gate_taps, rates,
        *far_memory(spread_f, spread_b),
    )
    z, out_up, out_down = pl.pallas_call(
        functools.partial(gated_kernel, chunks),
        in_specs=[whole(a.shape) for a in inputs] + [remote],
        out_specs=[whole((rows, 2 * chans)), whole((rows, chans)), whole((rows, chans))],
        out_shape=(shape((rows, 2 * chans), bf16), square, square),
        scratch_shapes=[
            pltpu.VMEM((rows + 16, chans), f32),
            pltpu.VMEM((2, tiles, modes, 128), f32),
            pltpu.VMEM((len(chunks), 2, chans, chans), bf16),
            pltpu.SemaphoreType.DMA((len(chunks), 2)),
        ],
        compiler_params=params,
        name="gated",
    )(*inputs, out_weight)
    hops = (3, -3, 2, -2, 1, -1, 0)
    chunks = tuple((c, hop) for hop in hops for c in range(2))
    parts = pl.pallas_call(
        functools.partial(rest_kernel, chunks),
        in_specs=[whole(z.shape), remote],
        out_specs=[whole((2, rows, chans))] * len(hops),
        out_shape=(pair,) * len(hops),
        scratch_shapes=[
            pltpu.VMEM((len(chunks), 2, chans, chans), bf16),
            pltpu.SemaphoreType.DMA((len(chunks), 2)),
        ],
        compiler_params=params,
        cost_estimate=pl.CostEstimate(
            flops=len(chunks) * 6 * chans**3, transcendentals=0, bytes_accessed=len(chunks) * 6 * chans**2
        ),
        name="rest",
    )(*far_memory(z), out_weight)

    up_sum, down_sum = turn(out_up, 1), turn(out_down, -1)
    nothing = jnp.zeros_like(up_sum, f32)
    up_sum = jnp.stack([up_sum.astype(f32), nothing])
    down_sum = jnp.stack([nothing, down_sum.astype(f32)])
    for hop in range(3):
        ups_now = (parts[2 * hop].astype(f32) + up_sum).astype(bf16)
        downs_now = (parts[2 * hop + 1].astype(f32) + down_sum).astype(bf16)
        up_sum, down_sum = turn(ups_now, 1).astype(f32), turn(downs_now, -1).astype(f32)
    total = parts[6].astype(f32) + up_sum + down_sum
    other = across(total[1].astype(bf16))
    return (total[0] + other.astype(f32)).astype(bf16)


def solution(mesh):
    in_specs = (
        P("seq", "tp"),
        P(),
        P(None, "tp"),
        P(None, "tp"),
        P(None, "tp"),
        P(None, "tp"),
        P(None, "tp"),
        P(None, "tp"),
        P("tp", None),
    )
    out_specs = P("seq", "tp")
    return jax.shard_map(body, mesh=mesh, in_specs=in_specs, out_specs=out_specs, check_vma=False)
```

time: 167 us -> 132 us (0.79)
  blocking collectives: 74.4 us -> 0 us
  starting transfers between devices: 9.35 us -> 45.3 us
  Pallas kernels: 29.1 us -> 36.3 us
  waiting for transfers between devices: 48.8 us -> 42.1 us
  other arithmetic: 0.96 us -> 4.96 us
    all_to_all x2 -> x0, blocking collectives: 74.4 us -> none  [the longest x1 54.8 us: body(): parts = lax.all_to_all(partial, 'tp', split_axis=0, concat_axis=0)]
    all_to_all x1, waiting for transfers between devices: 48.8 us -> 0.01 us  [body(): recv = lax.all_to_all(send, 'seq', split_axis=0, concat_axis=0)]
    ppermute x0 -> x20, waiting for transfers between devices: none -> 42.1 us  [the longest x16 30.3 us: turn(): lax.ppermute(a, 'tp', [(c * ring + i, c * ring + (i + hop) % ring) for c...]
    ppermute x0 -> x20, starting transfers between devices: none -> 37.8 us  [the longest x16 29.1 us: turn(): lax.ppermute(a, 'tp', [(c * ring + i, c * ring + (i + hop) % ring) for c...]
    pallas_call x2 -> x6, Pallas kernels: 29 us -> 35.3 us  [the longest x2 10.9 us: project(): pl.pallas_call(functools.partial(early_kernel, slots, len(arrays), not ca...]
    convert_element_type x0 -> x7, other arithmetic: none -> 3.94 us  [the longest x3 2.15 us: body(): downs_now = (parts[2 * hop + 1].astype(f32) + down_sum).astype(bf16)]
    broadcast_in_dim x1 -> x0, local copies, waits for them, and re-layouts: 2.46 us -> none  [body(): jnp.broadcast_to(hidden[None], (tp, rows, chans))]
    unnamed x10 -> x20, local copies, waits for them, and re-layouts: 0.02 us -> 2.18 us
  transfers between devices with their start and end apart: 1 -> 21, of which waited for: 1 -> 12; matrix products, arithmetic and copies ran while one was open for 0% -> 3% of each run, Pallas kernels for 0% -> 19%
where the time goes in v2:
time: 132 us; the launch traced here: 131 us
  starting transfers between devices  45.3 us (34%)
  waiting for transfers between devices  42.1 us (32%)
  Pallas kernels  36.3 us (27%)
  other arithmetic  4.96 us (4%)
  local copies, waits for them, and re-layouts  2.22 us (2%)
    ppermute x16, waiting for transfers between devices, turn(): lax.ppermute(a, 'tp', [(c * ring + i, c * ring + (i + hop) % ring) for c...  30.3 us
    ppermute x16, starting transfers between devices, turn(): lax.ppermute(a, 'tp', [(c * ring + i, c * ring + (i + hop) % ring) for c...  29.1 us
    pallas_call x2, Pallas kernels, project(): pl.pallas_call(functools.partial(early_kernel, slots, len(arrays), not ca...  10.9 us
    pallas_call x1, Pallas kernels, body(): pl.pallas_call(functools.partial(rest_kernel, chunks), in_specs=[whole(z....  9.53 us
    ppermute x2, waiting for transfers between devices, across(): return lax.ppermute(a, 'tp', [(i, (i + ring) % tp) for i in range(tp)])  8.02 us
    all_to_all x1, starting transfers between devices, body(): recv = lax.all_to_all(send, 'seq', split_axis=0, concat_axis=0)  7.47 us
    pallas_call x1, Pallas kernels, body(): pl.pallas_call(functools.partial(states_kernel, slots, 2), in_specs=[remo...  6.37 us
    pallas_call x1, Pallas kernels, body(): pl.pallas_call(functools.partial(gated_kernel, chunks), in_specs=[whole(a...  5.28 us
  transfers between devices with their start and end apart: 21, of which 12 were waited for; matrix products, arithmetic and copies ran while one was open for 3% of the time, Pallas kernels for 19%

profile of v2, /device:TPU:4, one launch (start us, length us, event | category | flops | bytes accessed | tf_op | source)
XLA Modules:
  0.0 131.1 jit_solution(209431893917899498)
XLA Ops:
  0.0 1.2 collective-permute-start
  1.2 4.2 %collective-permute-done = bf16[256,256]{1,0:T(8,128)(2,1)S(1)} collective-permute-done((bf16[256,256]{1,0:T(8,128)(2,1)}, bf16[256,256]{1,0:T(8,128)(2,1)S(1)}, u32[]{:S(2)}, u32[]{:S(2)}) %collective-permute-start) | collective-permute-done | bytes 131104 | tf_op jit(solution)/shard_map/ppermute | solution.py:293
  6.4 5.9 %collective-permute-start.5 = (bf16[2,256,256]{2,1,0:T(8,128)(2,1)S(1)}, bf16[2,256,256]{2,1,0:T(8,128)(2,1)S(1)}, u32[]{:S(2)}, u32[]{:S(2)}) collective-permute-start(bf16[2,256,256]{2,1,0:T(8,128)(2,1)S(1)} %pad_maximum_fusion.refs_0_), channel_id=1, source_target_pairs={{0,7},{1,0},{2,1},{3,2},{4,3},{5,4},{6,5},{7,6},{8,15},{9,8},{10,9... | collective-permute-start | bytes 786440 | tf_op jit(solution)/shard_map/ppermute | solution.py:288
  12.3 4.7 %collective-permute-done.5.refs_2_ = bf16[2,256,256]{2,1,0:T(8,128)(2,1)S(1)} collective-permute-done((bf16[2,256,256]{2,1,0:T(8,128)(2,1)S(1)}, bf16[2,256,256]{2,1,0:T(8,128)(2,1)S(1)}, u32[]{:S(2)}, u32[]{:S(2)}) %collective-permute-start.5) | collective-permute-done | bytes 262176 | tf_op jit(solution)/shard_map/ppermute | solution.py:288
  17.0 3.7 %collective-permute-start.6 = (bf16[2,256,256]{2,1,0:T(8,128)(2,1)S(1)}, bf16[2,256,256]{2,1,0:T(8,128)(2,1)S(1)}, u32[]{:S(2)}, u32[]{:S(2)}) collective-permute-start(bf16[2,256,256]{2,1,0:T(8,128)(2,1)S(1)} %collective-permute-done.5.refs_2_), channel_id=1, source_target_pairs={{0,7},{1,0},{2,1},{3,2},{4,3},{5,4},{6,5},{7,6},{8,15},{9,8},{10,9... | collective-permute-start | bytes 786440 | tf_op jit(solution)/shard_map/ppermute | solution.py:288
  20.7 3.9 %collective-permute-done.6.refs_4_ = bf16[2,256,256]{2,1,0:T(8,128)(2,1)S(1)} collective-permute-done((bf16[2,256,256]{2,1,0:T(8,128)(2,1)S(1)}, bf16[2,256,256]{2,1,0:T(8,128)(2,1)S(1)}, u32[]{:S(2)}, u32[]{:S(2)}) %collective-permute-start.6) | collective-permute-done | bytes 262176 | tf_op jit(solution)/shard_map/ppermute | solution.py:288
  24.6 3.7 %collective-permute-start.7 = (bf16[2,256,256]{2,1,0:T(8,128)(2,1)S(1)}, bf16[2,256,256]{2,1,0:T(8,128)(2,1)S(1)}, u32[]{:S(2)}, u32[]{:S(2)}) collective-permute-start(bf16[2,256,256]{2,1,0:T(8,128)(2,1)S(1)} %collective-permute-done.6.refs_4_), channel_id=1, source_target_pairs={{0,7},{1,0},{2,1},{3,2},{4,3},{5,4},{6,5},{7,6},{8,15},{9,8},{10,9... | collective-permute-start | bytes 786440 | tf_op jit(solution)/shard_map/ppermute | solution.py:288
  30.7 1.7 %collective-permute-done.7.refs_1_ = bf16[2,256,256]{2,1,0:T(8,128)(2,1)S(1)} collective-permute-done((bf16[2,256,256]{2,1,0:T(8,128)(2,1)S(1)}, bf16[2,256,256]{2,1,0:T(8,128)(2,1)S(1)}, u32[]{:S(2)}, u32[]{:S(2)}) %collective-permute-start.7) | collective-permute-done | bytes 262176 | tf_op jit(solution)/shard_map/ppermute | solution.py:288
  32.5 3.8 %collective-permute-start.8 = (bf16[256,256]{1,0:T(8,128)(2,1)S(1)}, bf16[256,256]{1,0:T(8,128)(2,1)S(1)}, u32[]{:S(2)}, u32[]{:S(2)}) collective-permute-start(bf16[256,256]{1,0:T(8,128)(2,1)S(1)} %slice_bitcast_fusion.1), channel_id=1, source_target_pairs={{0,7},{1,0},{2,1},{3,2},{4,3},{5,4},{6,5},{7,6},{8,15},{9,8},{10,9... | collective-permute-start | bytes 393224 | tf_op jit(solution)/shard_map/ppermute | solution.py:288
  37.3 6.0 %project.2 = (f32[2,256,512]{2,1,0:T(8,128)}, f32[256,256]{1,0:T(8,128)}) custom-call(bf16[2,256,256]{2,1,0:T(8,128)(2,1)S(1)} %pad_maximum_fusion.refs_0_, bf16[2,256,256]{2,1,0:T(8,128)(2,1)S(1)} %collective-permute-done.1.refs_1_, bf16[2,256,256]{2,1,0:T(8,128)(2,1)S(1)} %collective-permute-done.5.refs_2_, ...), custom_call_target="tpu_custom_call" | custom-call | flops 1677721600 | bytes 6553600 | tf_op jit(solution)/shard_map/project/pallas_call | solution.py:319
  43.3 4.9 %project.3 = (f32[2,256,512]{2,1,0:T(8,128)}, f32[256,256]{1,0:T(8,128)}) custom-call(bf16[2,256,256]{2,1,0:T(8,128)(2,1)S(1)} %collective-permute-done.3.refs_0_, bf16[2,256,256]{2,1,0:T(8,128)(2,1)S(1)} %collective-permute-done.7.refs_1_, f32[16,1,256]{2,1,0:T(1,128)S(1)} %bitcast.18, bf16[4096,256]{1,0:T(8,128)(2,1)} %refs_3_.3, ...), custom_call_target="tpu_custom_call" | custom-call | flops 671088640 | bytes 2621440 | tf_op jit(solution)/shard_map/project/pallas_call | solution.py:319
  48.2 6.4 %states.1 = (f32[16,16,512]{2,1,0:T(8,128)}, f32[2,16,16,256]{3,2,1,0:T(8,128)}, f32[2,16,16,256]{3,2,1,0:T(8,128)}, f32[2,16,16,256]{3,2,1,0:T(8,128)}, f32[256...) custom-call(bf16[256,256]{1,0:T(8,128)(2,1)S(1)} %collective-permute-done.4.refs_0_, ...), custom_call_target="tpu_custom_call" | custom-call | tf_op jit(solution)/shard_map/states/pallas_call | solution.py:345
  54.6 7.5 %all-to-all-start = ((f32[16,16,512]{2,1,0:T(8,128)}), f32[16,16,512]{2,1,0:T(8,128)S(1)}, u32[]{:S(2)}, u32[]{:S(2)}) async-start(f32[16,16,512]{2,1,0:T(8,128)} %get-tuple-element.35), calls=%async_computation | async-start | bytes 1048576 | tf_op jit(solution)/shard_map/all_to_all | solution.py:383
  62.1 4.3 %collective-permute-start.9 = (f32[8,512]{1,0:T(8,128)}, f32[8,512]{1,0:T(8,128)S(1)}, u32[]{:S(2)}, u32[]{:S(2)}) collective-permute-start(f32[8,512]{1,0:T(8,128)} %get-tuple-element.41), channel_id=1, source_target_pairs={{16,0},{32,16},{48,32},{64,48},{80,64},{96,80},{112,96},{128,112},... | collective-permute-start | bytes 49160 | tf_op jit(solution)/shard_map/ppermute | solution.py:386
  66.4 1.9 %collective-permute-start.10 = (f32[8,512]{1,0:T(8,128)}, f32[8,512]{1,0:T(8,128)S(1)}, u32[]{:S(2)}, u32[]{:S(2)}) collective-permute-start(f32[8,512]{1,0:T(8,128)} %get-tuple-element.42), channel_id=1, source_target_pairs={{0,16},{16,32},{32,48},{48,64},{64,80},{80,96},{96,112},{112,128},... | collective-permute-start | bytes 49160 | tf_op jit(solution)/shard_map/ppermute | solution.py:385
  68.3 3.2 %near.1.local_ref = f32[2,16,16,256]{3,2,1,0:T(8,128)} custom-call(f32[2,16,16,256]{3,2,1,0:T(8,128)} %get-tuple-element.38.sv_ref, f32[40,256]{1,0:T(8,128)} %get-tuple-element.39.near_ref), custom_call_target="tpu_custom_call" | custom-call | tf_op jit(solution)/shard_map/near/pallas_call | solution.py:388
  71.5 3.8 %collective-permute-done.10.below_ref = f32[8,512]{1,0:T(8,128)S(1)} collective-permute-done((f32[8,512]{1,0:T(8,128)}, f32[8,512]{1,0:T(8,128)S(1)}, u32[]{:S(2)}, u32[]{:S(2)}) %collective-permute-start.10) | collective-permute-done | bytes 16416 | tf_op jit(solution)/shard_map/ppermute | solution.py:385
  75.3 5.3 %gated.1 = (bf16[256,512]{1,0:T(8,128)(2,1)}, bf16[256,256]{1,0:T(8,128)(2,1)}, bf16[256,256]{1,0:T(8,128)(2,1)}) custom-call(f32[16,16,512]{2,1,0:T(8,128)S(1)} %all-to-all-done.recv_ref, f32[2,16,16,256]{3,2,1,0:T(8,128)} %get-tuple-element.36.fore_ref, f32[2,16,16,256]{3,2,1,0:T(8,128)} %get-tuple-element.37.back_ref, f32[2,16,16,256]{3,2,1,0:T(8,128)} %near.1.local_ref, ...), custom_call_target="tpu_custom_call" | custom-call | tf_op jit(solution)/shard_map/gated/pallas_call | solution.py:402
  80.7 3.5 %collective-permute-start.15 = (bf16[256,256]{1,0:T(8,128)(2,1)}, bf16[256,256]{1,0:T(8,128)(2,1)S(1)}, u32[]{:S(2)}, u32[]{:S(2)}) collective-permute-start(bf16[256,256]{1,0:T(8,128)(2,1)} %get-tuple-element.54), channel_id=1, source_target_pairs={{0,7},{1,0},{2,1},{3,2},{4,3},{5,4},{6,5},{7,6},{8,15},{9,8},{10,9... | collective-permute-start | bytes 393224 | tf_op jit(solution)/shard_map/ppermute | solution.py:288
  84.2 9.5 %rest.1 = (bf16[2,256,256]{2,1,0:T(8,128)(2,1)}, bf16[2,256,256]{2,1,0:T(8,128)(2,1)}, bf16[2,256,256]{2,1,0:T(8,128)(2,1)}, bf16[2,256,256]{2,1,0:T(8,128)(2,1)...) custom-call(bf16[256,512]{1,0:T(8,128)(2,1)} %get-tuple-element.45.z_ref, ...), custom_call_target="tpu_custom_call" | custom-call | flops 1409286144 | bytes 5505024 | tf_op jit(solution)/shard_map/rest/pallas_call | solution.py:418
  93.8 1.1 add_convert_fusion.2
  94.9 1.8 %collective-permute-start.16 = (bf16[2,256,256]{2,1,0:T(8,128)(2,1)S(1)}, bf16[2,256,256]{2,1,0:T(8,128)(2,1)S(1)}, u32[]{:S(2)}, u32[]{:S(2)}) collective-permute-start(bf16[2,256,256]{2,1,0:T(8,128)(2,1)S(1)} %add_convert_fusion.2), channel_id=1, source_target_pairs={{0,7},{1,0},{2,1},{3,2},{4,3},{5,4},{6,5},{7,6},{8,15},{9,8},{10,9... | collective-permute-start | bytes 786440 | tf_op jit(solution)/shard_map/ppermute | solution.py:288
  98.0 4.9 %collective-permute-done.16 = bf16[2,256,256]{2,1,0:T(8,128)(2,1)S(1)} collective-permute-done((bf16[2,256,256]{2,1,0:T(8,128)(2,1)S(1)}, bf16[2,256,256]{2,1,0:T(8,128)(2,1)S(1)}, u32[]{:S(2)}, u32[]{:S(2)}) %collective-permute-start.16) | collective-permute-done | bytes 262176 | tf_op jit(solution)/shard_map/ppermute | solution.py:288
  104.0 2.0 %collective-permute-start.17 = (bf16[2,256,256]{2,1,0:T(8,128)(2,1)S(1)}, bf16[2,256,256]{2,1,0:T(8,128)(2,1)S(1)}, u32[]{:S(2)}, u32[]{:S(2)}) collective-permute-start(bf16[2,256,256]{2,1,0:T(8,128)(2,1)S(1)} %add_convert_fusion.1), channel_id=1, source_target_pairs={{0,7},{1,0},{2,1},{3,2},{4,3},{5,4},{6,5},{7,6},{8,15},{9,8},{10,9... | collective-permute-start | bytes 786440 | tf_op jit(solution)/shard_map/ppermute | solution.py:288
  106.0 1.2 collective-permute-done.12
  107.4 5.2 %collective-permute-done.17 = bf16[2,256,256]{2,1,0:T(8,128)(2,1)S(1)} collective-permute-done((bf16[2,256,256]{2,1,0:T(8,128)(2,1)S(1)}, bf16[2,256,256]{2,1,0:T(8,128)(2,1)S(1)}, u32[]{:S(2)}, u32[]{:S(2)}) %collective-permute-start.17) | collective-permute-done | bytes 262176 | tf_op jit(solution)/shard_map/ppermute | solution.py:288
  112.7 3.8 %collective-permute-start.18 = (bf16[2,256,256]{2,1,0:T(8,128)(2,1)S(1)}, bf16[2,256,256]{2,1,0:T(8,128)(2,1)S(1)}, u32[]{:S(2)}, u32[]{:S(2)}) collective-permute-start(bf16[2,256,256]{2,1,0:T(8,128)(2,1)S(1)} %add_convert_fusion), channel_id=1, source_target_pairs={{0,7},{1,0},{2,1},{3,2},{4,3},{5,4},{6,5},{7,6},{8,15},{9,8},{10,9... | collective-permute-start | bytes 786440 | tf_op jit(solution)/shard_map/ppermute | solution.py:288
  116.5 1.0 collective-permute-done.13
  117.7 2.7 %collective-permute-done.18 = bf16[2,256,256]{2,1,0:T(8,128)(2,1)S(1)} collective-permute-done((bf16[2,256,256]{2,1,0:T(8,128)(2,1)S(1)}, bf16[2,256,256]{2,1,0:T(8,128)(2,1)S(1)}, u32[]{:S(2)}, u32[]{:S(2)}) %collective-permute-start.18) | collective-permute-done | bytes 262176 | tf_op jit(solution)/shard_map/ppermute | solution.py:288
  120.4 4.9 %collective-permute-done.14 = bf16[2,256,256]{2,1,0:T(8,128)(2,1)S(1)} collective-permute-done((bf16[2,256,256]{2,1,0:T(8,128)(2,1)S(1)}, bf16[2,256,256]{2,1,0:T(8,128)(2,1)S(1)}, u32[]{:S(2)}, u32[]{:S(2)}) %collective-permute-start.14) | collective-permute-done | bytes 262176 | tf_op jit(solution)/shard_map/ppermute | solution.py:288
  125.4 1.3 collective-permute-start.19
  126.6 3.8 %collective-permute-done.19 = bf16[256,256]{1,0:T(8,128)(2,1)S(1)} collective-permute-done((bf16[256,256]{1,0:T(8,128)(2,1)S(1)}, bf16[256,256]{1,0:T(8,128)(2,1)S(1)}, u32[]{:S(2)}, u32[]{:S(2)}) %collective-permute-start.19) | collective-permute-done | bytes 131104 | tf_op jit(solution)/shard_map/ppermute | solution.py:293
  (49 shorter events, 8.0 us)
Async XLA Ops:
  0.0 5.4 %collective-permute-start = (bf16[256,256]{1,0:T(8,128)(2,1)}, bf16[256,256]{1,0:T(8,128)(2,1)S(1)}, u32[]{:S(2)}, u32[]{:S(2)}) collective-permute-start(bf16[256,256]{1,0:T(8,128)(2,1)} %param.9), channel_id=1, source_target_pairs={{0,8},{1,9},{2,10},{3,11},{4,12},{5,13},{6,14},{7,15},{8,0},{9,1},... | collective-permute-start | bytes 393224 | tf_op jit(solution)/shard_map/ppermute | solution.py:293
  6.4 10.6 %collective-permute-start.5 = (bf16[2,256,256]{2,1,0:T(8,128)(2,1)S(1)}, bf16[2,256,256]{2,1,0:T(8,128)(2,1)S(1)}, u32[]{:S(2)}, u32[]{:S(2)}) collective-permute-start(bf16[2,256,256]{2,1,0:T(8,128)(2,1)S(1)} %pad_maximum_fusion.refs_0_), channel_id=1, source_target_pairs={{0,7},{1,0},{2,1},{3,2},{4,3},{5,4},{6,5},{7,6},{8,15},{9,8},{10,9... | collective-permute-start | bytes 786440 | tf_op jit(solution)/shard_map/ppermute | solution.py:288
  12.3 8.4 %collective-permute-start.1 = (bf16[2,256,256]{2,1,0:T(8,128)(2,1)S(1)}, bf16[2,256,256]{2,1,0:T(8,128)(2,1)S(1)}, u32[]{:S(2)}, u32[]{:S(2)}) collective-permute-start(bf16[2,256,256]{2,1,0:T(8,128)(2,1)S(1)} %pad_maximum_fusion.refs_0_), channel_id=1, source_target_pairs={{0,1},{1,2},{2,3},{3,4},{4,5},{5,6},{6,7},{7,0},{8,9},{9,10},{10,1... | collective-permute-start | bytes 786440 | tf_op jit(solution)/shard_map/ppermute | solution.py:288
  17.0 7.6 %collective-permute-start.6 = (bf16[2,256,256]{2,1,0:T(8,128)(2,1)S(1)}, bf16[2,256,256]{2,1,0:T(8,128)(2,1)S(1)}, u32[]{:S(2)}, u32[]{:S(2)}) collective-permute-start(bf16[2,256,256]{2,1,0:T(8,128)(2,1)S(1)} %collective-permute-done.5.refs_2_), channel_id=1, source_target_pairs={{0,7},{1,0},{2,1},{3,2},{4,3},{5,4},{6,5},{7,6},{8,15},{9,8},{10,9... | collective-permute-start | bytes 786440 | tf_op jit(solution)/shard_map/ppermute | solution.py:288
  20.7 7.6 %collective-permute-start.2 = (bf16[2,256,256]{2,1,0:T(8,128)(2,1)S(1)}, bf16[2,256,256]{2,1,0:T(8,128)(2,1)S(1)}, u32[]{:S(2)}, u32[]{:S(2)}) collective-permute-start(bf16[2,256,256]{2,1,0:T(8,128)(2,1)S(1)} %collective-permute-done.1.refs_1_), channel_id=1, source_target_pairs={{0,1},{1,2},{2,3},{3,4},{4,5},{5,6},{6,7},{7,0},{8,9},{9,10},{10,1... | collective-permute-start | bytes 786440 | tf_op jit(solution)/shard_map/ppermute | solution.py:288
  24.6 7.9 %collective-permute-start.7 = (bf16[2,256,256]{2,1,0:T(8,128)(2,1)S(1)}, bf16[2,256,256]{2,1,0:T(8,128)(2,1)S(1)}, u32[]{:S(2)}, u32[]{:S(2)}) collective-permute-start(bf16[2,256,256]{2,1,0:T(8,128)(2,1)S(1)} %collective-permute-done.6.refs_4_), channel_id=1, source_target_pairs={{0,7},{1,0},{2,1},{3,2},{4,3},{5,4},{6,5},{7,6},{8,15},{9,8},{10,9... | collective-permute-start | bytes 786440 | tf_op jit(solution)/shard_map/ppermute | solution.py:288
  28.3 8.0 %collective-permute-start.3 = (bf16[2,256,256]{2,1,0:T(8,128)(2,1)S(1)}, bf16[2,256,256]{2,1,0:T(8,128)(2,1)S(1)}, u32[]{:S(2)}, u32[]{:S(2)}) collective-permute-start(bf16[2,256,256]{2,1,0:T(8,128)(2,1)S(1)} %collective-permute-done.2.refs_3_), channel_id=1, source_target_pairs={{0,1},{1,2},{2,3},{3,4},{4,5},{5,6},{6,7},{7,0},{8,9},{9,10},{10,1... | collective-permute-start | bytes 786440 | tf_op jit(solution)/shard_map/ppermute | solution.py:288
  28.3 0.7 copy-start.1
  29.0 0.7 copy-start.3
  32.5 15.7 %collective-permute-start.8 = (bf16[256,256]{1,0:T(8,128)(2,1)S(1)}, bf16[256,256]{1,0:T(8,128)(2,1)S(1)}, u32[]{:S(2)}, u32[]{:S(2)}) collective-permute-start(bf16[256,256]{1,0:T(8,128)(2,1)S(1)} %slice_bitcast_fusion.1), channel_id=1, source_target_pairs={{0,7},{1,0},{2,1},{3,2},{4,3},{5,4},{6,5},{7,6},{8,15},{9,8},{10,9... | collective-permute-start | bytes 393224 | tf_op jit(solution)/shard_map/ppermute | solution.py:288
  36.3 11.9 %collective-permute-start.4 = (bf16[256,256]{1,0:T(8,128)(2,1)S(1)}, bf16[256,256]{1,0:T(8,128)(2,1)S(1)}, u32[]{:S(2)}, u32[]{:S(2)}) collective-permute-start(bf16[256,256]{1,0:T(8,128)(2,1)S(1)} %slice_bitcast_fusion.2), channel_id=1, source_target_pairs={{0,1},{1,2},{2,3},{3,4},{4,5},{5,6},{6,7},{7,0},{8,9},{9,10},{10,1... | collective-permute-start | bytes 393224 | tf_op jit(solution)/shard_map/ppermute | solution.py:288
  36.5 0.7 copy-start
  43.2 5.0 %copy-start.4 = (f32[3,256]{1,0:T(4,128)S(1)}, f32[3,256]{1,0:T(4,128)}, u32[]{:S(2)}) copy-start(f32[3,256]{1,0:T(4,128)} %refs_7_.3) | copy-start | bytes 9220
  54.6 20.7 %copy-start.2 = (f32[16,256]{1,0:T(8,128)S(1)}, f32[16,256]{1,0:T(8,128)}, u32[]{:S(2)}) copy-start(f32[16,256]{1,0:T(8,128)} %rates_ref.3) | copy-start | bytes 49156
  54.6 20.7 %copy-start.5 = (f32[3,256]{1,0:T(4,128)S(1)}, f32[3,256]{1,0:T(4,128)}, u32[]{:S(2)}) copy-start(f32[3,256]{1,0:T(4,128)} %gt_ref.1) | copy-start | bytes 9220
  54.6 20.7 %all-to-all-start = ((f32[16,16,512]{2,1,0:T(8,128)}), f32[16,16,512]{2,1,0:T(8,128)S(1)}, u32[]{:S(2)}, u32[]{:S(2)}) async-start(f32[16,16,512]{2,1,0:T(8,128)} %get-tuple-element.35), calls=%async_computation | async-start | bytes 1048576 | tf_op jit(solution)/shard_map/all_to_all | solution.py:383
  62.1 9.4 %collective-permute-start.9 = (f32[8,512]{1,0:T(8,128)}, f32[8,512]{1,0:T(8,128)S(1)}, u32[]{:S(2)}, u32[]{:S(2)}) collective-permute-start(f32[8,512]{1,0:T(8,128)} %get-tuple-element.41), channel_id=1, source_target_pairs={{16,0},{32,16},{48,32},{64,48},{80,64},{96,80},{112,96},{128,112},... | collective-permute-start | bytes 49160 | tf_op jit(solution)/shard_map/ppermute | solution.py:386
  66.4 8.9 %collective-permute-start.10 = (f32[8,512]{1,0:T(8,128)}, f32[8,512]{1,0:T(8,128)S(1)}, u32[]{:S(2)}, u32[]{:S(2)}) collective-permute-start(f32[8,512]{1,0:T(8,128)} %get-tuple-element.42), channel_id=1, source_target_pairs={{0,16},{16,32},{32,48},{48,64},{64,80},{80,96},{96,112},{112,128},... | collective-permute-start | bytes 49160 | tf_op jit(solution)/shard_map/ppermute | solution.py:385
  80.6 16.1 %collective-permute-start.11 = (bf16[256,256]{1,0:T(8,128)(2,1)}, bf16[256,256]{1,0:T(8,128)(2,1)S(1)}, u32[]{:S(2)}, u32[]{:S(2)}) collective-permute-start(bf16[256,256]{1,0:T(8,128)(2,1)} %get-tuple-element.50), channel_id=1, source_target_pairs={{0,1},{1,2},{2,3},{3,4},{4,5},{5,6},{6,7},{7,0},{8,9},{9,10},{10,1... | collective-permute-start | bytes 393224 | tf_op jit(solution)/shard_map/ppermute | solution.py:288
  80.7 13.1 %collective-permute-start.15 = (bf16[256,256]{1,0:T(8,128)(2,1)}, bf16[256,256]{1,0:T(8,128)(2,1)S(1)}, u32[]{:S(2)}, u32[]{:S(2)}) collective-permute-start(bf16[256,256]{1,0:T(8,128)(2,1)} %get-tuple-element.54), channel_id=1, source_target_pairs={{0,7},{1,0},{2,1},{3,2},{4,3},{5,4},{6,5},{7,6},{8,15},{9,8},{10,9... | collective-permute-start | bytes 393224 | tf_op jit(solution)/shard_map/ppermute | solution.py:288
  93.7 13.5 %copy-start.9 = (bf16[2,256,256]{2,1,0:T(8,128)(2,1)S(1)}, bf16[2,256,256]{2,1,0:T(8,128)(2,1)}, u32[]{:S(2)}) copy-start(bf16[2,256,256]{2,1,0:T(8,128)(2,1)} %get-tuple-element.48) | copy-start | bytes 786436
  93.8 18.9 %copy-start.8 = (bf16[2,256,256]{2,1,0:T(8,128)(2,1)S(1)}, bf16[2,256,256]{2,1,0:T(8,128)(2,1)}, u32[]{:S(2)}) copy-start(bf16[2,256,256]{2,1,0:T(8,128)(2,1)} %get-tuple-element.51) | copy-start | bytes 786436
  93.8 23.7 %copy-start.7 = (bf16[2,256,256]{2,1,0:T(8,128)(2,1)S(1)}, bf16[2,256,256]{2,1,0:T(8,128)(2,1)}, u32[]{:S(2)}) copy-start(bf16[2,256,256]{2,1,0:T(8,128)(2,1)} %get-tuple-element.47) | copy-start | bytes 786436
  93.8 31.5 %copy-start.6 = (bf16[2,256,256]{2,1,0:T(8,128)(2,1)S(1)}, bf16[2,256,256]{2,1,0:T(8,128)(2,1)}, u32[]{:S(2)}) copy-start(bf16[2,256,256]{2,1,0:T(8,128)(2,1)} %get-tuple-element.46) | copy-start | bytes 786436
  94.9 8.1 %collective-permute-start.16 = (bf16[2,256,256]{2,1,0:T(8,128)(2,1)S(1)}, bf16[2,256,256]{2,1,0:T(8,128)(2,1)S(1)}, u32[]{:S(2)}, u32[]{:S(2)}) collective-permute-start(bf16[2,256,256]{2,1,0:T(8,128)(2,1)S(1)} %add_convert_fusion.2), channel_id=1, source_target_pairs={{0,7},{1,0},{2,1},{3,2},{4,3},{5,4},{6,5},{7,6},{8,15},{9,8},{10,9... | collective-permute-start | bytes 786440 | tf_op jit(solution)/shard_map/ppermute | solution.py:288
  97.6 9.6 %collective-permute-start.12 = (bf16[2,256,256]{2,1,0:T(8,128)(2,1)S(1)}, bf16[2,256,256]{2,1,0:T(8,128)(2,1)S(1)}, u32[]{:S(2)}, u32[]{:S(2)}) collective-permute-start(bf16[2,256,256]{2,1,0:T(8,128)(2,1)S(1)} %add_convert_fusion.5), channel_id=1, source_target_pairs={{0,1},{1,2},{2,3},{3,4},{4,5},{5,6},{6,7},{7,0},{8,9},{9,10},{10,1... | collective-permute-start | bytes 786440 | tf_op jit(solution)/shard_map/ppermute | solution.py:288
  104.0 8.7 %collective-permute-start.17 = (bf16[2,256,256]{2,1,0:T(8,128)(2,1)S(1)}, bf16[2,256,256]{2,1,0:T(8,128)(2,1)S(1)}, u32[]{:S(2)}, u32[]{:S(2)}) collective-permute-start(bf16[2,256,256]{2,1,0:T(8,128)(2,1)S(1)} %add_convert_fusion.1), channel_id=1, source_target_pairs={{0,7},{1,0},{2,1},{3,2},{4,3},{5,4},{6,5},{7,6},{8,15},{9,8},{10,9... | collective-permute-start | bytes 786440 | tf_op jit(solution)/shard_map/ppermute | solution.py:288
  107.3 10.2 %collective-permute-start.13 = (bf16[2,256,256]{2,1,0:T(8,128)(2,1)S(1)}, bf16[2,256,256]{2,1,0:T(8,128)(2,1)S(1)}, u32[]{:S(2)}, u32[]{:S(2)}) collective-permute-start(bf16[2,256,256]{2,1,0:T(8,128)(2,1)S(1)} %add_convert_fusion.4), channel_id=1, source_target_pairs={{0,1},{1,2},{2,3},{3,4},{4,5},{5,6},{6,7},{7,0},{8,9},{9,10},{10,1... | collective-permute-start | bytes 786440 | tf_op jit(solution)/shard_map/ppermute | solution.py:288
  112.7 7.7 %collective-permute-start.18 = (bf16[2,256,256]{2,1,0:T(8,128)(2,1)S(1)}, bf16[2,256,256]{2,1,0:T(8,128)(2,1)S(1)}, u32[]{:S(2)}, u32[]{:S(2)}) collective-permute-start(bf16[2,256,256]{2,1,0:T(8,128)(2,1)S(1)} %add_convert_fusion), channel_id=1, source_target_pairs={{0,7},{1,0},{2,1},{3,2},{4,3},{5,4},{6,5},{7,6},{8,15},{9,8},{10,9... | collective-permute-start | bytes 786440 | tf_op jit(solution)/shard_map/ppermute | solution.py:288
  117.6 7.7 %collective-permute-start.14 = (bf16[2,256,256]{2,1,0:T(8,128)(2,1)S(1)}, bf16[2,256,256]{2,1,0:T(8,128)(2,1)S(1)}, u32[]{:S(2)}, u32[]{:S(2)}) collective-permute-start(bf16[2,256,256]{2,1,0:T(8,128)(2,1)S(1)} %add_convert_fusion.3), channel_id=1, source_target_pairs={{0,1},{1,2},{2,3},{3,4},{4,5},{5,6},{6,7},{7,0},{8,9},{9,10},{10,1... | collective-permute-start | bytes 786440 | tf_op jit(solution)/shard_map/ppermute | solution.py:288
  125.4 5.1 %collective-permute-start.19 = (bf16[256,256]{1,0:T(8,128)(2,1)S(1)}, bf16[256,256]{1,0:T(8,128)(2,1)S(1)}, u32[]{:S(2)}, u32[]{:S(2)}) collective-permute-start(bf16[256,256]{1,0:T(8,128)(2,1)S(1)} %fusion.2), channel_id=1, source_target_pairs={{0,8},{1,9},{2,10},{3,11},{4,12},{5,13},{6,14},{7,15},{8,0},{9,1},... | collective-permute-start | bytes 393224 | tf_op jit(solution)/shard_map/ppermute | solution.py:293

commit v3 on v2

--- a/solution.py
+++ b/solution.py
@@ -292,6 +292,7 @@
     def across(a):
         return lax.ppermute(a, "tp", [(i, (i + ring) % tp) for i in range(tp)])
 
+    rates, residues = far_memory(rates, residues)
     powers, near, spread_f, spread_b = pl.pallas_call(
         tables_kernel,
         out_shape=(
@@ -305,15 +306,7 @@
     )(rates, residues)
     gain = norm_gain.reshape(tp, 1, chans)
     value_weight, gate_weight, out_weight = far_memory(value_weight, gate_weight, out_weight)
-
-    ups, downs = [], []
-    ahead = behind = jnp.stack([hidden, across(hidden)])
-    start = ahead
-    for _ in range(3):
-        ahead, behind = turn(ahead, 1), turn(behind, -1)
-        ups.append(ahead)
-        downs.append(behind)
-    last_up, last_down = turn(ahead[0], 1), turn(behind[1], -1)
+    gain, value_taps, gate_taps = far_memory(gain, value_taps, gate_taps)
 
     def project(arrays, slots, carried):
         return pl.pallas_call(
@@ -338,8 +331,17 @@
     def pair_slots(hops):
         return tuple((n, c, c, hop) for n, hop in enumerate(hops) for c in range(2))
 
-    carried = project([start, ups[0], downs[0], ups[1], downs[1]], pair_slots((0, -1, 1, -2, 2)), ())
-    carried = project([ups[2], downs[2]], pair_slots((-3, 3)), far_memory(*carried))
+    start = jnp.stack([hidden, across(hidden)])
+    up1, down1 = turn(start, 1), turn(start, -1)
+    up1, down1, powers, near, spread_f, spread_b = lax.optimization_barrier(
+        (up1, down1, powers, near, spread_f, spread_b)
+    )
+    up2, down2 = turn(up1, 1), turn(down1, -1)
+    up3, down3 = turn(up2, 1), turn(down2, -1)
+    carried = project([start, up1, down1, up2, down2], pair_slots((0, -1, 1, -2, 2)), ())
+    up3, down3, carried = lax.optimization_barrier((up3, down3, carried))
+    last_up, last_down = turn(up3[0], 1), turn(down3[1], -1)
+    carried = project([up3, down3], pair_slots((-3, 3)), far_memory(*carried))
 
     slots = ((0, None, 0, -4), (1, None, 1, 4))
     send, fore, back, sv, gates, first, last = pl.pallas_call(
@@ -413,33 +415,37 @@
         compiler_params=params,
         name="gated",
     )(*inputs, out_weight)
-    hops = (3, -3, 2, -2, 1, -1, 0)
-    chunks = tuple((c, hop) for hop in hops for c in range(2))
-    parts = pl.pallas_call(
-        functools.partial(rest_kernel, chunks),
-        in_specs=[whole(z.shape), remote],
-        out_specs=[whole((2, rows, chans))] * len(hops),
-        out_shape=(pair,) * len(hops),
-        scratch_shapes=[
-            pltpu.VMEM((len(chunks), 2, chans, chans), bf16),
-            pltpu.SemaphoreType.DMA((len(chunks), 2)),
-        ],
-        compiler_params=params,
-        cost_estimate=pl.CostEstimate(
-            flops=len(chunks) * 6 * chans**3, transcendentals=0, bytes_accessed=len(chunks) * 6 * chans**2
-        ),
-        name="rest",
-    )(*far_memory(z), out_weight)
+
+    def rest(z, hops):
+        chunks = tuple((c, hop) for hop in hops for c in range(2))
+        return pl.pallas_call(
+            functools.partial(rest_kernel, chunks),
+            in_specs=[whole(z.shape), remote],
+            out_specs=[whole((2, rows, chans))] * len(hops),
+            out_shape=(pair,) * len(hops),
+            scratch_shapes=[
+                pltpu.VMEM((len(chunks), 2, chans, chans), bf16),
+                pltpu.SemaphoreType.DMA((len(chunks), 2)),
+            ],
+            compiler_params=params,
+            cost_estimate=pl.CostEstimate(
+                flops=len(chunks) * 6 * chans**3, transcendentals=0, bytes_accessed=len(chunks) * 6 * chans**2
+            ),
+            name="rest",
+        )(*far_memory(z), out_weight)
 
     up_sum, down_sum = turn(out_up, 1), turn(out_down, -1)
     nothing = jnp.zeros_like(up_sum, f32)
     up_sum = jnp.stack([up_sum.astype(f32), nothing])
     down_sum = jnp.stack([nothing, down_sum.astype(f32)])
-    for hop in range(3):
-        ups_now = (parts[2 * hop].astype(f32) + up_sum).astype(bf16)
-        downs_now = (parts[2 * hop + 1].astype(f32) + down_sum).astype(bf16)
+    parts = rest(z, (3, -3))
+    for hop in (2, 1, 0):
+        ups_now = (parts[0].astype(f32) + up_sum).astype(bf16)
+        downs_now = (parts[1].astype(f32) + down_sum).astype(bf16)
+        ups_now, downs_now, z = lax.optimization_barrier((ups_now, downs_now, z))
         up_sum, down_sum = turn(ups_now, 1).astype(f32), turn(downs_now, -1).astype(f32)
-    total = parts[6].astype(f32) + up_sum + down_sum
+        parts = rest(z, (hop, -hop) if hop else (0,))
+    total = parts[0].astype(f32) + up_sum + down_sum
     other = across(total[1].astype(bf16))
     return (total[0] + other.astype(f32)).astype(bf16)
 

time: 132 us -> 126 us (0.955)
  the two profiles are of different devices: /device:TPU:4 before, /device:TPU:24 now
where the time goes in v3:
time: 126 us; the launch traced here: 125 us
  Pallas kernels  45.6 us (36%)
  starting transfers between devices  42.7 us (34%)
  waiting for transfers between devices  28 us (22%)
  other arithmetic  8.67 us (7%)
    ppermute x16, starting transfers between devices, turn(): lax.ppermute(a, 'tp', [(c * ring + i, c * ring + (i + hop) % ring) for c...  28.9 us
    pallas_call x4, Pallas kernels, rest(): pl.pallas_call(functools.partial(rest_kernel, chunks), in_specs=[whole(z....  17.3 us
    ppermute x16, waiting for transfers between devices, turn(): lax.ppermute(a, 'tp', [(c * ring + i, c * ring + (i + hop) % ring) for c...  17 us
    pallas_call x2, Pallas kernels, project(): pl.pallas_call(functools.partial(early_kernel, slots, len(arrays), not ca...  11.6 us
    ppermute x2, waiting for transfers between devices, across(): return lax.ppermute(a, 'tp', [(i, (i + ring) % tp) for i in range(tp)])  8.34 us
    all_to_all x1, starting transfers between devices, body(): recv = lax.all_to_all(send, 'seq', split_axis=0, concat_axis=0)  7.19 us
    pallas_call x1, Pallas kernels, body(): pl.pallas_call(functools.partial(states_kernel, slots, 2), in_specs=[remo...  6.39 us
    pallas_call x1, Pallas kernels, body(): pl.pallas_call(functools.partial(gated_kernel, chunks), in_specs=[whole(a...  5.3 us
  transfers between devices with their start and end apart: 21, of which 10 were waited for; matrix products, arithmetic and copies ran while one was open for 2% of the time, Pallas kernels for 27%

profile of v3, /device:TPU:24, one launch (start us, length us, event | category | flops | bytes accessed | tf_op | source)
XLA Modules:
  0.0 125.3 jit_solution(17065789539448189093)
XLA Ops:
  0.0 1.5 %collective-permute-start = (bf16[256,256]{1,0:T(8,128)(2,1)}, bf16[256,256]{1,0:T(8,128)(2,1)S(1)}, u32[]{:S(2)}, u32[]{:S(2)}) collective-permute-start(bf16[256,256]{1,0:T(8,128)(2,1)} %param.9), channel_id=1, source_target_pairs={{0,8},{1,9},{2,10},{3,11},{4,12},{5,13},{6,14},{7,15},{8,0},{9,1},... | collective-permute-start | bytes 393224 | tf_op jit(solution)/shard_map/ppermute | solution.py:293
  1.5 4.0 %collective-permute-done = bf16[256,256]{1,0:T(8,128)(2,1)S(1)} collective-permute-done((bf16[256,256]{1,0:T(8,128)(2,1)}, bf16[256,256]{1,0:T(8,128)(2,1)S(1)}, u32[]{:S(2)}, u32[]{:S(2)}) %collective-permute-start) | collective-permute-done | bytes 131104 | tf_op jit(solution)/shard_map/ppermute | solution.py:293
  6.4 5.9 %collective-permute-start.2 = (bf16[2,256,256]{2,1,0:T(8,128)(2,1)S(1)}, bf16[2,256,256]{2,1,0:T(8,128)(2,1)S(1)}, u32[]{:S(2)}, u32[]{:S(2)}) collective-permute-start(bf16[2,256,256]{2,1,0:T(8,128)(2,1)S(1)} %pad_maximum_fusion.refs_0_), channel_id=1, source_target_pairs={{0,7},{1,0},{2,1},{3,2},{4,3},{5,4},{6,5},{7,6},{8,15},{9,8},{10,9... | collective-permute-start | bytes 786440 | tf_op jit(solution)/shard_map/ppermute | solution.py:288
  12.3 1.7 %tables.1 = (f32[18,16,256]{2,1,0:T(8,128)}, f32[40,256]{1,0:T(8,128)}, f32[16,16,256]{2,1,0:T(8,128)}, f32[16,16,256]{2,1,0:T(8,128)}) custom-call(f32[16,256]{1,0:T(8,128)} %rates_ref.3, f32[16,256]{1,0:T(8,128)} %residues_ref.1), custom_call_target="tpu_custom_call" | custom-call | tf_op jit(solution)/shard_map/tables/pallas_call | solution.py:296
  14.0 3.0 %collective-permute-done.2.refs_2_ = bf16[2,256,256]{2,1,0:T(8,128)(2,1)S(1)} collective-permute-done((bf16[2,256,256]{2,1,0:T(8,128)(2,1)S(1)}, bf16[2,256,256]{2,1,0:T(8,128)(2,1)S(1)}, u32[]{:S(2)}, u32[]{:S(2)}) %collective-permute-start.2) | collective-permute-done | bytes 262176 | tf_op jit(solution)/shard_map/ppermute | solution.py:288
  17.0 3.4 %collective-permute-done.1.refs_1_ = bf16[2,256,256]{2,1,0:T(8,128)(2,1)S(1)} collective-permute-done((bf16[2,256,256]{2,1,0:T(8,128)(2,1)S(1)}, bf16[2,256,256]{2,1,0:T(8,128)(2,1)S(1)}, u32[]{:S(2)}, u32[]{:S(2)}) %collective-permute-start.1) | collective-permute-done | bytes 262176 | tf_op jit(solution)/shard_map/ppermute | solution.py:288
  20.4 3.2 %collective-permute-start.5 = (bf16[2,256,256]{2,1,0:T(8,128)(2,1)S(1)}, bf16[2,256,256]{2,1,0:T(8,128)(2,1)S(1)}, u32[]{:S(2)}, u32[]{:S(2)}) collective-permute-start(bf16[2,256,256]{2,1,0:T(8,128)(2,1)S(1)} %collective-permute-done.2.refs_2_), channel_id=1, source_target_pairs={{0,7},{1,0},{2,1},{3,2},{4,3},{5,4},{6,5},{7,6},{8,15},{9,8},{10,9... | collective-permute-start | bytes 786440 | tf_op jit(solution)/shard_map/ppermute | solution.py:288
  23.7 4.3 %collective-permute-done.3.refs_3_ = bf16[2,256,256]{2,1,0:T(8,128)(2,1)S(1)} collective-permute-done((bf16[2,256,256]{2,1,0:T(8,128)(2,1)S(1)}, bf16[2,256,256]{2,1,0:T(8,128)(2,1)S(1)}, u32[]{:S(2)}, u32[]{:S(2)}) %collective-permute-start.3) | collective-permute-done | bytes 262176 | tf_op jit(solution)/shard_map/ppermute | solution.py:288
  28.0 3.2 %collective-permute-start.6 = (bf16[2,256,256]{2,1,0:T(8,128)(2,1)S(1)}, bf16[2,256,256]{2,1,0:T(8,128)(2,1)S(1)}, u32[]{:S(2)}, u32[]{:S(2)}) collective-permute-start(bf16[2,256,256]{2,1,0:T(8,128)(2,1)S(1)} %collective-permute-done.5.refs_4_), channel_id=1, source_target_pairs={{0,7},{1,0},{2,1},{3,2},{4,3},{5,4},{6,5},{7,6},{8,15},{9,8},{10,9... | collective-permute-start | bytes 786440 | tf_op jit(solution)/shard_map/ppermute | solution.py:288
  31.2 6.7 %project.2 = (f32[2,256,512]{2,1,0:T(8,128)}, f32[256,256]{1,0:T(8,128)}) custom-call(bf16[2,256,256]{2,1,0:T(8,128)(2,1)S(1)} %pad_maximum_fusion.refs_0_, bf16[2,256,256]{2,1,0:T(8,128)(2,1)S(1)} %collective-permute-done.1.refs_1_, bf16[2,256,256]{2,1,0:T(8,128)(2,1)S(1)} %collective-permute-done.2.refs_2_, ...), custom_call_target="tpu_custom_call" | custom-call | flops 1677721600 | bytes 6553600 | tf_op jit(solution)/shard_map/project/pallas_call | solution.py:312
  38.1 3.2 %collective-permute-start.8 = (bf16[256,256]{1,0:T(8,128)(2,1)S(1)}, bf16[256,256]{1,0:T(8,128)(2,1)S(1)}, u32[]{:S(2)}, u32[]{:S(2)}) collective-permute-start(bf16[256,256]{1,0:T(8,128)(2,1)S(1)} %slice_bitcast_fusion.1), channel_id=1, source_target_pairs={{0,7},{1,0},{2,1},{3,2},{4,3},{5,4},{6,5},{7,6},{8,15},{9,8},{10,9... | collective-permute-start | bytes 393224 | tf_op jit(solution)/shard_map/ppermute | solution.py:288
  41.3 5.0 %project.3 = (f32[2,256,512]{2,1,0:T(8,128)}, f32[256,256]{1,0:T(8,128)}) custom-call(bf16[2,256,256]{2,1,0:T(8,128)(2,1)S(1)} %collective-permute-done.4.refs_0_, bf16[2,256,256]{2,1,0:T(8,128)(2,1)S(1)} %collective-permute-done.6.refs_1_, f32[16,1,256]{2,1,0:T(1,128)} %bitcast.22, bf16[4096,256]{1,0:T(8,128)(2,1)} %refs_3_.3, bf16[4096,256]{1,0:T(8,128)(2,1)} %refs_4_.3, ...), custom_call_target="tpu_custom_call" | custom-call | flops 671088640 | bytes 2621440 | tf_op jit(solution)/shard_map/project/pallas_call | solution.py:312
  46.3 6.4 %states.1 = (f32[16,16,512]{2,1,0:T(8,128)}, f32[2,16,16,256]{3,2,1,0:T(8,128)}, f32[2,16,16,256]{3,2,1,0:T(8,128)}, f32[2,16,16,256]{3,2,1,0:T(8,128)}, f32[256...) custom-call(bf16[256,256]{1,0:T(8,128)(2,1)S(1)} %collective-permute-done.7.refs_0_, ...), custom_call_target="tpu_custom_call" | custom-call | tf_op jit(solution)/shard_map/states/pallas_call | solution.py:347
  52.7 7.2 %all-to-all-start = ((f32[16,16,512]{2,1,0:T(8,128)}), f32[16,16,512]{2,1,0:T(8,128)S(1)}, u32[]{:S(2)}, u32[]{:S(2)}) async-start(f32[16,16,512]{2,1,0:T(8,128)} %get-tuple-element.63), calls=%async_computation | async-start | bytes 1048576 | tf_op jit(solution)/shard_map/all_to_all | solution.py:385
  59.9 2.5 %collective-permute-start.9 = (f32[8,512]{1,0:T(8,128)}, f32[8,512]{1,0:T(8,128)S(1)}, u32[]{:S(2)}, u32[]{:S(2)}) collective-permute-start(f32[8,512]{1,0:T(8,128)} %get-tuple-element.69), channel_id=1, source_target_pairs={{16,0},{32,16},{48,32},{64,48},{80,64},{96,80},{112,96},{128,112},... | collective-permute-start | bytes 49160 | tf_op jit(solution)/shard_map/ppermute | solution.py:388
  62.4 1.9 %collective-permute-start.10 = (f32[8,512]{1,0:T(8,128)}, f32[8,512]{1,0:T(8,128)S(1)}, u32[]{:S(2)}, u32[]{:S(2)}) collective-permute-start(f32[8,512]{1,0:T(8,128)} %get-tuple-element.70), channel_id=1, source_target_pairs={{0,16},{16,32},{32,48},{48,64},{64,80},{80,96},{96,112},{112,128},... | collective-permute-start | bytes 49160 | tf_op jit(solution)/shard_map/ppermute | solution.py:387
  64.3 3.2 %near.1.local_ref = f32[2,16,16,256]{3,2,1,0:T(8,128)} custom-call(f32[2,16,16,256]{3,2,1,0:T(8,128)} %get-tuple-element.66.sv_ref, f32[40,256]{1,0:T(8,128)} %get-tuple-element.67.near_ref), custom_call_target="tpu_custom_call" | custom-call | tf_op jit(solution)/shard_map/near/pallas_call | solution.py:390
  67.8 2.4 %all-to-all-done.recv_ref = f32[16,16,512]{2,1,0:T(8,128)S(1)} async-done(((f32[16,16,512]{2,1,0:T(8,128)}), f32[16,16,512]{2,1,0:T(8,128)S(1)}, u32[]{:S(2)}, u32[]{:S(2)}) %all-to-all-start) | async-done | bytes 524320 | tf_op jit(solution)/shard_map/all_to_all | solution.py:385
  70.2 5.3 %gated.1 = (bf16[256,512]{1,0:T(8,128)(2,1)}, bf16[256,256]{1,0:T(8,128)(2,1)}, bf16[256,256]{1,0:T(8,128)(2,1)}) custom-call(f32[16,16,512]{2,1,0:T(8,128)S(1)} %all-to-all-done.recv_ref, f32[2,16,16,256]{3,2,1,0:T(8,128)} %get-tuple-element.64.fore_ref, f32[2,16,16,256]{3,2,1,0:T(8,128)} %get-tuple-element.65.back_ref, f32[2,16,16,256]{3,2,1,0:T(8,128)} %near.1.local_ref, ...), custom_call_target="tpu_custom_call" | custom-call | tf_op jit(solution)/shard_map/gated/pallas_call | solution.py:404
  75.6 3.2 %collective-permute-start.12 = (bf16[256,256]{1,0:T(8,128)(2,1)}, bf16[256,256]{1,0:T(8,128)(2,1)S(1)}, u32[]{:S(2)}, u32[]{:S(2)}) collective-permute-start(bf16[256,256]{1,0:T(8,128)(2,1)} %get-tuple-element.77), channel_id=1, source_target_pairs={{0,7},{1,0},{2,1},{3,2},{4,3},{5,4},{6,5},{7,6},{8,15},{9,8},{10,9... | collective-permute-start | bytes 393224 | tf_op jit(solution)/shard_map/ppermute | solution.py:288
  78.8 4.6 %rest.4 = (bf16[2,256,256]{2,1,0:T(8,128)(2,1)}, bf16[2,256,256]{2,1,0:T(8,128)(2,1)}) custom-call(bf16[256,512]{1,0:T(8,128)(2,1)} %get-tuple-element.88.z_ref, bf16[256,4096]{1,0:T(8,128)(2,1)} %wo_ref.9), custom_call_target="tpu_custom_call" | custom-call | flops 402653184 | bytes 1572864 | tf_op jit(solution)/shard_map/rest/pallas_call | solution.py:421
  85.5 3.2 %collective-permute-start.14 = (bf16[2,256,256]{2,1,0:T(8,128)(2,1)S(1)}, bf16[2,256,256]{2,1,0:T(8,128)(2,1)S(1)}, u32[]{:S(2)}, u32[]{:S(2)}) collective-permute-start(bf16[2,256,256]{2,1,0:T(8,128)(2,1)S(1)} %add_convert_fusion.4), channel_id=1, source_target_pairs={{0,7},{1,0},{2,1},{3,2},{4,3},{5,4},{6,5},{7,6},{8,15},{9,8},{10,9... | collective-permute-start | bytes 786440 | tf_op jit(solution)/shard_map/ppermute | solution.py:288
  88.7 4.6 %rest.5 = (bf16[2,256,256]{2,1,0:T(8,128)(2,1)}, bf16[2,256,256]{2,1,0:T(8,128)(2,1)}) custom-call(bf16[256,512]{1,0:T(8,128)(2,1)} %get-tuple-element.88.z_ref, bf16[256,4096]{1,0:T(8,128)(2,1)} %wo_ref.9), custom_call_target="tpu_custom_call" | custom-call | flops 402653184 | bytes 1572864 | tf_op jit(solution)/shard_map/rest/pallas_call | solution.py:421
  93.3 1.9 %collective-permute-done.13 = bf16[2,256,256]{2,1,0:T(8,128)(2,1)S(1)} collective-permute-done((bf16[2,256,256]{2,1,0:T(8,128)(2,1)S(1)}, bf16[2,256,256]{2,1,0:T(8,128)(2,1)S(1)}, u32[]{:S(2)}, u32[]{:S(2)}) %collective-permute-start.13) | collective-permute-done | bytes 262176 | tf_op jit(solution)/shard_map/ppermute | solution.py:288
  97.3 3.2 %collective-permute-start.16 = (bf16[2,256,256]{2,1,0:T(8,128)(2,1)S(1)}, bf16[2,256,256]{2,1,0:T(8,128)(2,1)S(1)}, u32[]{:S(2)}, u32[]{:S(2)}) collective-permute-start(bf16[2,256,256]{2,1,0:T(8,128)(2,1)S(1)} %add_convert_fusion.2), channel_id=1, source_target_pairs={{0,7},{1,0},{2,1},{3,2},{4,3},{5,4},{6,5},{7,6},{8,15},{9,8},{10,9... | collective-permute-start | bytes 786440 | tf_op jit(solution)/shard_map/ppermute | solution.py:288
  100.5 4.6 %rest.6 = (bf16[2,256,256]{2,1,0:T(8,128)(2,1)}, bf16[2,256,256]{2,1,0:T(8,128)(2,1)}) custom-call(bf16[256,512]{1,0:T(8,128)(2,1)} %get-tuple-element.88.z_ref, bf16[256,4096]{1,0:T(8,128)(2,1)} %wo_ref.9), custom_call_target="tpu_custom_call" | custom-call | flops 402653184 | bytes 1572864 | tf_op jit(solution)/shard_map/rest/pallas_call | solution.py:421
  105.1 2.1 %collective-permute-done.15 = bf16[2,256,256]{2,1,0:T(8,128)(2,1)S(1)} collective-permute-done((bf16[2,256,256]{2,1,0:T(8,128)(2,1)S(1)}, bf16[2,256,256]{2,1,0:T(8,128)(2,1)S(1)}, u32[]{:S(2)}, u32[]{:S(2)}) %collective-permute-start.15) | collective-permute-done | bytes 262176 | tf_op jit(solution)/shard_map/ppermute | solution.py:288
  109.3 3.2 %collective-permute-start.18 = (bf16[2,256,256]{2,1,0:T(8,128)(2,1)S(1)}, bf16[2,256,256]{2,1,0:T(8,128)(2,1)S(1)}, u32[]{:S(2)}, u32[]{:S(2)}) collective-permute-start(bf16[2,256,256]{2,1,0:T(8,128)(2,1)S(1)} %add_convert_fusion), channel_id=1, source_target_pairs={{0,7},{1,0},{2,1},{3,2},{4,3},{5,4},{6,5},{7,6},{8,15},{9,8},{10,9... | collective-permute-start | bytes 786440 | tf_op jit(solution)/shard_map/ppermute | solution.py:288
  112.6 3.6 %rest.7 = bf16[2,256,256]{2,1,0:T(8,128)(2,1)} custom-call(bf16[256,512]{1,0:T(8,128)(2,1)} %get-tuple-element.88.z_ref, bf16[256,4096]{1,0:T(8,128)(2,1)} %wo_ref.9), custom_call_target="tpu_custom_call" | custom-call | flops 201326592 | bytes 786432 | tf_op jit(solution)/shard_map/rest/pallas_call | solution.py:421
  116.2 2.3 %collective-permute-done.17 = bf16[2,256,256]{2,1,0:T(8,128)(2,1)S(1)} collective-permute-done((bf16[2,256,256]{2,1,0:T(8,128)(2,1)S(1)}, bf16[2,256,256]{2,1,0:T(8,128)(2,1)S(1)}, u32[]{:S(2)}, u32[]{:S(2)}) %collective-permute-start.17) | collective-permute-done | bytes 262176 | tf_op jit(solution)/shard_map/ppermute | solution.py:288
  118.5 1.0 convert_add_fusion
  120.2 4.4 %collective-permute-done.19 = bf16[256,256]{1,0:T(8,128)(2,1)S(1)} collective-permute-done((bf16[256,256]{1,0:T(8,128)(2,1)S(1)}, bf16[256,256]{1,0:T(8,128)(2,1)S(1)}, u32[]{:S(2)}, u32[]{:S(2)}) %collective-permute-start.19) | collective-permute-done | bytes 131104 | tf_op jit(solution)/shard_map/ppermute | solution.py:293
  (32 shorter events, 9.1 us)
Async XLA Ops:
  0.0 5.4 %collective-permute-start = (bf16[256,256]{1,0:T(8,128)(2,1)}, bf16[256,256]{1,0:T(8,128)(2,1)S(1)}, u32[]{:S(2)}, u32[]{:S(2)}) collective-permute-start(bf16[256,256]{1,0:T(8,128)(2,1)} %param.9), channel_id=1, source_target_pairs={{0,8},{1,9},{2,10},{3,11},{4,12},{5,13},{6,14},{7,15},{8,0},{9,1},... | collective-permute-start | bytes 393224 | tf_op jit(solution)/shard_map/ppermute | solution.py:293
  6.4 10.6 %collective-permute-start.2 = (bf16[2,256,256]{2,1,0:T(8,128)(2,1)S(1)}, bf16[2,256,256]{2,1,0:T(8,128)(2,1)S(1)}, u32[]{:S(2)}, u32[]{:S(2)}) collective-permute-start(bf16[2,256,256]{2,1,0:T(8,128)(2,1)S(1)} %pad_maximum_fusion.refs_0_), channel_id=1, source_target_pairs={{0,7},{1,0},{2,1},{3,2},{4,3},{5,4},{6,5},{7,6},{8,15},{9,8},{10,9... | collective-permute-start | bytes 786440 | tf_op jit(solution)/shard_map/ppermute | solution.py:288
  12.3 8.1 %collective-permute-start.1 = (bf16[2,256,256]{2,1,0:T(8,128)(2,1)S(1)}, bf16[2,256,256]{2,1,0:T(8,128)(2,1)S(1)}, u32[]{:S(2)}, u32[]{:S(2)}) collective-permute-start(bf16[2,256,256]{2,1,0:T(8,128)(2,1)S(1)} %pad_maximum_fusion.refs_0_), channel_id=1, source_target_pairs={{0,1},{1,2},{2,3},{3,4},{4,5},{5,6},{6,7},{7,0},{8,9},{9,10},{10,1... | collective-permute-start | bytes 786440 | tf_op jit(solution)/shard_map/ppermute | solution.py:288
  20.4 7.6 %collective-permute-start.3 = (bf16[2,256,256]{2,1,0:T(8,128)(2,1)S(1)}, bf16[2,256,256]{2,1,0:T(8,128)(2,1)S(1)}, u32[]{:S(2)}, u32[]{:S(2)}) collective-permute-start(bf16[2,256,256]{2,1,0:T(8,128)(2,1)S(1)} %collective-permute-done.1.refs_1_), channel_id=1, source_target_pairs={{0,1},{1,2},{2,3},{3,4},{4,5},{5,6},{6,7},{7,0},{8,9},{9,10},{10,1... | collective-permute-start | bytes 786440 | tf_op jit(solution)/shard_map/ppermute | solution.py:288
  20.4 7.6 %collective-permute-start.5 = (bf16[2,256,256]{2,1,0:T(8,128)(2,1)S(1)}, bf16[2,256,256]{2,1,0:T(8,128)(2,1)S(1)}, u32[]{:S(2)}, u32[]{:S(2)}) collective-permute-start(bf16[2,256,256]{2,1,0:T(8,128)(2,1)S(1)} %collective-permute-done.2.refs_2_), channel_id=1, source_target_pairs={{0,7},{1,0},{2,1},{3,2},{4,3},{5,4},{6,5},{7,6},{8,15},{9,8},{10,9... | collective-permute-start | bytes 786440 | tf_op jit(solution)/shard_map/ppermute | solution.py:288
  28.0 9.9 %collective-permute-start.4 = (bf16[2,256,256]{2,1,0:T(8,128)(2,1)S(1)}, bf16[2,256,256]{2,1,0:T(8,128)(2,1)S(1)}, u32[]{:S(2)}, u32[]{:S(2)}) collective-permute-start(bf16[2,256,256]{2,1,0:T(8,128)(2,1)S(1)} %collective-permute-done.3.refs_3_), channel_id=1, source_target_pairs={{0,1},{1,2},{2,3},{3,4},{4,5},{5,6},{6,7},{7,0},{8,9},{9,10},{10,1... | collective-permute-start | bytes 786440 | tf_op jit(solution)/shard_map/ppermute | solution.py:288
  28.0 9.9 %collective-permute-start.6 = (bf16[2,256,256]{2,1,0:T(8,128)(2,1)S(1)}, bf16[2,256,256]{2,1,0:T(8,128)(2,1)S(1)}, u32[]{:S(2)}, u32[]{:S(2)}) collective-permute-start(bf16[2,256,256]{2,1,0:T(8,128)(2,1)S(1)} %collective-permute-done.5.refs_4_), channel_id=1, source_target_pairs={{0,7},{1,0},{2,1},{3,2},{4,3},{5,4},{6,5},{7,6},{8,15},{9,8},{10,9... | collective-permute-start | bytes 786440 | tf_op jit(solution)/shard_map/ppermute | solution.py:288
  38.0 8.3 %collective-permute-start.7 = (bf16[256,256]{1,0:T(8,128)(2,1)S(1)}, bf16[256,256]{1,0:T(8,128)(2,1)S(1)}, u32[]{:S(2)}, u32[]{:S(2)}) collective-permute-start(bf16[256,256]{1,0:T(8,128)(2,1)S(1)} %slice_bitcast_fusion.2), channel_id=1, source_target_pairs={{0,1},{1,2},{2,3},{3,4},{4,5},{5,6},{6,7},{7,0},{8,9},{9,10},{10,1... | collective-permute-start | bytes 393224 | tf_op jit(solution)/shard_map/ppermute | solution.py:288
  38.1 8.2 %collective-permute-start.8 = (bf16[256,256]{1,0:T(8,128)(2,1)S(1)}, bf16[256,256]{1,0:T(8,128)(2,1)S(1)}, u32[]{:S(2)}, u32[]{:S(2)}) collective-permute-start(bf16[256,256]{1,0:T(8,128)(2,1)S(1)} %slice_bitcast_fusion.1), channel_id=1, source_target_pairs={{0,7},{1,0},{2,1},{3,2},{4,3},{5,4},{6,5},{7,6},{8,15},{9,8},{10,9... | collective-permute-start | bytes 393224 | tf_op jit(solution)/shard_map/ppermute | solution.py:288
  52.7 17.5 %all-to-all-start = ((f32[16,16,512]{2,1,0:T(8,128)}), f32[16,16,512]{2,1,0:T(8,128)S(1)}, u32[]{:S(2)}, u32[]{:S(2)}) async-start(f32[16,16,512]{2,1,0:T(8,128)} %get-tuple-element.63), calls=%async_computation | async-start | bytes 1048576 | tf_op jit(solution)/shard_map/all_to_all | solution.py:385
  59.9 7.6 %collective-permute-start.9 = (f32[8,512]{1,0:T(8,128)}, f32[8,512]{1,0:T(8,128)S(1)}, u32[]{:S(2)}, u32[]{:S(2)}) collective-permute-start(f32[8,512]{1,0:T(8,128)} %get-tuple-element.69), channel_id=1, source_target_pairs={{16,0},{32,16},{48,32},{64,48},{80,64},{96,80},{112,96},{128,112},... | collective-permute-start | bytes 49160 | tf_op jit(solution)/shard_map/ppermute | solution.py:388
  62.4 5.4 %collective-permute-start.10 = (f32[8,512]{1,0:T(8,128)}, f32[8,512]{1,0:T(8,128)S(1)}, u32[]{:S(2)}, u32[]{:S(2)}) collective-permute-start(f32[8,512]{1,0:T(8,128)} %get-tuple-element.70), channel_id=1, source_target_pairs={{0,16},{16,32},{32,48},{48,64},{64,80},{80,96},{96,112},{112,128},... | collective-permute-start | bytes 49160 | tf_op jit(solution)/shard_map/ppermute | solution.py:387
  75.5 7.9 %collective-permute-start.11 = (bf16[256,256]{1,0:T(8,128)(2,1)}, bf16[256,256]{1,0:T(8,128)(2,1)S(1)}, u32[]{:S(2)}, u32[]{:S(2)}) collective-permute-start(bf16[256,256]{1,0:T(8,128)(2,1)} %get-tuple-element.75), channel_id=1, source_target_pairs={{0,1},{1,2},{2,3},{3,4},{4,5},{5,6},{6,7},{7,0},{8,9},{9,10},{10,1... | collective-permute-start | bytes 393224 | tf_op jit(solution)/shard_map/ppermute | solution.py:288
  75.6 8.8 %collective-permute-start.12 = (bf16[256,256]{1,0:T(8,128)(2,1)}, bf16[256,256]{1,0:T(8,128)(2,1)S(1)}, u32[]{:S(2)}, u32[]{:S(2)}) collective-permute-start(bf16[256,256]{1,0:T(8,128)(2,1)} %get-tuple-element.77), channel_id=1, source_target_pairs={{0,7},{1,0},{2,1},{3,2},{4,3},{5,4},{6,5},{7,6},{8,15},{9,8},{10,9... | collective-permute-start | bytes 393224 | tf_op jit(solution)/shard_map/ppermute | solution.py:288
  85.4 9.8 %collective-permute-start.13 = (bf16[2,256,256]{2,1,0:T(8,128)(2,1)S(1)}, bf16[2,256,256]{2,1,0:T(8,128)(2,1)S(1)}, u32[]{:S(2)}, u32[]{:S(2)}) collective-permute-start(bf16[2,256,256]{2,1,0:T(8,128)(2,1)S(1)} %add_convert_fusion.5), channel_id=1, source_target_pairs={{0,1},{1,2},{2,3},{3,4},{4,5},{5,6},{6,7},{7,0},{8,9},{9,10},{10,1... | collective-permute-start | bytes 786440 | tf_op jit(solution)/shard_map/ppermute | solution.py:288
  85.5 10.7 %collective-permute-start.14 = (bf16[2,256,256]{2,1,0:T(8,128)(2,1)S(1)}, bf16[2,256,256]{2,1,0:T(8,128)(2,1)S(1)}, u32[]{:S(2)}, u32[]{:S(2)}) collective-permute-start(bf16[2,256,256]{2,1,0:T(8,128)(2,1)S(1)} %add_convert_fusion.4), channel_id=1, source_target_pairs={{0,7},{1,0},{2,1},{3,2},{4,3},{5,4},{6,5},{7,6},{8,15},{9,8},{10,9... | collective-permute-start | bytes 786440 | tf_op jit(solution)/shard_map/ppermute | solution.py:288
  97.2 10.0 %collective-permute-start.15 = (bf16[2,256,256]{2,1,0:T(8,128)(2,1)S(1)}, bf16[2,256,256]{2,1,0:T(8,128)(2,1)S(1)}, u32[]{:S(2)}, u32[]{:S(2)}) collective-permute-start(bf16[2,256,256]{2,1,0:T(8,128)(2,1)S(1)} %add_convert_fusion.3), channel_id=1, source_target_pairs={{0,1},{1,2},{2,3},{3,4},{4,5},{5,6},{6,7},{7,0},{8,9},{9,10},{10,1... | collective-permute-start | bytes 786440 | tf_op jit(solution)/shard_map/ppermute | solution.py:288
  97.3 10.9 %collective-permute-start.16 = (bf16[2,256,256]{2,1,0:T(8,128)(2,1)S(1)}, bf16[2,256,256]{2,1,0:T(8,128)(2,1)S(1)}, u32[]{:S(2)}, u32[]{:S(2)}) collective-permute-start(bf16[2,256,256]{2,1,0:T(8,128)(2,1)S(1)} %add_convert_fusion.2), channel_id=1, source_target_pairs={{0,7},{1,0},{2,1},{3,2},{4,3},{5,4},{6,5},{7,6},{8,15},{9,8},{10,9... | collective-permute-start | bytes 786440 | tf_op jit(solution)/shard_map/ppermute | solution.py:288
  109.2 9.2 %collective-permute-start.17 = (bf16[2,256,256]{2,1,0:T(8,128)(2,1)S(1)}, bf16[2,256,256]{2,1,0:T(8,128)(2,1)S(1)}, u32[]{:S(2)}, u32[]{:S(2)}) collective-permute-start(bf16[2,256,256]{2,1,0:T(8,128)(2,1)S(1)} %add_convert_fusion.1), channel_id=1, source_target_pairs={{0,1},{1,2},{2,3},{3,4},{4,5},{5,6},{6,7},{7,0},{8,9},{9,10},{10,1... | collective-permute-start | bytes 786440 | tf_op jit(solution)/shard_map/ppermute | solution.py:288
  109.3 9.1 %collective-permute-start.18 = (bf16[2,256,256]{2,1,0:T(8,128)(2,1)S(1)}, bf16[2,256,256]{2,1,0:T(8,128)(2,1)S(1)}, u32[]{:S(2)}, u32[]{:S(2)}) collective-permute-start(bf16[2,256,256]{2,1,0:T(8,128)(2,1)S(1)} %add_convert_fusion), channel_id=1, source_target_pairs={{0,7},{1,0},{2,1},{3,2},{4,3},{5,4},{6,5},{7,6},{8,15},{9,8},{10,9... | collective-permute-start | bytes 786440 | tf_op jit(solution)/shard_map/ppermute | solution.py:288
  119.5 5.1 %collective-permute-start.19 = (bf16[256,256]{1,0:T(8,128)(2,1)S(1)}, bf16[256,256]{1,0:T(8,128)(2,1)S(1)}, u32[]{:S(2)}, u32[]{:S(2)}) collective-permute-start(bf16[256,256]{1,0:T(8,128)(2,1)S(1)} %fusion.2), channel_id=1, source_target_pairs={{0,8},{1,9},{2,10},{3,11},{4,12},{5,13},{6,14},{7,15},{8,0},{9,1},... | collective-permute-start | bytes 393224 | tf_op jit(solution)/shard_map/ppermute | solution.py:293

commit v4 on v3

--- a/solution.py
+++ b/solution.py
@@ -50,10 +50,11 @@
     return pl.ds(pl.multiple_of(block * size, size), size)
 
 
-def accumulate(slots, x_refs, gain_ref, weights, x_buf, w_buf, sems, acc_ref, sq_ref, fresh):
+def accumulate(slots, x_refs, gain_ref, weights, x_buf, w_buf, sems, acc_ref, sq_ref, carried=(), sinks=()):
     tp = lax.axis_size("tp")
     place = lax.axis_index("tp")
     rows, chans = x_buf.shape[1:]
+    last = len(slots)
     copies = []
     for n, (array, entry, column, hop) in enumerate(slots):
         block = shard_at(place, column, hop, tp)
@@ -72,50 +73,71 @@
         for copy in group:
             copy.start()
         copies.append(group)
+        if n == 0 and carried:
+            acc_in, sq_in = carried
+            before = [
+                pltpu.make_async_copy(acc_in.at[0], acc_ref.at[0], sems.at[last, 0]),
+                pltpu.make_async_copy(acc_in.at[1], acc_ref.at[1], sems.at[last, 1]),
+                pltpu.make_async_copy(sq_in, sq_ref, sems.at[last, 2]),
+            ]
+            for copy in before:
+                copy.start()
     flip = reversal(chans)
-    wide = w_buf.shape[3]
+    after = []
+
+    def leave(index, source, sink, ready):
+        if sinks and ready:
+            copy = pltpu.make_async_copy(source, sink, sems.at[last + 1, index])
+            copy.start()
+            after.append(copy)
+
     for n, (array, entry, column, hop) in enumerate(slots):
         block = shard_at(place, column, hop, tp)
         for copy in copies[n]:
             copy.wait()
         x = x_buf[n]
         part = x.astype(f32)
+        square = part * part
+        square = sum(square[:, i : i + 128] for i in range(0, chans, 128))
         mirrored = jnp.dot(x, flip, preferred_element_type=f32)
         own = (part * gain_ref[block]).astype(bf16)
         far = (mirrored * gain_ref[tp - 1 - block]).astype(bf16)
         first = jnp.dot(own, w_buf[n, 0], preferred_element_type=f32)
+        if n == 0 and carried:
+            for copy in before:
+                copy.wait()
+        fresh = n == 0 and not carried
+        done = n == last - 1
+        acc_ref[0] = first if fresh else acc_ref[0] + first
+        sq_ref[...] = square if fresh else sq_ref[...] + square
+        if sinks:
+            leave(0, acc_ref.at[0], sinks[0].at[0], done)
+            leave(2, sq_ref, sinks[1], done)
         second = jnp.dot(far, w_buf[n, 1], preferred_element_type=f32)
-        if fresh and n == 0:
-            sq_ref[...] = part * part
-            acc_ref[0] = first
-            acc_ref[1] = second
-        else:
-            sq_ref[...] += part * part
-            acc_ref[0] += first
-            acc_ref[1] += second
-
-
-def early_kernel(slots, arrays, fresh, *refs):
+        acc_ref[1] = second if fresh else acc_ref[1] + second
+        if sinks:
+            leave(1, acc_ref.at[1], sinks[0].at[1], done)
+    for copy in after:
+        copy.wait()
+
+
+def early_kernel(slots, arrays, more, *refs):
     x_refs, refs = refs[:arrays], refs[arrays:]
     gain_ref, wv_ref, wg_ref, refs = refs[0], refs[1], refs[2], refs[3:]
-    if not fresh:
-        acc_in, sq_in, refs = refs[0], refs[1], refs[2:]
+    carried, sinks, refs = refs[:more], refs[more : more + 2], refs[more + 2 :]
     acc_ref, sq_ref, x_buf, w_buf, sems = refs
-    if not fresh:
-        acc_ref[...] = acc_in[...]
-        sq_ref[...] = sq_in[...]
-    accumulate(slots, x_refs, gain_ref, (wv_ref, wg_ref), x_buf, w_buf, sems, acc_ref, sq_ref, fresh)
+    accumulate(slots, x_refs, gain_ref, (wv_ref, wg_ref), x_buf, w_buf, sems, acc_ref, sq_ref, carried, sinks)
 
 
 def states_kernel(slots, arrays, *refs):
     x_refs, refs = refs[:arrays], refs[arrays:]
     gain_ref, wv_ref, wg_ref, acc_in, sq_in, vt_ref, pow_ref, refs = *refs[:7], refs[7:]
-    send_ref, fore_ref, back_ref, sv_ref, gates_ref, first_ref, last_ref, refs = *refs[:7], refs[7:]
+    send_ref, sv_ref, gates_ref, edge_ref, refs = *refs[:4], refs[4:]
     acc_ref, sq_ref, pad_ref, x_buf, w_buf, sems = refs
-    acc_ref[...] = acc_in[...]
-    sq_ref[...] = sq_in[...]
-    accumulate(slots, x_refs, gain_ref, (wv_ref, wg_ref), x_buf, w_buf, sems, acc_ref, sq_ref, False)
-    rows, chans = sq_ref.shape
+    accumulate(
+        slots, x_refs, gain_ref, (wv_ref, wg_ref), x_buf, w_buf, sems, acc_ref, sq_ref, (acc_in, sq_in)
+    )
+    rows, chans = x_buf.shape[1:]
     place = lax.axis_index("seq")
     places = lax.axis_size("seq")
     mean = jnp.sum(sq_ref[...], axis=1, keepdims=True) * (1.0 / (lax.axis_size("tp") * chans))
@@ -128,8 +150,12 @@
         strand = slice(s * chans, (s + 1) * chans)
         gates = acc_ref[s, :, chans:] * scale
         gates_ref[:, strand] = gates
-        first_ref[:, strand] = gates[0:8, :]
-        last_ref[:, strand] = gates[rows - 8 : rows, :]
+        for g in range(chans // 128):
+            row = s * (chans // 128) + g
+            first = gates[0:1, g * 128 : (g + 1) * 128]
+            last = gates[rows - 1 : rows, g * 128 : (g + 1) * 128]
+            for i in range(places):
+                send_ref[i, row : row + 1, 2 * chans :] = jnp.where(i > place, last, first)
         v = acc_ref[s, :, :chans] * scale
         pad_ref[0:8, :] = zeros8
         pad_ref[8 : 8 + rows, :] = v
@@ -140,6 +166,8 @@
         sv_ref[s] = sv.reshape(tiles, T, chans)
         all_low = tc * v[0:1, :] * low_ok
         all_high = ta * v[rows - 1 : rows, :] * high_ok
+        edge_ref[s, 0] = jnp.broadcast_to(all_low, (8, chans))
+        edge_ref[s, 1] = jnp.broadcast_to(all_high, (8, chans))
         for g in range(chans // 128):
             lanes = slice(g * 128, (g + 1) * 128)
             low, high = all_low[:, lanes], all_high[:, lanes]
@@ -150,7 +178,6 @@
                 fold = fold + pow_ref[T - 1 - j, :, lanes][None] * sv_ref[s, :, j : j + 1, lanes]
             state = jnp.broadcast_to(low, (16, 128))
             for n in range(tiles):
-                fore_ref[s, n, :, lanes] = state
                 state = jump * state + fold[n]
             ahead = state + inverse * high
             fold = jnp.zeros((tiles, 16, 128), f32)
@@ -158,7 +185,6 @@
                 fold = fold + pow_ref[j, :, lanes][None] * sv_ref[s, :, j : j + 1, lanes]
             state = jnp.broadcast_to(high, (16, 128))
             for n in reversed(range(tiles)):
-                back_ref[s, n, :, lanes] = state
                 state = jump * state + fold[n]
             behind = state + inverse * low
             wide = slice(s * chans + g * 128, s * chans + (g + 1) * 128)
@@ -166,16 +192,39 @@
                 send_ref[i, :, wide] = jnp.where(i > place, ahead, behind)
 
 
-def near_kernel(sv_ref, near_ref, local_ref):
+def spread(conv, spread_f_ref, spread_b_ref, st_ref, lanes):
+    for m in range(16):
+        conv = conv + spread_f_ref[m, :, lanes][None] * st_ref[0, :, m : m + 1, :]
+    for m in range(16):
+        conv = conv + spread_b_ref[m, :, lanes][None] * st_ref[1, :, m : m + 1, :]
+    return conv
+
+
+def local_kernel(sv_ref, edge_ref, pow_ref, near_ref, spread_f_ref, spread_b_ref, local_ref, st_ref):
     tiles = sv_ref.shape[1]
     chans = sv_ref.shape[3]
     for s in range(2):
         for g in range(chans // 128):
             lanes = slice(g * 128, (g + 1) * 128)
-            inner = jnp.zeros((tiles, T, 128), f32)
+            jump = pow_ref[T, :, lanes]
+            fold = jnp.zeros((tiles, 16, 128), f32)
             for j in range(T):
-                inner = inner + near_ref[T - j : 2 * T - j, lanes][None] * sv_ref[s, :, j : j + 1, lanes]
-            local_ref[s, :, :, lanes] = inner
+                fold = fold + pow_ref[T - 1 - j, :, lanes][None] * sv_ref[s, :, j : j + 1, lanes]
+            state = jnp.broadcast_to(edge_ref[s, 0, 0:1, lanes], (16, 128))
+            for n in range(tiles):
+                st_ref[0, n] = state
+                state = jump * state + fold[n]
+            fold = jnp.zeros((tiles, 16, 128), f32)
+            for j in range(T):
+                fold = fold + pow_ref[j, :, lanes][None] * sv_ref[s, :, j : j + 1, lanes]
+            state = jnp.broadcast_to(edge_ref[s, 1, 0:1, lanes], (16, 128))
+            for n in reversed(range(tiles)):
+                st_ref[1, n] = state
+                state = jump * state + fold[n]
+            conv = jnp.zeros((tiles, T, 128), f32)
+            for j in range(T):
+                conv = conv + near_ref[T - j : 2 * T - j, lanes][None] * sv_ref[s, :, j : j + 1, lanes]
+            local_ref[s, :, :, lanes] = spread(conv, spread_f_ref, spread_b_ref, st_ref, lanes)
 
 
 def fetch_columns(chunks, wo_ref, w_buf, sems):
@@ -205,7 +254,7 @@
 
 
 def gated_kernel(
-    chunks, recv_ref, fore_ref, back_ref, local_ref, gates_ref, above_ref, below_ref, gt_ref, rates_ref,
+    chunks, recv_ref, local_ref, gates_ref, gt_ref, rates_ref,
     spread_f_ref, spread_b_ref, wo_ref, z_ref, *refs,
 ):
     outs, (pad_ref, st_ref, w_buf, sems) = refs[: len(chunks)], refs[len(chunks) :]
@@ -214,13 +263,20 @@
     tiles = rows // T
     place = lax.axis_index("seq")
     places = lax.axis_size("seq")
+    low_ok = (place > 0).astype(f32)
+    high_ok = (place < places - 1).astype(f32)
+    below = jnp.maximum(place - 1, 0)
+    above = jnp.minimum(place + 1, places - 1)
     copies = fetch_columns(chunks, wo_ref, w_buf, sems)
     for s in range(2):
         wide = slice(s * chans, (s + 1) * chans)
         g = gates_ref[:, wide]
-        pad_ref[0:8, :] = below_ref[:, wide]
         pad_ref[8 : 8 + rows, :] = g
-        pad_ref[8 + rows : 16 + rows, :] = above_ref[:, wide]
+        for g2 in range(chans // 128):
+            row = s * (chans // 128) + g2
+            lanes = slice(g2 * 128, (g2 + 1) * 128)
+            pad_ref[7:8, lanes] = recv_ref[below, row : row + 1, 2 * chans :] * low_ok
+            pad_ref[8 + rows : 9 + rows, lanes] = recv_ref[above, row : row + 1, 2 * chans :] * high_ok
         a, c = (0, 2) if s == 0 else (2, 0)
         ta, tb, tc = gt_ref[a : a + 1, :], gt_ref[1:2, :], gt_ref[c : c + 1, :]
         sg = ta * pad_ref[7 : 7 + rows, :] + tb * g + tc * pad_ref[9 : 9 + rows, :]
@@ -238,15 +294,11 @@
                 carry_b = jnp.where(r > place, carry_b * hop + recv_ref[r, :, wide], carry_b)
             for n in range(tiles):
                 m = tiles - 1 - n
-                st_ref[0, n] = fore_ref[s, n, :, lanes] + carry_f
-                st_ref[1, m] = back_ref[s, m, :, lanes] + carry_b
+                st_ref[0, n] = carry_f
+                st_ref[1, m] = carry_b
                 carry_f = carry_f * jump
                 carry_b = carry_b * jump
-            conv = local_ref[s, :, :, lanes]
-            for m in range(16):
-                conv = conv + spread_f_ref[m, :, lanes][None] * st_ref[0, :, m : m + 1, :]
-            for m in range(16):
-                conv = conv + spread_b_ref[m, :, lanes][None] * st_ref[1, :, m : m + 1, :]
+            conv = spread(local_ref[s, :, :, lanes], spread_f_ref, spread_b_ref, st_ref, lanes)
             z_ref[:, wide] = (sg[:, lanes] * conv.reshape(rows, 128)).astype(bf16)
     flip = reversal(chans)
     for n, ref in enumerate(outs):
@@ -310,16 +362,16 @@
 
     def project(arrays, slots, carried):
         return pl.pallas_call(
-            functools.partial(early_kernel, slots, len(arrays), not carried),
-            in_specs=[remote] * len(arrays)
-            + [whole(gain.shape), remote, remote]
-            + [whole(a.shape) for a in carried],
-            out_specs=[whole((2, rows, 2 * chans)), whole((rows, chans))],
-            out_shape=(shape((2, rows, 2 * chans), f32), shape((rows, chans), f32)),
+            functools.partial(early_kernel, slots, len(arrays), len(carried)),
+            in_specs=[remote] * len(arrays) + [whole(gain.shape), remote, remote] + [remote] * len(carried),
+            out_specs=[remote, remote],
+            out_shape=(shape((2, rows, 2 * chans), f32), shape((rows, 128), f32)),
             scratch_shapes=[
+                pltpu.VMEM((2, rows, 2 * chans), f32),
+                pltpu.VMEM((rows, 128), f32),
                 pltpu.VMEM((len(slots), rows, chans), bf16),
                 pltpu.VMEM((len(slots), 2, chans, 2 * chans), bf16),
-                pltpu.SemaphoreType.DMA((len(slots), 5)),
+                pltpu.SemaphoreType.DMA((len(slots) + 2, 5)),
             ],
             compiler_params=params,
             cost_estimate=pl.CostEstimate(
@@ -333,47 +385,40 @@
 
     start = jnp.stack([hidden, across(hidden)])
     up1, down1 = turn(start, 1), turn(start, -1)
-    up1, down1, powers, near, spread_f, spread_b = lax.optimization_barrier(
-        (up1, down1, powers, near, spread_f, spread_b)
-    )
+    up1, powers, near, spread_f, spread_b = lax.optimization_barrier((up1, powers, near, spread_f, spread_b))
     up2, down2 = turn(up1, 1), turn(down1, -1)
+    carried = project([start, up1, down1], pair_slots((0, -1, 1)), ())
+    up2, carried = lax.optimization_barrier((up2, carried))
     up3, down3 = turn(up2, 1), turn(down2, -1)
-    carried = project([start, up1, down1, up2, down2], pair_slots((0, -1, 1, -2, 2)), ())
-    up3, down3, carried = lax.optimization_barrier((up3, down3, carried))
+    carried = project([up2, down2], pair_slots((-2, 2)), far_memory(*carried))
+    up3, carried = lax.optimization_barrier((up3, carried))
     last_up, last_down = turn(up3[0], 1), turn(down3[1], -1)
     carried = project([up3, down3], pair_slots((-3, 3)), far_memory(*carried))
 
     slots = ((0, None, 0, -4), (1, None, 1, 4))
-    send, fore, back, sv, gates, first, last = pl.pallas_call(
+    send, sv, gates, edge = pl.pallas_call(
         functools.partial(states_kernel, slots, 2),
-        in_specs=[remote, remote, whole(gain.shape), remote, remote]
-        + [whole(a.shape) for a in carried]
+        in_specs=[remote, remote, whole(gain.shape), remote, remote, remote, remote]
         + [whole(value_taps.shape), whole(powers.shape)],
         out_specs=[
-            whole((places, modes, 2 * chans)),
-            whole((2, tiles, modes, chans)),
-            whole((2, tiles, modes, chans)),
+            whole((places, modes, 2 * chans + 128)),
             whole((2, tiles, T, chans)),
             whole((rows, 2 * chans)),
-            whole((8, 2 * chans)),
-            whole((8, 2 * chans)),
+            whole((2, 2, 8, chans)),
         ],
         out_shape=(
-            shape((places, modes, 2 * chans), f32),
-            shape((2, tiles, modes, chans), f32),
-            shape((2, tiles, modes, chans), f32),
+            shape((places, modes, 2 * chans + 128), f32),
             shape((2, tiles, T, chans), f32),
             shape((rows, 2 * chans), f32),
-            shape((8, 2 * chans), f32),
-            shape((8, 2 * chans), f32),
+            shape((2, 2, 8, chans), f32),
         ),
         scratch_shapes=[
             pltpu.VMEM((2, rows, 2 * chans), f32),
-            pltpu.VMEM((rows, chans), f32),
+            pltpu.VMEM((rows, 128), f32),
             pltpu.VMEM((rows + 16, chans), f32),
             pltpu.VMEM((2, rows, chans), bf16),
             pltpu.VMEM((2, 2, chans, 2 * chans), bf16),
-            pltpu.SemaphoreType.DMA((2, 5)),
+            pltpu.SemaphoreType.DMA((4, 5)),
         ],
         compiler_params=params,
         name="states",
@@ -383,22 +428,19 @@
     )
 
     recv = lax.all_to_all(send, "seq", split_axis=0, concat_axis=0)
-    up = [(i, i + 1) for i in range(places - 1)]
-    below = lax.ppermute(last, "seq", up)
-    above = lax.ppermute(first, "seq", [(b, a) for a, b in up])
-
     local = pl.pallas_call(
-        near_kernel,
+        local_kernel,
         out_shape=shape((2, tiles, T, chans), f32),
+        scratch_shapes=[pltpu.VMEM((2, tiles, modes, 128), f32)],
         compiler_params=params,
-        name="near",
-    )(*far_memory(sv, near))
+        name="local",
+    )(*far_memory(sv, edge, powers, near, spread_f, spread_b))
 
     chunks = ((0, 4), (1, 4))
     square = shape((rows, chans), bf16)
     pair = shape((2, rows, chans), bf16)
     inputs = (
-        recv, *far_memory(fore, back, local, gates), above, below, gate_taps, rates,
+        recv, *far_memory(local, gates), gate_taps, rates,
         *far_memory(spread_f, spread_b),
     )
     z, out_up, out_down = pl.pallas_call(
@@ -442,7 +484,7 @@
     for hop in (2, 1, 0):
         ups_now = (parts[0].astype(f32) + up_sum).astype(bf16)
         downs_now = (parts[1].astype(f32) + down_sum).astype(bf16)
-        ups_now, downs_now, z = lax.optimization_barrier((ups_now, downs_now, z))
+        _, _, z = lax.optimization_barrier((ups_now, downs_now, z))
         up_sum, down_sum = turn(ups_now, 1).astype(f32), turn(downs_now, -1).astype(f32)
         parts = rest(z, (hop, -hop) if hop else (0,))
     total = parts[0].astype(f32) + up_sum + down_sum

time: 126 us -> 120 us (0.952)
  the two profiles are of different devices: /device:TPU:24 before, /device:TPU:96 now
where the time goes in v4:
time: 120 us; the launch traced here: 119 us
  Pallas kernels  50.6 us (42%)
  starting transfers between devices  35.2 us (29%)
  waiting for transfers between devices  24.2 us (20%)
  other arithmetic  8.67 us (7%)
    ppermute x16, starting transfers between devices, turn(): lax.ppermute(a, 'tp', [(c * ring + i, c * ring + (i + hop) % ring) for c...  25.9 us
    pallas_call x4, Pallas kernels, rest(): pl.pallas_call(functools.partial(rest_kernel, chunks), in_specs=[whole(z....  17.3 us
    pallas_call x3, Pallas kernels, project(): pl.pallas_call(functools.partial(early_kernel, slots, len(arrays), len(ca...  14.6 us
    ppermute x16, waiting for transfers between devices, turn(): lax.ppermute(a, 'tp', [(c * ring + i, c * ring + (i + hop) % ring) for c...  8.29 us
    ppermute x2, waiting for transfers between devices, across(): return lax.ppermute(a, 'tp', [(i, (i + ring) % tp) for i in range(tp)])  8.28 us
    all_to_all x1, waiting for transfers between devices, body(): recv = lax.all_to_all(send, 'seq', split_axis=0, concat_axis=0)  7.63 us
    all_to_all x1, starting transfers between devices, body(): recv = lax.all_to_all(send, 'seq', split_axis=0, concat_axis=0)  7.04 us
    pallas_call x1, Pallas kernels, body(): pl.pallas_call(local_kernel, out_shape=shape((2, tiles, T, chans), f32),...  6.14 us
  transfers between devices with their start and end apart: 19, of which 6 were waited for; matrix products, arithmetic and copies ran while one was open for 5% of the time, Pallas kernels for 33%

profile of v4, /device:TPU:96, one launch (start us, length us, event | category | flops | bytes accessed | tf_op | source)
XLA Modules:
  0.0 119.0 jit_solution(4400720889113709131)
XLA Ops:
  0.0 1.5 %collective-permute-start = (bf16[256,256]{1,0:T(8,128)(2,1)}, bf16[256,256]{1,0:T(8,128)(2,1)S(1)}, u32[]{:S(2)}, u32[]{:S(2)}) collective-permute-start(bf16[256,256]{1,0:T(8,128)(2,1)} %param.9), channel_id=1, source_target_pairs={{0,8},{1,9},{2,10},{3,11},{4,12},{5,13},{6,14},{7,15},{8,0},{9,1},... | collective-permute-start | bytes 393224 | tf_op jit(solution)/shard_map/ppermute | solution.py:345
  1.5 4.0 %collective-permute-done = bf16[256,256]{1,0:T(8,128)(2,1)S(1)} collective-permute-done((bf16[256,256]{1,0:T(8,128)(2,1)}, bf16[256,256]{1,0:T(8,128)(2,1)S(1)}, u32[]{:S(2)}, u32[]{:S(2)}) %collective-permute-start) | collective-permute-done | bytes 131104 | tf_op jit(solution)/shard_map/ppermute | solution.py:345
  6.4 3.2 %collective-permute-start.1 = (bf16[2,256,256]{2,1,0:T(8,128)(2,1)S(1)}, bf16[2,256,256]{2,1,0:T(8,128)(2,1)S(1)}, u32[]{:S(2)}, u32[]{:S(2)}) collective-permute-start(bf16[2,256,256]{2,1,0:T(8,128)(2,1)S(1)} %pad_maximum_fusion.refs_0_), channel_id=1, source_target_pairs={{0,1},{1,2},{2,3},{3,4},{4,5},{5,6},{6,7},{7,0},{8,9},{9,10},{10,1... | collective-permute-start | bytes 786440 | tf_op jit(solution)/shard_map/ppermute | solution.py:340
  9.6 1.7 %tables.1 = (f32[18,16,256]{2,1,0:T(8,128)}, f32[40,256]{1,0:T(8,128)}, f32[16,16,256]{2,1,0:T(8,128)}, f32[16,16,256]{2,1,0:T(8,128)}) custom-call(f32[16,256]{1,0:T(8,128)} %rates_ref.3, f32[16,256]{1,0:T(8,128)} %residues_ref.1), custom_call_target="tpu_custom_call" | custom-call | tf_op jit(solution)/shard_map/tables/pallas_call | solution.py:348
  11.3 3.0 %collective-permute-done.1.refs_1_ = bf16[2,256,256]{2,1,0:T(8,128)(2,1)S(1)} collective-permute-done((bf16[2,256,256]{2,1,0:T(8,128)(2,1)S(1)}, bf16[2,256,256]{2,1,0:T(8,128)(2,1)S(1)}, u32[]{:S(2)}, u32[]{:S(2)}) %collective-permute-start.1) | collective-permute-done | bytes 262176 | tf_op jit(solution)/shard_map/ppermute | solution.py:340
  14.3 3.7 %collective-permute-start.2 = (bf16[2,256,256]{2,1,0:T(8,128)(2,1)S(1)}, bf16[2,256,256]{2,1,0:T(8,128)(2,1)S(1)}, u32[]{:S(2)}, u32[]{:S(2)}) collective-permute-start(bf16[2,256,256]{2,1,0:T(8,128)(2,1)S(1)} %collective-permute-done.1.refs_1_), channel_id=1, source_target_pairs={{0,1},{1,2},{2,3},{3,4},{4,5},{5,6},{6,7},{7,0},{8,9},{9,10},{10,1... | collective-permute-start | bytes 786440 | tf_op jit(solution)/shard_map/ppermute | solution.py:340
  18.0 5.1 %project.3 = (f32[2,256,512]{2,1,0:T(8,128)}, f32[256,128]{1,0:T(8,128)}) custom-call(bf16[2,256,256]{2,1,0:T(8,128)(2,1)S(1)} %pad_maximum_fusion.refs_0_, bf16[2,256,256]{2,1,0:T(8,128)(2,1)S(1)} %collective-permute-done.1.refs_1_, bf16[2,256,256]{2,1,0:T(8,128)(2,1)S(1)} %collective-permute-done.3.refs_2_, f32[16,1,256]{2,1,0:T(1,128)} %bitcast.17, ...), custom_call_target="tpu_custom_call" | custom-call | flops 1006632960 | bytes 3932160 | tf_op jit(solution)/shard_map/project/pallas_call | solution.py:364
  23.1 3.3 %collective-permute-start.4 = (bf16[2,256,256]{2,1,0:T(8,128)(2,1)S(1)}, bf16[2,256,256]{2,1,0:T(8,128)(2,1)S(1)}, u32[]{:S(2)}, u32[]{:S(2)}) collective-permute-start(bf16[2,256,256]{2,1,0:T(8,128)(2,1)S(1)} %collective-permute-done.2.refs_0_), channel_id=1, source_target_pairs={{0,1},{1,2},{2,3},{3,4},{4,5},{5,6},{6,7},{7,0},{8,9},{9,10},{10,1... | collective-permute-start | bytes 786440 | tf_op jit(solution)/shard_map/ppermute | solution.py:340
  26.4 4.8 %project.4 = (f32[2,256,512]{2,1,0:T(8,128)}, f32[256,128]{1,0:T(8,128)}) custom-call(bf16[2,256,256]{2,1,0:T(8,128)(2,1)S(1)} %collective-permute-done.2.refs_0_, bf16[2,256,256]{2,1,0:T(8,128)(2,1)S(1)} %collective-permute-done.5.refs_1_, f32[16,1,256]{2,1,0:T(1,128)} %bitcast.18, bf16[4096,256]{1,0:T(8,128)(2,1)} %refs_3_.5, bf16[4096,256]{1,0:T(8,128)(2,1)} %refs_4_.7, ...), custom_call_target="tpu_custom_call" | custom-call | flops 671088640 | bytes 2621440 | tf_op jit(solution)/shard_map/project/pallas_call | solution.py:364
  31.2 3.3 %collective-permute-start.6 = (bf16[256,256]{1,0:T(8,128)(2,1)S(1)}, bf16[256,256]{1,0:T(8,128)(2,1)S(1)}, u32[]{:S(2)}, u32[]{:S(2)}) collective-permute-start(bf16[256,256]{1,0:T(8,128)(2,1)S(1)} %slice_bitcast_fusion.2), channel_id=1, source_target_pairs={{0,1},{1,2},{2,3},{3,4},{4,5},{5,6},{6,7},{7,0},{8,9},{9,10},{10,1... | collective-permute-start | bytes 393224 | tf_op jit(solution)/shard_map/ppermute | solution.py:340
  34.8 4.8 %project.5 = (f32[2,256,512]{2,1,0:T(8,128)}, f32[256,128]{1,0:T(8,128)}) custom-call(bf16[2,256,256]{2,1,0:T(8,128)(2,1)S(1)} %collective-permute-done.4.refs_0_, bf16[2,256,256]{2,1,0:T(8,128)(2,1)S(1)} %collective-permute-done.7.refs_1_, f32[16,1,256]{2,1,0:T(1,128)} %bitcast.19, bf16[4096,256]{1,0:T(8,128)(2,1)} %refs_3_.5, bf16[4096,256]{1,0:T(8,128)(2,1)} %refs_4_.7, ...), custom_call_target="tpu_custom_call" | custom-call | flops 671088640 | bytes 2621440 | tf_op jit(solution)/shard_map/project/pallas_call | solution.py:364
  39.6 1.4 %collective-permute-done.8.refs_1_ = bf16[256,256]{1,0:T(8,128)(2,1)S(1)} collective-permute-done((bf16[256,256]{1,0:T(8,128)(2,1)S(1)}, bf16[256,256]{1,0:T(8,128)(2,1)S(1)}, u32[]{:S(2)}, u32[]{:S(2)}) %collective-permute-start.8) | collective-permute-done | bytes 131104 | tf_op jit(solution)/shard_map/ppermute | solution.py:340
  41.0 5.8 %states.1 = (f32[16,16,640]{2,1,0:T(8,128)}, f32[2,16,16,256]{3,2,1,0:T(8,128)}, f32[256,512]{1,0:T(8,128)}, f32[2,2,8,256]{3,2,1,0:T(8,128)}) custom-call(bf16[256,256]{1,0:T(8,128)(2,1)S(1)} %collective-permute-done.6.refs_0_, bf16[256,256]{1,0:T(8,128)(2,1)S(1)} %collective-permute-done.8.refs_1_, f32[16,1,256]{2,1,0:T(1,128)} %bitcast.20, ...), custom_call_target="tpu_custom_call" | custom-call | tf_op jit(solution)/shard_map/states/pallas_call | solution.py:399
  46.8 7.0 %all-to-all-start = ((f32[16,16,640]{2,1,0:T(8,128)}), f32[16,16,640]{2,1,0:T(8,128)S(1)}, u32[]{:S(2)}, u32[]{:S(2)}) async-start(f32[16,16,640]{2,1,0:T(8,128)} %get-tuple-element.60), calls=%async_computation | async-start | bytes 1310720 | tf_op jit(solution)/shard_map/all_to_all | solution.py:430
  53.9 6.1 %local.1.local_ref = f32[2,16,16,256]{3,2,1,0:T(8,128)} custom-call(f32[2,16,16,256]{3,2,1,0:T(8,128)} %get-tuple-element.61.sv_ref, f32[2,2,8,256]{3,2,1,0:T(8,128)} %get-tuple-element.62.edge_ref, f32[18,16,256]{2,1,0:T(8,128)} %get-tuple-element.59.refs_8_.pow_ref, f32[40,256]{1,0:T(8,128)} %get-tuple-element.63.near_ref, ...), custom_call_target="tpu_custom_call" | custom-call | tf_op jit(solution)/shard_map/local/pallas_call | solution.py:431
  60.0 7.6 %all-to-all-done.recv_ref = f32[16,16,640]{2,1,0:T(8,128)S(1)} async-done(((f32[16,16,640]{2,1,0:T(8,128)}), f32[16,16,640]{2,1,0:T(8,128)S(1)}, u32[]{:S(2)}, u32[]{:S(2)}) %all-to-all-start) | async-done | bytes 655392 | tf_op jit(solution)/shard_map/all_to_all | solution.py:430
  67.6 5.0 %gated.1 = (bf16[256,512]{1,0:T(8,128)(2,1)}, bf16[256,256]{1,0:T(8,128)(2,1)}, bf16[256,256]{1,0:T(8,128)(2,1)}) custom-call(f32[16,16,640]{2,1,0:T(8,128)S(1)} %all-to-all-done.recv_ref, f32[2,16,16,256]{3,2,1,0:T(8,128)} %local.1.local_ref, f32[256,512]{1,0:T(8,128)} %get-tuple-element.66.gates_ref, f32[3,256]{1,0:T(4,128)} %gt_ref.1, ...), custom_call_target="tpu_custom_call" | custom-call | tf_op jit(solution)/shard_map/gated/pallas_call | solution.py:446
  72.6 2.0 %collective-permute-start.9 = (bf16[256,256]{1,0:T(8,128)(2,1)}, bf16[256,256]{1,0:T(8,128)(2,1)S(1)}, u32[]{:S(2)}, u32[]{:S(2)}) collective-permute-start(bf16[256,256]{1,0:T(8,128)(2,1)} %get-tuple-element.69), channel_id=1, source_target_pairs={{0,1},{1,2},{2,3},{3,4},{4,5},{5,6},{6,7},{7,0},{8,9},{9,10},{10,1... | collective-permute-start | bytes 393224 | tf_op jit(solution)/shard_map/ppermute | solution.py:340
  74.7 4.6 %rest.4 = (bf16[2,256,256]{2,1,0:T(8,128)(2,1)}, bf16[2,256,256]{2,1,0:T(8,128)(2,1)}) custom-call(bf16[256,512]{1,0:T(8,128)(2,1)} %get-tuple-element.78.z_ref, bf16[256,4096]{1,0:T(8,128)(2,1)} %wo_ref.9), custom_call_target="tpu_custom_call" | custom-call | flops 402653184 | bytes 1572864 | tf_op jit(solution)/shard_map/rest/pallas_call | solution.py:463
  80.3 3.2 %collective-permute-start.11 = (bf16[2,256,256]{2,1,0:T(8,128)(2,1)S(1)}, bf16[2,256,256]{2,1,0:T(8,128)(2,1)S(1)}, u32[]{:S(2)}, u32[]{:S(2)}) collective-permute-start(bf16[2,256,256]{2,1,0:T(8,128)(2,1)S(1)} %add_convert_fusion.5), channel_id=1, source_target_pairs={{0,1},{1,2},{2,3},{3,4},{4,5},{5,6},{6,7},{7,0},{8,9},{9,10},{10,1... | collective-permute-start | bytes 786440 | tf_op jit(solution)/shard_map/ppermute | solution.py:340
  84.6 4.6 %rest.5 = (bf16[2,256,256]{2,1,0:T(8,128)(2,1)}, bf16[2,256,256]{2,1,0:T(8,128)(2,1)}) custom-call(bf16[256,512]{1,0:T(8,128)(2,1)} %get-tuple-element.78.z_ref, bf16[256,4096]{1,0:T(8,128)(2,1)} %wo_ref.9), custom_call_target="tpu_custom_call" | custom-call | flops 402653184 | bytes 1572864 | tf_op jit(solution)/shard_map/rest/pallas_call | solution.py:463
  89.1 1.0 add_convert_fusion.3
  90.2 3.3 %collective-permute-start.13 = (bf16[2,256,256]{2,1,0:T(8,128)(2,1)S(1)}, bf16[2,256,256]{2,1,0:T(8,128)(2,1)S(1)}, u32[]{:S(2)}, u32[]{:S(2)}) collective-permute-start(bf16[2,256,256]{2,1,0:T(8,128)(2,1)S(1)} %add_convert_fusion.3), channel_id=1, source_target_pairs={{0,1},{1,2},{2,3},{3,4},{4,5},{5,6},{6,7},{7,0},{8,9},{9,10},{10,1... | collective-permute-start | bytes 786440 | tf_op jit(solution)/shard_map/ppermute | solution.py:340
  93.5 1.0 add_convert_fusion.2
  94.6 4.6 %rest.6 = (bf16[2,256,256]{2,1,0:T(8,128)(2,1)}, bf16[2,256,256]{2,1,0:T(8,128)(2,1)}) custom-call(bf16[256,512]{1,0:T(8,128)(2,1)} %get-tuple-element.78.z_ref, bf16[256,4096]{1,0:T(8,128)(2,1)} %wo_ref.9), custom_call_target="tpu_custom_call" | custom-call | flops 402653184 | bytes 1572864 | tf_op jit(solution)/shard_map/rest/pallas_call | solution.py:463
  99.2 1.0 add_convert_fusion.1
  100.2 3.3 %collective-permute-start.15 = (bf16[2,256,256]{2,1,0:T(8,128)(2,1)S(1)}, bf16[2,256,256]{2,1,0:T(8,128)(2,1)S(1)}, u32[]{:S(2)}, u32[]{:S(2)}) collective-permute-start(bf16[2,256,256]{2,1,0:T(8,128)(2,1)S(1)} %add_convert_fusion.1), channel_id=1, source_target_pairs={{0,1},{1,2},{2,3},{3,4},{4,5},{5,6},{6,7},{7,0},{8,9},{9,10},{10,1... | collective-permute-start | bytes 786440 | tf_op jit(solution)/shard_map/ppermute | solution.py:340
  103.5 1.0 add_convert_fusion
  104.6 3.6 %rest.7 = bf16[2,256,256]{2,1,0:T(8,128)(2,1)} custom-call(bf16[256,512]{1,0:T(8,128)(2,1)} %get-tuple-element.78.z_ref, bf16[256,4096]{1,0:T(8,128)(2,1)} %wo_ref.9), custom_call_target="tpu_custom_call" | custom-call | flops 201326592 | bytes 786432 | tf_op jit(solution)/shard_map/rest/pallas_call | solution.py:463
  108.2 3.9 %collective-permute-done.16 = bf16[2,256,256]{2,1,0:T(8,128)(2,1)S(1)} collective-permute-done((bf16[2,256,256]{2,1,0:T(8,128)(2,1)S(1)}, bf16[2,256,256]{2,1,0:T(8,128)(2,1)S(1)}, u32[]{:S(2)}, u32[]{:S(2)}) %collective-permute-start.16) | collective-permute-done | bytes 262176 | tf_op jit(solution)/shard_map/ppermute | solution.py:340
  112.2 1.0 convert_add_fusion
  113.9 4.3 %collective-permute-done.17 = bf16[256,256]{1,0:T(8,128)(2,1)S(1)} collective-permute-done((bf16[256,256]{1,0:T(8,128)(2,1)S(1)}, bf16[256,256]{1,0:T(8,128)(2,1)S(1)}, u32[]{:S(2)}, u32[]{:S(2)}) %collective-permute-start.17) | collective-permute-done | bytes 131104 | tf_op jit(solution)/shard_map/ppermute | solution.py:345
  (29 shorter events, 5.0 us)
Async XLA Ops:
  0.0 5.4 %collective-permute-start = (bf16[256,256]{1,0:T(8,128)(2,1)}, bf16[256,256]{1,0:T(8,128)(2,1)S(1)}, u32[]{:S(2)}, u32[]{:S(2)}) collective-permute-start(bf16[256,256]{1,0:T(8,128)(2,1)} %param.9), channel_id=1, source_target_pairs={{0,8},{1,9},{2,10},{3,11},{4,12},{5,13},{6,14},{7,15},{8,0},{9,1},... | collective-permute-start | bytes 393224 | tf_op jit(solution)/shard_map/ppermute | solution.py:345
  6.4 7.9 %collective-permute-start.1 = (bf16[2,256,256]{2,1,0:T(8,128)(2,1)S(1)}, bf16[2,256,256]{2,1,0:T(8,128)(2,1)S(1)}, u32[]{:S(2)}, u32[]{:S(2)}) collective-permute-start(bf16[2,256,256]{2,1,0:T(8,128)(2,1)S(1)} %pad_maximum_fusion.refs_0_), channel_id=1, source_target_pairs={{0,1},{1,2},{2,3},{3,4},{4,5},{5,6},{6,7},{7,0},{8,9},{9,10},{10,1... | collective-permute-start | bytes 786440 | tf_op jit(solution)/shard_map/ppermute | solution.py:340
  9.6 8.4 %collective-permute-start.3 = (bf16[2,256,256]{2,1,0:T(8,128)(2,1)S(1)}, bf16[2,256,256]{2,1,0:T(8,128)(2,1)S(1)}, u32[]{:S(2)}, u32[]{:S(2)}) collective-permute-start(bf16[2,256,256]{2,1,0:T(8,128)(2,1)S(1)} %pad_maximum_fusion.refs_0_), channel_id=1, source_target_pairs={{0,7},{1,0},{2,1},{3,2},{4,3},{5,4},{6,5},{7,6},{8,15},{9,8},{10,9... | collective-permute-start | bytes 786440 | tf_op jit(solution)/shard_map/ppermute | solution.py:340
  14.3 8.8 %collective-permute-start.2 = (bf16[2,256,256]{2,1,0:T(8,128)(2,1)S(1)}, bf16[2,256,256]{2,1,0:T(8,128)(2,1)S(1)}, u32[]{:S(2)}, u32[]{:S(2)}) collective-permute-start(bf16[2,256,256]{2,1,0:T(8,128)(2,1)S(1)} %collective-permute-done.1.refs_1_), channel_id=1, source_target_pairs={{0,1},{1,2},{2,3},{3,4},{4,5},{5,6},{6,7},{7,0},{8,9},{9,10},{10,1... | collective-permute-start | bytes 786440 | tf_op jit(solution)/shard_map/ppermute | solution.py:340
  18.0 8.4 %collective-permute-start.5 = (bf16[2,256,256]{2,1,0:T(8,128)(2,1)S(1)}, bf16[2,256,256]{2,1,0:T(8,128)(2,1)S(1)}, u32[]{:S(2)}, u32[]{:S(2)}) collective-permute-start(bf16[2,256,256]{2,1,0:T(8,128)(2,1)S(1)} %collective-permute-done.3.refs_2_), channel_id=1, source_target_pairs={{0,7},{1,0},{2,1},{3,2},{4,3},{5,4},{6,5},{7,6},{8,15},{9,8},{10,9... | collective-permute-start | bytes 786440 | tf_op jit(solution)/shard_map/ppermute | solution.py:340
  23.1 8.1 %collective-permute-start.4 = (bf16[2,256,256]{2,1,0:T(8,128)(2,1)S(1)}, bf16[2,256,256]{2,1,0:T(8,128)(2,1)S(1)}, u32[]{:S(2)}, u32[]{:S(2)}) collective-permute-start(bf16[2,256,256]{2,1,0:T(8,128)(2,1)S(1)} %collective-permute-done.2.refs_0_), channel_id=1, source_target_pairs={{0,1},{1,2},{2,3},{3,4},{4,5},{5,6},{6,7},{7,0},{8,9},{9,10},{10,1... | collective-permute-start | bytes 786440 | tf_op jit(solution)/shard_map/ppermute | solution.py:340
  26.4 8.1 %collective-permute-start.7 = (bf16[2,256,256]{2,1,0:T(8,128)(2,1)S(1)}, bf16[2,256,256]{2,1,0:T(8,128)(2,1)S(1)}, u32[]{:S(2)}, u32[]{:S(2)}) collective-permute-start(bf16[2,256,256]{2,1,0:T(8,128)(2,1)S(1)} %collective-permute-done.5.refs_1_), channel_id=1, source_target_pairs={{0,7},{1,0},{2,1},{3,2},{4,3},{5,4},{6,5},{7,6},{8,15},{9,8},{10,9... | collective-permute-start | bytes 786440 | tf_op jit(solution)/shard_map/ppermute | solution.py:340
  31.2 8.4 %collective-permute-start.6 = (bf16[256,256]{1,0:T(8,128)(2,1)S(1)}, bf16[256,256]{1,0:T(8,128)(2,1)S(1)}, u32[]{:S(2)}, u32[]{:S(2)}) collective-permute-start(bf16[256,256]{1,0:T(8,128)(2,1)S(1)} %slice_bitcast_fusion.2), channel_id=1, source_target_pairs={{0,1},{1,2},{2,3},{3,4},{4,5},{5,6},{6,7},{7,0},{8,9},{9,10},{10,1... | collective-permute-start | bytes 393224 | tf_op jit(solution)/shard_map/ppermute | solution.py:340
  34.5 6.4 %collective-permute-start.8 = (bf16[256,256]{1,0:T(8,128)(2,1)S(1)}, bf16[256,256]{1,0:T(8,128)(2,1)S(1)}, u32[]{:S(2)}, u32[]{:S(2)}) collective-permute-start(bf16[256,256]{1,0:T(8,128)(2,1)S(1)} %slice_bitcast_fusion.1), channel_id=1, source_target_pairs={{0,7},{1,0},{2,1},{3,2},{4,3},{5,4},{6,5},{7,6},{8,15},{9,8},{10,9... | collective-permute-start | bytes 393224 | tf_op jit(solution)/shard_map/ppermute | solution.py:340
  46.8 20.8 %all-to-all-start = ((f32[16,16,640]{2,1,0:T(8,128)}), f32[16,16,640]{2,1,0:T(8,128)S(1)}, u32[]{:S(2)}, u32[]{:S(2)}) async-start(f32[16,16,640]{2,1,0:T(8,128)} %get-tuple-element.60), calls=%async_computation | async-start | bytes 1310720 | tf_op jit(solution)/shard_map/all_to_all | solution.py:430
  72.6 6.7 %collective-permute-start.9 = (bf16[256,256]{1,0:T(8,128)(2,1)}, bf16[256,256]{1,0:T(8,128)(2,1)S(1)}, u32[]{:S(2)}, u32[]{:S(2)}) collective-permute-start(bf16[256,256]{1,0:T(8,128)(2,1)} %get-tuple-element.69), channel_id=1, source_target_pairs={{0,1},{1,2},{2,3},{3,4},{4,5},{5,6},{6,7},{7,0},{8,9},{9,10},{10,1... | collective-permute-start | bytes 393224 | tf_op jit(solution)/shard_map/ppermute | solution.py:340
  74.6 8.9 %collective-permute-start.10 = (bf16[256,256]{1,0:T(8,128)(2,1)}, bf16[256,256]{1,0:T(8,128)(2,1)S(1)}, u32[]{:S(2)}, u32[]{:S(2)}) collective-permute-start(bf16[256,256]{1,0:T(8,128)(2,1)} %get-tuple-element.71), channel_id=1, source_target_pairs={{0,7},{1,0},{2,1},{3,2},{4,3},{5,4},{6,5},{7,6},{8,15},{9,8},{10,9... | collective-permute-start | bytes 393224 | tf_op jit(solution)/shard_map/ppermute | solution.py:340
  80.3 8.8 %collective-permute-start.11 = (bf16[2,256,256]{2,1,0:T(8,128)(2,1)S(1)}, bf16[2,256,256]{2,1,0:T(8,128)(2,1)S(1)}, u32[]{:S(2)}, u32[]{:S(2)}) collective-permute-start(bf16[2,256,256]{2,1,0:T(8,128)(2,1)S(1)} %add_convert_fusion.5), channel_id=1, source_target_pairs={{0,1},{1,2},{2,3},{3,4},{4,5},{5,6},{6,7},{7,0},{8,9},{9,10},{10,1... | collective-permute-start | bytes 786440 | tf_op jit(solution)/shard_map/ppermute | solution.py:340
  84.5 9.0 %collective-permute-start.12 = (bf16[2,256,256]{2,1,0:T(8,128)(2,1)S(1)}, bf16[2,256,256]{2,1,0:T(8,128)(2,1)S(1)}, u32[]{:S(2)}, u32[]{:S(2)}) collective-permute-start(bf16[2,256,256]{2,1,0:T(8,128)(2,1)S(1)} %add_convert_fusion.4), channel_id=1, source_target_pairs={{0,7},{1,0},{2,1},{3,2},{4,3},{5,4},{6,5},{7,6},{8,15},{9,8},{10,9... | collective-permute-start | bytes 786440 | tf_op jit(solution)/shard_map/ppermute | solution.py:340
  90.2 9.0 %collective-permute-start.13 = (bf16[2,256,256]{2,1,0:T(8,128)(2,1)S(1)}, bf16[2,256,256]{2,1,0:T(8,128)(2,1)S(1)}, u32[]{:S(2)}, u32[]{:S(2)}) collective-permute-start(bf16[2,256,256]{2,1,0:T(8,128)(2,1)S(1)} %add_convert_fusion.3), channel_id=1, source_target_pairs={{0,1},{1,2},{2,3},{3,4},{4,5},{5,6},{6,7},{7,0},{8,9},{9,10},{10,1... | collective-permute-start | bytes 786440 | tf_op jit(solution)/shard_map/ppermute | solution.py:340
  94.5 9.0 %collective-permute-start.14 = (bf16[2,256,256]{2,1,0:T(8,128)(2,1)S(1)}, bf16[2,256,256]{2,1,0:T(8,128)(2,1)S(1)}, u32[]{:S(2)}, u32[]{:S(2)}) collective-permute-start(bf16[2,256,256]{2,1,0:T(8,128)(2,1)S(1)} %add_convert_fusion.2), channel_id=1, source_target_pairs={{0,7},{1,0},{2,1},{3,2},{4,3},{5,4},{6,5},{7,6},{8,15},{9,8},{10,9... | collective-permute-start | bytes 786440 | tf_op jit(solution)/shard_map/ppermute | solution.py:340
  100.2 8.0 %collective-permute-start.15 = (bf16[2,256,256]{2,1,0:T(8,128)(2,1)S(1)}, bf16[2,256,256]{2,1,0:T(8,128)(2,1)S(1)}, u32[]{:S(2)}, u32[]{:S(2)}) collective-permute-start(bf16[2,256,256]{2,1,0:T(8,128)(2,1)S(1)} %add_convert_fusion.1), channel_id=1, source_target_pairs={{0,1},{1,2},{2,3},{3,4},{4,5},{5,6},{6,7},{7,0},{8,9},{9,10},{10,1... | collective-permute-start | bytes 786440 | tf_op jit(solution)/shard_map/ppermute | solution.py:340
  104.5 7.7 %collective-permute-start.16 = (bf16[2,256,256]{2,1,0:T(8,128)(2,1)S(1)}, bf16[2,256,256]{2,1,0:T(8,128)(2,1)S(1)}, u32[]{:S(2)}, u32[]{:S(2)}) collective-permute-start(bf16[2,256,256]{2,1,0:T(8,128)(2,1)S(1)} %add_convert_fusion), channel_id=1, source_target_pairs={{0,7},{1,0},{2,1},{3,2},{4,3},{5,4},{6,5},{7,6},{8,15},{9,8},{10,9... | collective-permute-start | bytes 786440 | tf_op jit(solution)/shard_map/ppermute | solution.py:340
  113.2 5.1 %collective-permute-start.17 = (bf16[256,256]{1,0:T(8,128)(2,1)S(1)}, bf16[256,256]{1,0:T(8,128)(2,1)S(1)}, u32[]{:S(2)}, u32[]{:S(2)}) collective-permute-start(bf16[256,256]{1,0:T(8,128)(2,1)S(1)} %fusion.2), channel_id=1, source_target_pairs={{0,8},{1,9},{2,10},{3,11},{4,12},{5,13},{6,14},{7,15},{8,0},{9,1},... | collective-permute-start | bytes 393224 | tf_op jit(solution)/shard_map/ppermute | solution.py:345

commit v5 on v4

--- a/solution.py
+++ b/solution.py
@@ -306,11 +306,14 @@
 
 
 def rest_kernel(chunks, z_ref, wo_ref, *refs):
-    outs, (w_buf, sems) = refs[:-2], refs[-2:]
+    outs, (z_buf, w_buf, sems) = refs[:-3], refs[-3:]
+    arrive = pltpu.make_async_copy(z_ref, z_buf, sems.at[len(chunks), 0])
+    arrive.start()
     copies = fetch_columns(chunks, wo_ref, w_buf, sems)
     flip = reversal(w_buf.shape[2])
+    arrive.wait()
     for n in range(len(chunks)):
-        outs[n // 2][n % 2] = partial_chunk(n, copies, z_ref, w_buf, flip).astype(bf16)
+        outs[n // 2][n % 2] = partial_chunk(n, copies, z_buf, w_buf, flip).astype(bf16)
 
 
 def far_memory(*arrays):
@@ -462,12 +465,13 @@
         chunks = tuple((c, hop) for hop in hops for c in range(2))
         return pl.pallas_call(
             functools.partial(rest_kernel, chunks),
-            in_specs=[whole(z.shape), remote],
+            in_specs=[remote, remote],
             out_specs=[whole((2, rows, chans))] * len(hops),
             out_shape=(pair,) * len(hops),
             scratch_shapes=[
+                pltpu.VMEM(z.shape, bf16),
                 pltpu.VMEM((len(chunks), 2, chans, chans), bf16),
-                pltpu.SemaphoreType.DMA((len(chunks), 2)),
+                pltpu.SemaphoreType.DMA((len(chunks) + 1, 2)),
             ],
             compiler_params=params,
             cost_estimate=pl.CostEstimate(

time: 120 us -> 117 us (0.975)
  Pallas kernels: 50.6 us -> 47.2 us
    pallas_call x4, Pallas kernels: 17.3 us -> 13.9 us  [rest(): pl.pallas_call(functools.partial(rest_kernel, chunks), in_specs=[remote,...]
  transfers between devices with their start and end apart: 19 -> 19, of which waited for: 6 -> 6; matrix products, arithmetic and copies ran while one was open for 5% -> 5% of each run, Pallas kernels for 33% -> 31%
where the time goes in v5:
time: 117 us
  Pallas kernels  47.2 us (40%)
  starting transfers between devices  35.4 us (30%)
  waiting for transfers between devices  25.1 us (21%)
  other arithmetic  8.67 us (7%)
    ppermute x16, starting transfers between devices, turn(): lax.ppermute(a, 'tp', [(c * ring + i, c * ring + (i + hop) % ring) for c...  26.1 us
    pallas_call x3, Pallas kernels, project(): pl.pallas_call(functools.partial(early_kernel, slots, len(arrays), len(ca...  14.6 us
    pallas_call x4, Pallas kernels, rest(): pl.pallas_call(functools.partial(rest_kernel, chunks), in_specs=[remote,...  13.9 us
    ppermute x16, waiting for transfers between devices, turn(): lax.ppermute(a, 'tp', [(c * ring + i, c * ring + (i + hop) % ring) for c...  9.17 us
    ppermute x2, waiting for transfers between devices, across(): return lax.ppermute(a, 'tp', [(i, (i + ring) % tp) for i in range(tp)])  8.28 us
    all_to_all x1, waiting for transfers between devices, body(): recv = lax.all_to_all(send, 'seq', split_axis=0, concat_axis=0)  7.63 us
    all_to_all x1, starting transfers between devices, body(): recv = lax.all_to_all(send, 'seq', split_axis=0, concat_axis=0)  7.04 us
    pallas_call x1, Pallas kernels, body(): pl.pallas_call(local_kernel, out_shape=shape((2, tiles, T, chans), f32),...  6.14 us
  transfers between devices with their start and end apart: 19, of which 6 were waited for; matrix products, arithmetic and copies ran while one was open for 5% of the time, Pallas kernels for 31%

profile of v5, /device:TPU:96, one launch (start us, length us, event | category | flops | bytes accessed | tf_op | source)
XLA Modules:
  0.0 116.5 jit_solution(17864407142515190990)
XLA Ops:
  0.0 1.5 %collective-permute-start = (bf16[256,256]{1,0:T(8,128)(2,1)}, bf16[256,256]{1,0:T(8,128)(2,1)S(1)}, u32[]{:S(2)}, u32[]{:S(2)}) collective-permute-start(bf16[256,256]{1,0:T(8,128)(2,1)} %param.9), channel_id=1, source_target_pairs={{0,8},{1,9},{2,10},{3,11},{4,12},{5,13},{6,14},{7,15},{8,0},{9,1},... | collective-permute-start | bytes 393224 | tf_op jit(solution)/shard_map/ppermute | solution.py:348
  1.5 4.0 %collective-permute-done = bf16[256,256]{1,0:T(8,128)(2,1)S(1)} collective-permute-done((bf16[256,256]{1,0:T(8,128)(2,1)}, bf16[256,256]{1,0:T(8,128)(2,1)S(1)}, u32[]{:S(2)}, u32[]{:S(2)}) %collective-permute-start) | collective-permute-done | bytes 131104 | tf_op jit(solution)/shard_map/ppermute | solution.py:348
  6.4 3.2 %collective-permute-start.1 = (bf16[2,256,256]{2,1,0:T(8,128)(2,1)S(1)}, bf16[2,256,256]{2,1,0:T(8,128)(2,1)S(1)}, u32[]{:S(2)}, u32[]{:S(2)}) collective-permute-start(bf16[2,256,256]{2,1,0:T(8,128)(2,1)S(1)} %pad_maximum_fusion.refs_0_), channel_id=1, source_target_pairs={{0,1},{1,2},{2,3},{3,4},{4,5},{5,6},{6,7},{7,0},{8,9},{9,10},{10,1... | collective-permute-start | bytes 786440 | tf_op jit(solution)/shard_map/ppermute | solution.py:343
  9.6 1.7 %tables.1 = (f32[18,16,256]{2,1,0:T(8,128)}, f32[40,256]{1,0:T(8,128)}, f32[16,16,256]{2,1,0:T(8,128)}, f32[16,16,256]{2,1,0:T(8,128)}) custom-call(f32[16,256]{1,0:T(8,128)} %rates_ref.3, f32[16,256]{1,0:T(8,128)} %residues_ref.1), custom_call_target="tpu_custom_call" | custom-call | tf_op jit(solution)/shard_map/tables/pallas_call | solution.py:351
  11.3 3.0 %collective-permute-done.1.refs_1_ = bf16[2,256,256]{2,1,0:T(8,128)(2,1)S(1)} collective-permute-done((bf16[2,256,256]{2,1,0:T(8,128)(2,1)S(1)}, bf16[2,256,256]{2,1,0:T(8,128)(2,1)S(1)}, u32[]{:S(2)}, u32[]{:S(2)}) %collective-permute-start.1) | collective-permute-done | bytes 262176 | tf_op jit(solution)/shard_map/ppermute | solution.py:343
  14.3 3.7 %collective-permute-start.2 = (bf16[2,256,256]{2,1,0:T(8,128)(2,1)S(1)}, bf16[2,256,256]{2,1,0:T(8,128)(2,1)S(1)}, u32[]{:S(2)}, u32[]{:S(2)}) collective-permute-start(bf16[2,256,256]{2,1,0:T(8,128)(2,1)S(1)} %collective-permute-done.1.refs_1_), channel_id=1, source_target_pairs={{0,1},{1,2},{2,3},{3,4},{4,5},{5,6},{6,7},{7,0},{8,9},{9,10},{10,1... | collective-permute-start | bytes 786440 | tf_op jit(solution)/shard_map/ppermute | solution.py:343
  18.0 5.1 %project.3 = (f32[2,256,512]{2,1,0:T(8,128)}, f32[256,128]{1,0:T(8,128)}) custom-call(bf16[2,256,256]{2,1,0:T(8,128)(2,1)S(1)} %pad_maximum_fusion.refs_0_, bf16[2,256,256]{2,1,0:T(8,128)(2,1)S(1)} %collective-permute-done.1.refs_1_, bf16[2,256,256]{2,1,0:T(8,128)(2,1)S(1)} %collective-permute-done.3.refs_2_, f32[16,1,256]{2,1,0:T(1,128)} %bitcast.17, ...), custom_call_target="tpu_custom_call" | custom-call | flops 1006632960 | bytes 3932160 | tf_op jit(solution)/shard_map/project/pallas_call | solution.py:367
  23.1 3.3 %collective-permute-start.4 = (bf16[2,256,256]{2,1,0:T(8,128)(2,1)S(1)}, bf16[2,256,256]{2,1,0:T(8,128)(2,1)S(1)}, u32[]{:S(2)}, u32[]{:S(2)}) collective-permute-start(bf16[2,256,256]{2,1,0:T(8,128)(2,1)S(1)} %collective-permute-done.2.refs_0_), channel_id=1, source_target_pairs={{0,1},{1,2},{2,3},{3,4},{4,5},{5,6},{6,7},{7,0},{8,9},{9,10},{10,1... | collective-permute-start | bytes 786440 | tf_op jit(solution)/shard_map/ppermute | solution.py:343
  26.4 4.8 %project.4 = (f32[2,256,512]{2,1,0:T(8,128)}, f32[256,128]{1,0:T(8,128)}) custom-call(bf16[2,256,256]{2,1,0:T(8,128)(2,1)S(1)} %collective-permute-done.2.refs_0_, bf16[2,256,256]{2,1,0:T(8,128)(2,1)S(1)} %collective-permute-done.5.refs_1_, f32[16,1,256]{2,1,0:T(1,128)} %bitcast.18, bf16[4096,256]{1,0:T(8,128)(2,1)} %refs_3_.5, bf16[4096,256]{1,0:T(8,128)(2,1)} %refs_4_.7, ...), custom_call_target="tpu_custom_call" | custom-call | flops 671088640 | bytes 2621440 | tf_op jit(solution)/shard_map/project/pallas_call | solution.py:367
  31.2 3.3 %collective-permute-start.6 = (bf16[256,256]{1,0:T(8,128)(2,1)S(1)}, bf16[256,256]{1,0:T(8,128)(2,1)S(1)}, u32[]{:S(2)}, u32[]{:S(2)}) collective-permute-start(bf16[256,256]{1,0:T(8,128)(2,1)S(1)} %slice_bitcast_fusion.2), channel_id=1, source_target_pairs={{0,1},{1,2},{2,3},{3,4},{4,5},{5,6},{6,7},{7,0},{8,9},{9,10},{10,1... | collective-permute-start | bytes 393224 | tf_op jit(solution)/shard_map/ppermute | solution.py:343
  34.8 4.8 %project.5 = (f32[2,256,512]{2,1,0:T(8,128)}, f32[256,128]{1,0:T(8,128)}) custom-call(bf16[2,256,256]{2,1,0:T(8,128)(2,1)S(1)} %collective-permute-done.4.refs_0_, bf16[2,256,256]{2,1,0:T(8,128)(2,1)S(1)} %collective-permute-done.7.refs_1_, f32[16,1,256]{2,1,0:T(1,128)} %bitcast.19, bf16[4096,256]{1,0:T(8,128)(2,1)} %refs_3_.5, bf16[4096,256]{1,0:T(8,128)(2,1)} %refs_4_.7, ...), custom_call_target="tpu_custom_call" | custom-call | flops 671088640 | bytes 2621440 | tf_op jit(solution)/shard_map/project/pallas_call | solution.py:367
  39.6 1.4 %collective-permute-done.8.refs_1_ = bf16[256,256]{1,0:T(8,128)(2,1)S(1)} collective-permute-done((bf16[256,256]{1,0:T(8,128)(2,1)S(1)}, bf16[256,256]{1,0:T(8,128)(2,1)S(1)}, u32[]{:S(2)}, u32[]{:S(2)}) %collective-permute-start.8) | collective-permute-done | bytes 131104 | tf_op jit(solution)/shard_map/ppermute | solution.py:343
  41.0 5.8 %states.1 = (f32[16,16,640]{2,1,0:T(8,128)}, f32[2,16,16,256]{3,2,1,0:T(8,128)}, f32[256,512]{1,0:T(8,128)}, f32[2,2,8,256]{3,2,1,0:T(8,128)}) custom-call(bf16[256,256]{1,0:T(8,128)(2,1)S(1)} %collective-permute-done.6.refs_0_, bf16[256,256]{1,0:T(8,128)(2,1)S(1)} %collective-permute-done.8.refs_1_, f32[16,1,256]{2,1,0:T(1,128)} %bitcast.20, ...), custom_call_target="tpu_custom_call" | custom-call | tf_op jit(solution)/shard_map/states/pallas_call | solution.py:402
  46.8 7.0 %all-to-all-start = ((f32[16,16,640]{2,1,0:T(8,128)}), f32[16,16,640]{2,1,0:T(8,128)S(1)}, u32[]{:S(2)}, u32[]{:S(2)}) async-start(f32[16,16,640]{2,1,0:T(8,128)} %get-tuple-element.60), calls=%async_computation | async-start | bytes 1310720 | tf_op jit(solution)/shard_map/all_to_all | solution.py:433
  53.9 6.1 %local.1.local_ref = f32[2,16,16,256]{3,2,1,0:T(8,128)} custom-call(f32[2,16,16,256]{3,2,1,0:T(8,128)} %get-tuple-element.61.sv_ref, f32[2,2,8,256]{3,2,1,0:T(8,128)} %get-tuple-element.62.edge_ref, f32[18,16,256]{2,1,0:T(8,128)} %get-tuple-element.59.refs_8_.pow_ref, f32[40,256]{1,0:T(8,128)} %get-tuple-element.63.near_ref, ...), custom_call_target="tpu_custom_call" | custom-call | tf_op jit(solution)/shard_map/local/pallas_call | solution.py:434
  60.0 7.6 %all-to-all-done.recv_ref = f32[16,16,640]{2,1,0:T(8,128)S(1)} async-done(((f32[16,16,640]{2,1,0:T(8,128)}), f32[16,16,640]{2,1,0:T(8,128)S(1)}, u32[]{:S(2)}, u32[]{:S(2)}) %all-to-all-start) | async-done | bytes 655392 | tf_op jit(solution)/shard_map/all_to_all | solution.py:433
  67.6 5.0 %gated.1 = (bf16[256,512]{1,0:T(8,128)(2,1)}, bf16[256,256]{1,0:T(8,128)(2,1)}, bf16[256,256]{1,0:T(8,128)(2,1)}) custom-call(f32[16,16,640]{2,1,0:T(8,128)S(1)} %all-to-all-done.recv_ref, f32[2,16,16,256]{3,2,1,0:T(8,128)} %local.1.local_ref, f32[256,512]{1,0:T(8,128)} %get-tuple-element.66.gates_ref, f32[3,256]{1,0:T(4,128)} %gt_ref.1, ...), custom_call_target="tpu_custom_call" | custom-call | tf_op jit(solution)/shard_map/gated/pallas_call | solution.py:449
  72.6 2.0 %collective-permute-start.9 = (bf16[256,256]{1,0:T(8,128)(2,1)}, bf16[256,256]{1,0:T(8,128)(2,1)S(1)}, u32[]{:S(2)}, u32[]{:S(2)}) collective-permute-start(bf16[256,256]{1,0:T(8,128)(2,1)} %get-tuple-element.69), channel_id=1, source_target_pairs={{0,1},{1,2},{2,3},{3,4},{4,5},{5,6},{6,7},{7,0},{8,9},{9,10},{10,1... | collective-permute-start | bytes 393224 | tf_op jit(solution)/shard_map/ppermute | solution.py:343
  74.7 3.7 %rest.4 = (bf16[2,256,256]{2,1,0:T(8,128)(2,1)}, bf16[2,256,256]{2,1,0:T(8,128)(2,1)}) custom-call(bf16[256,512]{1,0:T(8,128)(2,1)} %get-tuple-element.78.z_ref, bf16[256,4096]{1,0:T(8,128)(2,1)} %wo_ref.9), custom_call_target="tpu_custom_call" | custom-call | flops 402653184 | bytes 1572864 | tf_op jit(solution)/shard_map/rest/pallas_call | solution.py:466
  79.4 3.2 %collective-permute-start.11 = (bf16[2,256,256]{2,1,0:T(8,128)(2,1)S(1)}, bf16[2,256,256]{2,1,0:T(8,128)(2,1)S(1)}, u32[]{:S(2)}, u32[]{:S(2)}) collective-permute-start(bf16[2,256,256]{2,1,0:T(8,128)(2,1)S(1)} %add_convert_fusion.5), channel_id=1, source_target_pairs={{0,1},{1,2},{2,3},{3,4},{4,5},{5,6},{6,7},{7,0},{8,9},{9,10},{10,1... | collective-permute-start | bytes 786440 | tf_op jit(solution)/shard_map/ppermute | solution.py:343
  83.7 3.7 %rest.5 = (bf16[2,256,256]{2,1,0:T(8,128)(2,1)}, bf16[2,256,256]{2,1,0:T(8,128)(2,1)}) custom-call(bf16[256,512]{1,0:T(8,128)(2,1)} %get-tuple-element.78.z_ref, bf16[256,4096]{1,0:T(8,128)(2,1)} %wo_ref.9), custom_call_target="tpu_custom_call" | custom-call | flops 402653184 | bytes 1572864 | tf_op jit(solution)/shard_map/rest/pallas_call | solution.py:466
  87.4 1.0 add_convert_fusion.3
  88.4 3.5 %collective-permute-start.13 = (bf16[2,256,256]{2,1,0:T(8,128)(2,1)S(1)}, bf16[2,256,256]{2,1,0:T(8,128)(2,1)S(1)}, u32[]{:S(2)}, u32[]{:S(2)}) collective-permute-start(bf16[2,256,256]{2,1,0:T(8,128)(2,1)S(1)} %add_convert_fusion.3), channel_id=1, source_target_pairs={{0,1},{1,2},{2,3},{3,4},{4,5},{5,6},{6,7},{7,0},{8,9},{9,10},{10,1... | collective-permute-start | bytes 786440 | tf_op jit(solution)/shard_map/ppermute | solution.py:343
  91.9 1.0 add_convert_fusion.2
  93.0 3.7 %rest.6 = (bf16[2,256,256]{2,1,0:T(8,128)(2,1)}, bf16[2,256,256]{2,1,0:T(8,128)(2,1)}) custom-call(bf16[256,512]{1,0:T(8,128)(2,1)} %get-tuple-element.78.z_ref, bf16[256,4096]{1,0:T(8,128)(2,1)} %wo_ref.9), custom_call_target="tpu_custom_call" | custom-call | flops 402653184 | bytes 1572864 | tf_op jit(solution)/shard_map/rest/pallas_call | solution.py:466
  96.7 1.0 add_convert_fusion.1
  97.8 3.3 %collective-permute-start.15 = (bf16[2,256,256]{2,1,0:T(8,128)(2,1)S(1)}, bf16[2,256,256]{2,1,0:T(8,128)(2,1)S(1)}, u32[]{:S(2)}, u32[]{:S(2)}) collective-permute-start(bf16[2,256,256]{2,1,0:T(8,128)(2,1)S(1)} %add_convert_fusion.1), channel_id=1, source_target_pairs={{0,1},{1,2},{2,3},{3,4},{4,5},{5,6},{6,7},{7,0},{8,9},{9,10},{10,1... | collective-permute-start | bytes 786440 | tf_op jit(solution)/shard_map/ppermute | solution.py:343
  101.1 1.0 add_convert_fusion
  102.2 2.7 %rest.7 = bf16[2,256,256]{2,1,0:T(8,128)(2,1)} custom-call(bf16[256,512]{1,0:T(8,128)(2,1)} %get-tuple-element.78.z_ref, bf16[256,4096]{1,0:T(8,128)(2,1)} %wo_ref.9), custom_call_target="tpu_custom_call" | custom-call | flops 201326592 | bytes 786432 | tf_op jit(solution)/shard_map/rest/pallas_call | solution.py:466
  104.9 4.8 %collective-permute-done.16 = bf16[2,256,256]{2,1,0:T(8,128)(2,1)S(1)} collective-permute-done((bf16[2,256,256]{2,1,0:T(8,128)(2,1)S(1)}, bf16[2,256,256]{2,1,0:T(8,128)(2,1)S(1)}, u32[]{:S(2)}, u32[]{:S(2)}) %collective-permute-start.16) | collective-permute-done | bytes 262176 | tf_op jit(solution)/shard_map/ppermute | solution.py:343
  109.7 1.0 convert_add_fusion
  111.5 4.3 %collective-permute-done.17 = bf16[256,256]{1,0:T(8,128)(2,1)S(1)} collective-permute-done((bf16[256,256]{1,0:T(8,128)(2,1)S(1)}, bf16[256,256]{1,0:T(8,128)(2,1)S(1)}, u32[]{:S(2)}, u32[]{:S(2)}) %collective-permute-start.17) | collective-permute-done | bytes 131104 | tf_op jit(solution)/shard_map/ppermute | solution.py:348
  (29 shorter events, 5.1 us)
Async XLA Ops:
  0.0 5.4 %collective-permute-start = (bf16[256,256]{1,0:T(8,128)(2,1)}, bf16[256,256]{1,0:T(8,128)(2,1)S(1)}, u32[]{:S(2)}, u32[]{:S(2)}) collective-permute-start(bf16[256,256]{1,0:T(8,128)(2,1)} %param.9), channel_id=1, source_target_pairs={{0,8},{1,9},{2,10},{3,11},{4,12},{5,13},{6,14},{7,15},{8,0},{9,1},... | collective-permute-start | bytes 393224 | tf_op jit(solution)/shard_map/ppermute | solution.py:348
  6.4 7.9 %collective-permute-start.1 = (bf16[2,256,256]{2,1,0:T(8,128)(2,1)S(1)}, bf16[2,256,256]{2,1,0:T(8,128)(2,1)S(1)}, u32[]{:S(2)}, u32[]{:S(2)}) collective-permute-start(bf16[2,256,256]{2,1,0:T(8,128)(2,1)S(1)} %pad_maximum_fusion.refs_0_), channel_id=1, source_target_pairs={{0,1},{1,2},{2,3},{3,4},{4,5},{5,6},{6,7},{7,0},{8,9},{9,10},{10,1... | collective-permute-start | bytes 786440 | tf_op jit(solution)/shard_map/ppermute | solution.py:343
  9.6 8.4 %collective-permute-start.3 = (bf16[2,256,256]{2,1,0:T(8,128)(2,1)S(1)}, bf16[2,256,256]{2,1,0:T(8,128)(2,1)S(1)}, u32[]{:S(2)}, u32[]{:S(2)}) collective-permute-start(bf16[2,256,256]{2,1,0:T(8,128)(2,1)S(1)} %pad_maximum_fusion.refs_0_), channel_id=1, source_target_pairs={{0,7},{1,0},{2,1},{3,2},{4,3},{5,4},{6,5},{7,6},{8,15},{9,8},{10,9... | collective-permute-start | bytes 786440 | tf_op jit(solution)/shard_map/ppermute | solution.py:343
  14.3 8.8 %collective-permute-start.2 = (bf16[2,256,256]{2,1,0:T(8,128)(2,1)S(1)}, bf16[2,256,256]{2,1,0:T(8,128)(2,1)S(1)}, u32[]{:S(2)}, u32[]{:S(2)}) collective-permute-start(bf16[2,256,256]{2,1,0:T(8,128)(2,1)S(1)} %collective-permute-done.1.refs_1_), channel_id=1, source_target_pairs={{0,1},{1,2},{2,3},{3,4},{4,5},{5,6},{6,7},{7,0},{8,9},{9,10},{10,1... | collective-permute-start | bytes 786440 | tf_op jit(solution)/shard_map/ppermute | solution.py:343
  18.0 8.4 %collective-permute-start.5 = (bf16[2,256,256]{2,1,0:T(8,128)(2,1)S(1)}, bf16[2,256,256]{2,1,0:T(8,128)(2,1)S(1)}, u32[]{:S(2)}, u32[]{:S(2)}) collective-permute-start(bf16[2,256,256]{2,1,0:T(8,128)(2,1)S(1)} %collective-permute-done.3.refs_2_), channel_id=1, source_target_pairs={{0,7},{1,0},{2,1},{3,2},{4,3},{5,4},{6,5},{7,6},{8,15},{9,8},{10,9... | collective-permute-start | bytes 786440 | tf_op jit(solution)/shard_map/ppermute | solution.py:343
  23.1 8.1 %collective-permute-start.4 = (bf16[2,256,256]{2,1,0:T(8,128)(2,1)S(1)}, bf16[2,256,256]{2,1,0:T(8,128)(2,1)S(1)}, u32[]{:S(2)}, u32[]{:S(2)}) collective-permute-start(bf16[2,256,256]{2,1,0:T(8,128)(2,1)S(1)} %collective-permute-done.2.refs_0_), channel_id=1, source_target_pairs={{0,1},{1,2},{2,3},{3,4},{4,5},{5,6},{6,7},{7,0},{8,9},{9,10},{10,1... | collective-permute-start | bytes 786440 | tf_op jit(solution)/shard_map/ppermute | solution.py:343
  26.4 8.1 %collective-permute-start.7 = (bf16[2,256,256]{2,1,0:T(8,128)(2,1)S(1)}, bf16[2,256,256]{2,1,0:T(8,128)(2,1)S(1)}, u32[]{:S(2)}, u32[]{:S(2)}) collective-permute-start(bf16[2,256,256]{2,1,0:T(8,128)(2,1)S(1)} %collective-permute-done.5.refs_1_), channel_id=1, source_target_pairs={{0,7},{1,0},{2,1},{3,2},{4,3},{5,4},{6,5},{7,6},{8,15},{9,8},{10,9... | collective-permute-start | bytes 786440 | tf_op jit(solution)/shard_map/ppermute | solution.py:343
  31.2 8.4 %collective-permute-start.6 = (bf16[256,256]{1,0:T(8,128)(2,1)S(1)}, bf16[256,256]{1,0:T(8,128)(2,1)S(1)}, u32[]{:S(2)}, u32[]{:S(2)}) collective-permute-start(bf16[256,256]{1,0:T(8,128)(2,1)S(1)} %slice_bitcast_fusion.2), channel_id=1, source_target_pairs={{0,1},{1,2},{2,3},{3,4},{4,5},{5,6},{6,7},{7,0},{8,9},{9,10},{10,1... | collective-permute-start | bytes 393224 | tf_op jit(solution)/shard_map/ppermute | solution.py:343
  34.5 6.4 %collective-permute-start.8 = (bf16[256,256]{1,0:T(8,128)(2,1)S(1)}, bf16[256,256]{1,0:T(8,128)(2,1)S(1)}, u32[]{:S(2)}, u32[]{:S(2)}) collective-permute-start(bf16[256,256]{1,0:T(8,128)(2,1)S(1)} %slice_bitcast_fusion.1), channel_id=1, source_target_pairs={{0,7},{1,0},{2,1},{3,2},{4,3},{5,4},{6,5},{7,6},{8,15},{9,8},{10,9... | collective-permute-start | bytes 393224 | tf_op jit(solution)/shard_map/ppermute | solution.py:343
  46.8 20.8 %all-to-all-start = ((f32[16,16,640]{2,1,0:T(8,128)}), f32[16,16,640]{2,1,0:T(8,128)S(1)}, u32[]{:S(2)}, u32[]{:S(2)}) async-start(f32[16,16,640]{2,1,0:T(8,128)} %get-tuple-element.60), calls=%async_computation | async-start | bytes 1310720 | tf_op jit(solution)/shard_map/all_to_all | solution.py:433
  72.6 5.8 %collective-permute-start.9 = (bf16[256,256]{1,0:T(8,128)(2,1)}, bf16[256,256]{1,0:T(8,128)(2,1)S(1)}, u32[]{:S(2)}, u32[]{:S(2)}) collective-permute-start(bf16[256,256]{1,0:T(8,128)(2,1)} %get-tuple-element.69), channel_id=1, source_target_pairs={{0,1},{1,2},{2,3},{3,4},{4,5},{5,6},{6,7},{7,0},{8,9},{9,10},{10,1... | collective-permute-start | bytes 393224 | tf_op jit(solution)/shard_map/ppermute | solution.py:343
  74.6 8.0 %collective-permute-start.10 = (bf16[256,256]{1,0:T(8,128)(2,1)}, bf16[256,256]{1,0:T(8,128)(2,1)S(1)}, u32[]{:S(2)}, u32[]{:S(2)}) collective-permute-start(bf16[256,256]{1,0:T(8,128)(2,1)} %get-tuple-element.71), channel_id=1, source_target_pairs={{0,7},{1,0},{2,1},{3,2},{4,3},{5,4},{6,5},{7,6},{8,15},{9,8},{10,9... | collective-permute-start | bytes 393224 | tf_op jit(solution)/shard_map/ppermute | solution.py:343
  79.4 8.0 %collective-permute-start.11 = (bf16[2,256,256]{2,1,0:T(8,128)(2,1)S(1)}, bf16[2,256,256]{2,1,0:T(8,128)(2,1)S(1)}, u32[]{:S(2)}, u32[]{:S(2)}) collective-permute-start(bf16[2,256,256]{2,1,0:T(8,128)(2,1)S(1)} %add_convert_fusion.5), channel_id=1, source_target_pairs={{0,1},{1,2},{2,3},{3,4},{4,5},{5,6},{6,7},{7,0},{8,9},{9,10},{10,1... | collective-permute-start | bytes 786440 | tf_op jit(solution)/shard_map/ppermute | solution.py:343
  83.6 8.3 %collective-permute-start.12 = (bf16[2,256,256]{2,1,0:T(8,128)(2,1)S(1)}, bf16[2,256,256]{2,1,0:T(8,128)(2,1)S(1)}, u32[]{:S(2)}, u32[]{:S(2)}) collective-permute-start(bf16[2,256,256]{2,1,0:T(8,128)(2,1)S(1)} %add_convert_fusion.4), channel_id=1, source_target_pairs={{0,7},{1,0},{2,1},{3,2},{4,3},{5,4},{6,5},{7,6},{8,15},{9,8},{10,9... | collective-permute-start | bytes 786440 | tf_op jit(solution)/shard_map/ppermute | solution.py:343
  88.4 8.3 %collective-permute-start.13 = (bf16[2,256,256]{2,1,0:T(8,128)(2,1)S(1)}, bf16[2,256,256]{2,1,0:T(8,128)(2,1)S(1)}, u32[]{:S(2)}, u32[]{:S(2)}) collective-permute-start(bf16[2,256,256]{2,1,0:T(8,128)(2,1)S(1)} %add_convert_fusion.3), channel_id=1, source_target_pairs={{0,1},{1,2},{2,3},{3,4},{4,5},{5,6},{6,7},{7,0},{8,9},{9,10},{10,1... | collective-permute-start | bytes 786440 | tf_op jit(solution)/shard_map/ppermute | solution.py:343
  92.9 8.1 %collective-permute-start.14 = (bf16[2,256,256]{2,1,0:T(8,128)(2,1)S(1)}, bf16[2,256,256]{2,1,0:T(8,128)(2,1)S(1)}, u32[]{:S(2)}, u32[]{:S(2)}) collective-permute-start(bf16[2,256,256]{2,1,0:T(8,128)(2,1)S(1)} %add_convert_fusion.2), channel_id=1, source_target_pairs={{0,7},{1,0},{2,1},{3,2},{4,3},{5,4},{6,5},{7,6},{8,15},{9,8},{10,9... | collective-permute-start | bytes 786440 | tf_op jit(solution)/shard_map/ppermute | solution.py:343
  97.8 7.2 %collective-permute-start.15 = (bf16[2,256,256]{2,1,0:T(8,128)(2,1)S(1)}, bf16[2,256,256]{2,1,0:T(8,128)(2,1)S(1)}, u32[]{:S(2)}, u32[]{:S(2)}) collective-permute-start(bf16[2,256,256]{2,1,0:T(8,128)(2,1)S(1)} %add_convert_fusion.1), channel_id=1, source_target_pairs={{0,1},{1,2},{2,3},{3,4},{4,5},{5,6},{6,7},{7,0},{8,9},{9,10},{10,1... | collective-permute-start | bytes 786440 | tf_op jit(solution)/shard_map/ppermute | solution.py:343
  102.1 7.7 %collective-permute-start.16 = (bf16[2,256,256]{2,1,0:T(8,128)(2,1)S(1)}, bf16[2,256,256]{2,1,0:T(8,128)(2,1)S(1)}, u32[]{:S(2)}, u32[]{:S(2)}) collective-permute-start(bf16[2,256,256]{2,1,0:T(8,128)(2,1)S(1)} %add_convert_fusion), channel_id=1, source_target_pairs={{0,7},{1,0},{2,1},{3,2},{4,3},{5,4},{6,5},{7,6},{8,15},{9,8},{10,9... | collective-permute-start | bytes 786440 | tf_op jit(solution)/shard_map/ppermute | solution.py:343
  110.8 5.1 %collective-permute-start.17 = (bf16[256,256]{1,0:T(8,128)(2,1)S(1)}, bf16[256,256]{1,0:T(8,128)(2,1)S(1)}, u32[]{:S(2)}, u32[]{:S(2)}) collective-permute-start(bf16[256,256]{1,0:T(8,128)(2,1)S(1)} %fusion.2), channel_id=1, source_target_pairs={{0,8},{1,9},{2,10},{3,11},{4,12},{5,13},{6,14},{7,15},{8,0},{9,1},... | collective-permute-start | bytes 393224 | tf_op jit(solution)/shard_map/ppermute | solution.py:348

commit v6 on v5

--- a/solution.py
+++ b/solution.py
@@ -396,12 +396,11 @@
     carried = project([up2, down2], pair_slots((-2, 2)), far_memory(*carried))
     up3, carried = lax.optimization_barrier((up3, carried))
     last_up, last_down = turn(up3[0], 1), turn(down3[1], -1)
-    carried = project([up3, down3], pair_slots((-3, 3)), far_memory(*carried))
-
-    slots = ((0, None, 0, -4), (1, None, 1, 4))
+
+    slots = pair_slots((-3, 3)) + ((2, None, 0, -4), (3, None, 1, 4))
     send, sv, gates, edge = pl.pallas_call(
-        functools.partial(states_kernel, slots, 2),
-        in_specs=[remote, remote, whole(gain.shape), remote, remote, remote, remote]
+        functools.partial(states_kernel, slots, 4),
+        in_specs=[remote] * 4 + [whole(gain.shape), remote, remote, remote, remote]
         + [whole(value_taps.shape), whole(powers.shape)],
         out_specs=[
             whole((places, modes, 2 * chans + 128)),
@@ -419,14 +418,14 @@
             pltpu.VMEM((2, rows, 2 * chans), f32),
             pltpu.VMEM((rows, 128), f32),
             pltpu.VMEM((rows + 16, chans), f32),
-            pltpu.VMEM((2, rows, chans), bf16),
-            pltpu.VMEM((2, 2, chans, 2 * chans), bf16),
-            pltpu.SemaphoreType.DMA((4, 5)),
+            pltpu.VMEM((len(slots), rows, chans), bf16),
+            pltpu.VMEM((len(slots), 2, chans, 2 * chans), bf16),
+            pltpu.SemaphoreType.DMA((len(slots) + 1, 5)),
         ],
         compiler_params=params,
         name="states",
     )(
-        last_up, last_down, gain, value_weight, gate_weight, *far_memory(*carried), value_taps,
+        up3, down3, last_up, last_down, gain, value_weight, gate_weight, *far_memory(*carried), value_taps,
         *far_memory(powers),
     )
 

time: 117 us -> 124 us (1.060)
  the two profiles are of different devices: /device:TPU:96 before, /device:TPU:4 now
where the time goes in v6:
time: 124 us; the launch traced here: 121 us
  Pallas kernels  43.6 us (35%)
  starting transfers between devices  37.7 us (30%)
  waiting for transfers between devices  31.2 us (25%)
  other arithmetic  8.67 us (7%)
    ppermute x16, starting transfers between devices, turn(): lax.ppermute(a, 'tp', [(c * ring + i, c * ring + (i + hop) % ring) for c...  27.8 us
    ppermute x16, waiting for transfers between devices, turn(): lax.ppermute(a, 'tp', [(c * ring + i, c * ring + (i + hop) % ring) for c...  18.5 us
    pallas_call x4, Pallas kernels, rest(): pl.pallas_call(functools.partial(rest_kernel, chunks), in_specs=[remote,...  13.8 us
    pallas_call x2, Pallas kernels, project(): pl.pallas_call(functools.partial(early_kernel, slots, len(arrays), len(ca...  9.84 us
    ppermute x2, waiting for transfers between devices, across(): return lax.ppermute(a, 'tp', [(i, (i + ring) % tp) for i in range(tp)])  8.02 us
    all_to_all x1, starting transfers between devices, body(): recv = lax.all_to_all(send, 'seq', split_axis=0, concat_axis=0)  7.47 us
    pallas_call x1, Pallas kernels, body(): pl.pallas_call(functools.partial(states_kernel, slots, 4), in_specs=[remo...  7.06 us
    pallas_call x1, Pallas kernels, body(): pl.pallas_call(local_kernel, out_shape=shape((2, tiles, T, chans), f32),...  6.14 us
  transfers between devices with their start and end apart: 19, of which 9 were waited for; matrix products, arithmetic and copies ran while one was open for 5% of the time, Pallas kernels for 26%

profile of v6, /device:TPU:4, one launch (start us, length us, event | category | flops | bytes accessed | tf_op | source)
XLA Modules:
  0.0 121.4 jit_solution(15030421213404942172)
XLA Ops:
  0.0 1.2 collective-permute-start
  1.2 4.2 %collective-permute-done = bf16[256,256]{1,0:T(8,128)(2,1)S(1)} collective-permute-done((bf16[256,256]{1,0:T(8,128)(2,1)}, bf16[256,256]{1,0:T(8,128)(2,1)S(1)}, u32[]{:S(2)}, u32[]{:S(2)}) %collective-permute-start) | collective-permute-done | bytes 131104 | tf_op jit(solution)/shard_map/ppermute | solution.py:348
  6.4 5.9 %collective-permute-start.3 = (bf16[2,256,256]{2,1,0:T(8,128)(2,1)S(1)}, bf16[2,256,256]{2,1,0:T(8,128)(2,1)S(1)}, u32[]{:S(2)}, u32[]{:S(2)}) collective-permute-start(bf16[2,256,256]{2,1,0:T(8,128)(2,1)S(1)} %pad_maximum_fusion.refs_0_), channel_id=1, source_target_pairs={{0,7},{1,0},{2,1},{3,2},{4,3},{5,4},{6,5},{7,6},{8,15},{9,8},{10,9... | collective-permute-start | bytes 786440 | tf_op jit(solution)/shard_map/ppermute | solution.py:343
  12.3 4.7 %collective-permute-done.3.refs_2_ = bf16[2,256,256]{2,1,0:T(8,128)(2,1)S(1)} collective-permute-done((bf16[2,256,256]{2,1,0:T(8,128)(2,1)S(1)}, bf16[2,256,256]{2,1,0:T(8,128)(2,1)S(1)}, u32[]{:S(2)}, u32[]{:S(2)}) %collective-permute-start.3) | collective-permute-done | bytes 262176 | tf_op jit(solution)/shard_map/ppermute | solution.py:343
  17.0 3.7 %collective-permute-start.5 = (bf16[2,256,256]{2,1,0:T(8,128)(2,1)S(1)}, bf16[2,256,256]{2,1,0:T(8,128)(2,1)S(1)}, u32[]{:S(2)}, u32[]{:S(2)}) collective-permute-start(bf16[2,256,256]{2,1,0:T(8,128)(2,1)S(1)} %collective-permute-done.3.refs_2_), channel_id=1, source_target_pairs={{0,7},{1,0},{2,1},{3,2},{4,3},{5,4},{6,5},{7,6},{8,15},{9,8},{10,9... | collective-permute-start | bytes 786440 | tf_op jit(solution)/shard_map/ppermute | solution.py:343
  20.7 1.7 %tables.1 = (f32[18,16,256]{2,1,0:T(8,128)}, f32[40,256]{1,0:T(8,128)}, f32[16,16,256]{2,1,0:T(8,128)}, f32[16,16,256]{2,1,0:T(8,128)}) custom-call(f32[16,256]{1,0:T(8,128)} %rates_ref.3, f32[16,256]{1,0:T(8,128)} %residues_ref.1), custom_call_target="tpu_custom_call" | custom-call | tf_op jit(solution)/shard_map/tables/pallas_call | solution.py:351
  22.4 2.2 %collective-permute-done.5.refs_1_ = bf16[2,256,256]{2,1,0:T(8,128)(2,1)S(1)} collective-permute-done((bf16[2,256,256]{2,1,0:T(8,128)(2,1)S(1)}, bf16[2,256,256]{2,1,0:T(8,128)(2,1)S(1)}, u32[]{:S(2)}, u32[]{:S(2)}) %collective-permute-start.5) | collective-permute-done | bytes 262176 | tf_op jit(solution)/shard_map/ppermute | solution.py:343
  24.6 3.7 %collective-permute-start.6 = (bf16[2,256,256]{2,1,0:T(8,128)(2,1)S(1)}, bf16[2,256,256]{2,1,0:T(8,128)(2,1)S(1)}, u32[]{:S(2)}, u32[]{:S(2)}) collective-permute-start(bf16[2,256,256]{2,1,0:T(8,128)(2,1)S(1)} %collective-permute-done.5.refs_1_), channel_id=1, source_target_pairs={{0,7},{1,0},{2,1},{3,2},{4,3},{5,4},{6,5},{7,6},{8,15},{9,8},{10,9... | collective-permute-start | bytes 786440 | tf_op jit(solution)/shard_map/ppermute | solution.py:343
  28.3 5.1 %project.2 = (f32[2,256,512]{2,1,0:T(8,128)}, f32[256,128]{1,0:T(8,128)}) custom-call(bf16[2,256,256]{2,1,0:T(8,128)(2,1)S(1)} %pad_maximum_fusion.refs_0_, bf16[2,256,256]{2,1,0:T(8,128)(2,1)S(1)} %collective-permute-done.1.refs_1_, bf16[2,256,256]{2,1,0:T(8,128)(2,1)S(1)} %collective-permute-done.3.refs_2_, f32[16,1,256]{2,1,0:T(1,128)} %bitcast.17, ...), custom_call_target="tpu_custom_call" | custom-call | flops 1006632960 | bytes 3932160 | tf_op jit(solution)/shard_map/project/pallas_call | solution.py:367
  33.4 4.8 %project.3 = (f32[2,256,512]{2,1,0:T(8,128)}, f32[256,128]{1,0:T(8,128)}) custom-call(bf16[2,256,256]{2,1,0:T(8,128)(2,1)S(1)} %collective-permute-done.2.refs_0_, bf16[2,256,256]{2,1,0:T(8,128)(2,1)S(1)} %collective-permute-done.5.refs_1_, f32[16,1,256]{2,1,0:T(1,128)} %bitcast.18, bf16[4096,256]{1,0:T(8,128)(2,1)} %refs_5_.3, bf16[4096,256]{1,0:T(8,128)(2,1)} %refs_6_.1, ...), custom_call_target="tpu_custom_call" | custom-call | flops 671088640 | bytes 2621440 | tf_op jit(solution)/shard_map/project/pallas_call | solution.py:367
  38.3 3.3 %collective-permute-start.8 = (bf16[256,256]{1,0:T(8,128)(2,1)S(1)}, bf16[256,256]{1,0:T(8,128)(2,1)S(1)}, u32[]{:S(2)}, u32[]{:S(2)}) collective-permute-start(bf16[256,256]{1,0:T(8,128)(2,1)S(1)} %slice_bitcast_fusion.1), channel_id=1, source_target_pairs={{0,7},{1,0},{2,1},{3,2},{4,3},{5,4},{6,5},{7,6},{8,15},{9,8},{10,9... | collective-permute-start | bytes 393224 | tf_op jit(solution)/shard_map/ppermute | solution.py:343
  41.9 2.2 %collective-permute-done.8.refs_3_ = bf16[256,256]{1,0:T(8,128)(2,1)S(1)} collective-permute-done((bf16[256,256]{1,0:T(8,128)(2,1)S(1)}, bf16[256,256]{1,0:T(8,128)(2,1)S(1)}, u32[]{:S(2)}, u32[]{:S(2)}) %collective-permute-start.8) | collective-permute-done | bytes 131104 | tf_op jit(solution)/shard_map/ppermute | solution.py:343
  44.1 3.9 %collective-permute-done.7.refs_2_ = bf16[256,256]{1,0:T(8,128)(2,1)S(1)} collective-permute-done((bf16[256,256]{1,0:T(8,128)(2,1)S(1)}, bf16[256,256]{1,0:T(8,128)(2,1)S(1)}, u32[]{:S(2)}, u32[]{:S(2)}) %collective-permute-start.7) | collective-permute-done | bytes 131104 | tf_op jit(solution)/shard_map/ppermute | solution.py:343
  48.0 7.1 %states.1 = (f32[16,16,640]{2,1,0:T(8,128)}, f32[2,16,16,256]{3,2,1,0:T(8,128)}, f32[256,512]{1,0:T(8,128)}, f32[2,2,8,256]{3,2,1,0:T(8,128)}) custom-call(bf16[2,256,256]{2,1,0:T(8,128)(2,1)S(1)} %collective-permute-done.4.refs_0_, bf16[2,256,256]{2,1,0:T(8,128)(2,1)S(1)} %collective-permute-done.6.refs_1_, ...), custom_call_target="tpu_custom_call" | custom-call | tf_op jit(solution)/shard_map/states/pallas_call | solution.py:401
  55.1 7.5 %all-to-all-start = ((f32[16,16,640]{2,1,0:T(8,128)}), f32[16,16,640]{2,1,0:T(8,128)S(1)}, u32[]{:S(2)}, u32[]{:S(2)}) async-start(f32[16,16,640]{2,1,0:T(8,128)} %get-tuple-element.56), calls=%async_computation | async-start | bytes 1310720 | tf_op jit(solution)/shard_map/all_to_all | solution.py:432
  62.6 6.1 %local.1.local_ref = f32[2,16,16,256]{3,2,1,0:T(8,128)} custom-call(f32[2,16,16,256]{3,2,1,0:T(8,128)} %get-tuple-element.57.sv_ref, f32[2,2,8,256]{3,2,1,0:T(8,128)} %get-tuple-element.58.edge_ref, f32[18,16,256]{2,1,0:T(8,128)} %get-tuple-element.55.refs_10_.pow_ref, f32[40,256]{1,0:T(8,128)} %get-tuple-element.59.near_ref, ...), custom_call_target="tpu_custom_call" | custom-call | tf_op jit(solution)/shard_map/local/pallas_call | solution.py:433
  68.7 4.8 %all-to-all-done.recv_ref = f32[16,16,640]{2,1,0:T(8,128)S(1)} async-done(((f32[16,16,640]{2,1,0:T(8,128)}), f32[16,16,640]{2,1,0:T(8,128)S(1)}, u32[]{:S(2)}, u32[]{:S(2)}) %all-to-all-start) | async-done | bytes 655392 | tf_op jit(solution)/shard_map/all_to_all | solution.py:432
  73.5 5.0 %gated.1 = (bf16[256,512]{1,0:T(8,128)(2,1)}, bf16[256,256]{1,0:T(8,128)(2,1)}, bf16[256,256]{1,0:T(8,128)(2,1)}) custom-call(f32[16,16,640]{2,1,0:T(8,128)S(1)} %all-to-all-done.recv_ref, f32[2,16,16,256]{3,2,1,0:T(8,128)} %local.1.local_ref, f32[256,512]{1,0:T(8,128)} %get-tuple-element.62.gates_ref, f32[3,256]{1,0:T(4,128)} %gt_ref.1, ...), custom_call_target="tpu_custom_call" | custom-call | tf_op jit(solution)/shard_map/gated/pallas_call | solution.py:448
  78.5 2.0 %collective-permute-start.9 = (bf16[256,256]{1,0:T(8,128)(2,1)}, bf16[256,256]{1,0:T(8,128)(2,1)S(1)}, u32[]{:S(2)}, u32[]{:S(2)}) collective-permute-start(bf16[256,256]{1,0:T(8,128)(2,1)} %get-tuple-element.65), channel_id=1, source_target_pairs={{0,1},{1,2},{2,3},{3,4},{4,5},{5,6},{6,7},{7,0},{8,9},{9,10},{10,1... | collective-permute-start | bytes 393224 | tf_op jit(solution)/shard_map/ppermute | solution.py:343
  80.5 3.7 %rest.4 = (bf16[2,256,256]{2,1,0:T(8,128)(2,1)}, bf16[2,256,256]{2,1,0:T(8,128)(2,1)}) custom-call(bf16[256,512]{1,0:T(8,128)(2,1)} %get-tuple-element.74.z_ref, bf16[256,4096]{1,0:T(8,128)(2,1)} %wo_ref.9), custom_call_target="tpu_custom_call" | custom-call | flops 402653184 | bytes 1572864 | tf_op jit(solution)/shard_map/rest/pallas_call | solution.py:465
  85.3 1.6 %collective-permute-start.12 = (bf16[2,256,256]{2,1,0:T(8,128)(2,1)S(1)}, bf16[2,256,256]{2,1,0:T(8,128)(2,1)S(1)}, u32[]{:S(2)}, u32[]{:S(2)}) collective-permute-start(bf16[2,256,256]{2,1,0:T(8,128)(2,1)S(1)} %add_convert_fusion.4), channel_id=1, source_target_pairs={{0,7},{1,0},{2,1},{3,2},{4,3},{5,4},{6,5},{7,6},{8,15},{9,8},{10,9... | collective-permute-start | bytes 786440 | tf_op jit(solution)/shard_map/ppermute | solution.py:343
  88.6 3.7 %rest.5 = (bf16[2,256,256]{2,1,0:T(8,128)(2,1)}, bf16[2,256,256]{2,1,0:T(8,128)(2,1)}) custom-call(bf16[256,512]{1,0:T(8,128)(2,1)} %get-tuple-element.74.z_ref, bf16[256,4096]{1,0:T(8,128)(2,1)} %wo_ref.9), custom_call_target="tpu_custom_call" | custom-call | flops 402653184 | bytes 1572864 | tf_op jit(solution)/shard_map/rest/pallas_call | solution.py:465
  93.9 2.9 %collective-permute-start.14 = (bf16[2,256,256]{2,1,0:T(8,128)(2,1)S(1)}, bf16[2,256,256]{2,1,0:T(8,128)(2,1)S(1)}, u32[]{:S(2)}, u32[]{:S(2)}) collective-permute-start(bf16[2,256,256]{2,1,0:T(8,128)(2,1)S(1)} %add_convert_fusion.2), channel_id=1, source_target_pairs={{0,7},{1,0},{2,1},{3,2},{4,3},{5,4},{6,5},{7,6},{8,15},{9,8},{10,9... | collective-permute-start | bytes 786440 | tf_op jit(solution)/shard_map/ppermute | solution.py:343
  96.8 1.0 add_convert_fusion.3
  97.9 3.7 %rest.6 = (bf16[2,256,256]{2,1,0:T(8,128)(2,1)}, bf16[2,256,256]{2,1,0:T(8,128)(2,1)}) custom-call(bf16[256,512]{1,0:T(8,128)(2,1)} %get-tuple-element.74.z_ref, bf16[256,4096]{1,0:T(8,128)(2,1)} %wo_ref.9), custom_call_target="tpu_custom_call" | custom-call | flops 402653184 | bytes 1572864 | tf_op jit(solution)/shard_map/rest/pallas_call | solution.py:465
  101.6 1.0 add_convert_fusion
  102.7 3.3 %collective-permute-start.16 = (bf16[2,256,256]{2,1,0:T(8,128)(2,1)S(1)}, bf16[2,256,256]{2,1,0:T(8,128)(2,1)S(1)}, u32[]{:S(2)}, u32[]{:S(2)}) collective-permute-start(bf16[2,256,256]{2,1,0:T(8,128)(2,1)S(1)} %add_convert_fusion), channel_id=1, source_target_pairs={{0,7},{1,0},{2,1},{3,2},{4,3},{5,4},{6,5},{7,6},{8,15},{9,8},{10,9... | collective-permute-start | bytes 786440 | tf_op jit(solution)/shard_map/ppermute | solution.py:343
  107.1 2.7 %rest.7 = bf16[2,256,256]{2,1,0:T(8,128)(2,1)} custom-call(bf16[256,512]{1,0:T(8,128)(2,1)} %get-tuple-element.74.z_ref, bf16[256,4096]{1,0:T(8,128)(2,1)} %wo_ref.9), custom_call_target="tpu_custom_call" | custom-call | flops 201326592 | bytes 786432 | tf_op jit(solution)/shard_map/rest/pallas_call | solution.py:465
  109.9 4.8 %collective-permute-done.15 = bf16[2,256,256]{2,1,0:T(8,128)(2,1)S(1)} collective-permute-done((bf16[2,256,256]{2,1,0:T(8,128)(2,1)S(1)}, bf16[2,256,256]{2,1,0:T(8,128)(2,1)S(1)}, u32[]{:S(2)}, u32[]{:S(2)}) %collective-permute-start.15) | collective-permute-done | bytes 262176 | tf_op jit(solution)/shard_map/ppermute | solution.py:343
  114.6 1.0 convert_add_fusion
  115.7 1.3 %collective-permute-start.17 = (bf16[256,256]{1,0:T(8,128)(2,1)S(1)}, bf16[256,256]{1,0:T(8,128)(2,1)S(1)}, u32[]{:S(2)}, u32[]{:S(2)}) collective-permute-start(bf16[256,256]{1,0:T(8,128)(2,1)S(1)} %fusion.2), channel_id=1, source_target_pairs={{0,8},{1,9},{2,10},{3,11},{4,12},{5,13},{6,14},{7,15},{8,0},{9,1},... | collective-permute-start | bytes 393224 | tf_op jit(solution)/shard_map/ppermute | solution.py:348
  117.0 3.8 %collective-permute-done.17 = bf16[256,256]{1,0:T(8,128)(2,1)S(1)} collective-permute-done((bf16[256,256]{1,0:T(8,128)(2,1)S(1)}, bf16[256,256]{1,0:T(8,128)(2,1)S(1)}, u32[]{:S(2)}, u32[]{:S(2)}) %collective-permute-start.17) | collective-permute-done | bytes 131104 | tf_op jit(solution)/shard_map/ppermute | solution.py:348
  (28 shorter events, 7.7 us)
Async XLA Ops:
  0.0 5.4 %collective-permute-start = (bf16[256,256]{1,0:T(8,128)(2,1)}, bf16[256,256]{1,0:T(8,128)(2,1)S(1)}, u32[]{:S(2)}, u32[]{:S(2)}) collective-permute-start(bf16[256,256]{1,0:T(8,128)(2,1)} %param.9), channel_id=1, source_target_pairs={{0,8},{1,9},{2,10},{3,11},{4,12},{5,13},{6,14},{7,15},{8,0},{9,1},... | collective-permute-start | bytes 393224 | tf_op jit(solution)/shard_map/ppermute | solution.py:348
  6.4 10.6 %collective-permute-start.3 = (bf16[2,256,256]{2,1,0:T(8,128)(2,1)S(1)}, bf16[2,256,256]{2,1,0:T(8,128)(2,1)S(1)}, u32[]{:S(2)}, u32[]{:S(2)}) collective-permute-start(bf16[2,256,256]{2,1,0:T(8,128)(2,1)S(1)} %pad_maximum_fusion.refs_0_), channel_id=1, source_target_pairs={{0,7},{1,0},{2,1},{3,2},{4,3},{5,4},{6,5},{7,6},{8,15},{9,8},{10,9... | collective-permute-start | bytes 786440 | tf_op jit(solution)/shard_map/ppermute | solution.py:343
  12.3 10.1 %collective-permute-start.1 = (bf16[2,256,256]{2,1,0:T(8,128)(2,1)S(1)}, bf16[2,256,256]{2,1,0:T(8,128)(2,1)S(1)}, u32[]{:S(2)}, u32[]{:S(2)}) collective-permute-start(bf16[2,256,256]{2,1,0:T(8,128)(2,1)S(1)} %pad_maximum_fusion.refs_0_), channel_id=1, source_target_pairs={{0,1},{1,2},{2,3},{3,4},{4,5},{5,6},{6,7},{7,0},{8,9},{9,10},{10,1... | collective-permute-start | bytes 786440 | tf_op jit(solution)/shard_map/ppermute | solution.py:343
  17.0 7.6 %collective-permute-start.5 = (bf16[2,256,256]{2,1,0:T(8,128)(2,1)S(1)}, bf16[2,256,256]{2,1,0:T(8,128)(2,1)S(1)}, u32[]{:S(2)}, u32[]{:S(2)}) collective-permute-start(bf16[2,256,256]{2,1,0:T(8,128)(2,1)S(1)} %collective-permute-done.3.refs_2_), channel_id=1, source_target_pairs={{0,7},{1,0},{2,1},{3,2},{4,3},{5,4},{6,5},{7,6},{8,15},{9,8},{10,9... | collective-permute-start | bytes 786440 | tf_op jit(solution)/shard_map/ppermute | solution.py:343
  22.4 10.9 %collective-permute-start.2 = (bf16[2,256,256]{2,1,0:T(8,128)(2,1)S(1)}, bf16[2,256,256]{2,1,0:T(8,128)(2,1)S(1)}, u32[]{:S(2)}, u32[]{:S(2)}) collective-permute-start(bf16[2,256,256]{2,1,0:T(8,128)(2,1)S(1)} %collective-permute-done.1.refs_1_), channel_id=1, source_target_pairs={{0,1},{1,2},{2,3},{3,4},{4,5},{5,6},{6,7},{7,0},{8,9},{9,10},{10,1... | collective-permute-start | bytes 786440 | tf_op jit(solution)/shard_map/ppermute | solution.py:343
  24.6 13.7 %collective-permute-start.6 = (bf16[2,256,256]{2,1,0:T(8,128)(2,1)S(1)}, bf16[2,256,256]{2,1,0:T(8,128)(2,1)S(1)}, u32[]{:S(2)}, u32[]{:S(2)}) collective-permute-start(bf16[2,256,256]{2,1,0:T(8,128)(2,1)S(1)} %collective-permute-done.5.refs_1_), channel_id=1, source_target_pairs={{0,7},{1,0},{2,1},{3,2},{4,3},{5,4},{6,5},{7,6},{8,15},{9,8},{10,9... | collective-permute-start | bytes 786440 | tf_op jit(solution)/shard_map/ppermute | solution.py:343
  33.4 8.2 %collective-permute-start.4 = (bf16[2,256,256]{2,1,0:T(8,128)(2,1)S(1)}, bf16[2,256,256]{2,1,0:T(8,128)(2,1)S(1)}, u32[]{:S(2)}, u32[]{:S(2)}) collective-permute-start(bf16[2,256,256]{2,1,0:T(8,128)(2,1)S(1)} %collective-permute-done.2.refs_0_), channel_id=1, source_target_pairs={{0,1},{1,2},{2,3},{3,4},{4,5},{5,6},{6,7},{7,0},{8,9},{9,10},{10,1... | collective-permute-start | bytes 786440 | tf_op jit(solution)/shard_map/ppermute | solution.py:343
  38.3 5.8 %collective-permute-start.8 = (bf16[256,256]{1,0:T(8,128)(2,1)S(1)}, bf16[256,256]{1,0:T(8,128)(2,1)S(1)}, u32[]{:S(2)}, u32[]{:S(2)}) collective-permute-start(bf16[256,256]{1,0:T(8,128)(2,1)S(1)} %slice_bitcast_fusion.1), channel_id=1, source_target_pairs={{0,7},{1,0},{2,1},{3,2},{4,3},{5,4},{6,5},{7,6},{8,15},{9,8},{10,9... | collective-permute-start | bytes 393224 | tf_op jit(solution)/shard_map/ppermute | solution.py:343
  41.6 6.4 %collective-permute-start.7 = (bf16[256,256]{1,0:T(8,128)(2,1)S(1)}, bf16[256,256]{1,0:T(8,128)(2,1)S(1)}, u32[]{:S(2)}, u32[]{:S(2)}) collective-permute-start(bf16[256,256]{1,0:T(8,128)(2,1)S(1)} %slice_bitcast_fusion.2), channel_id=1, source_target_pairs={{0,1},{1,2},{2,3},{3,4},{4,5},{5,6},{6,7},{7,0},{8,9},{9,10},{10,1... | collective-permute-start | bytes 393224 | tf_op jit(solution)/shard_map/ppermute | solution.py:343
  55.1 18.4 %all-to-all-start = ((f32[16,16,640]{2,1,0:T(8,128)}), f32[16,16,640]{2,1,0:T(8,128)S(1)}, u32[]{:S(2)}, u32[]{:S(2)}) async-start(f32[16,16,640]{2,1,0:T(8,128)} %get-tuple-element.56), calls=%async_computation | async-start | bytes 1310720 | tf_op jit(solution)/shard_map/all_to_all | solution.py:432
  78.4 5.8 %collective-permute-start.10 = (bf16[256,256]{1,0:T(8,128)(2,1)}, bf16[256,256]{1,0:T(8,128)(2,1)S(1)}, u32[]{:S(2)}, u32[]{:S(2)}) collective-permute-start(bf16[256,256]{1,0:T(8,128)(2,1)} %get-tuple-element.67), channel_id=1, source_target_pairs={{0,7},{1,0},{2,1},{3,2},{4,3},{5,4},{6,5},{7,6},{8,15},{9,8},{10,9... | collective-permute-start | bytes 393224 | tf_op jit(solution)/shard_map/ppermute | solution.py:343
  78.5 8.3 %collective-permute-start.9 = (bf16[256,256]{1,0:T(8,128)(2,1)}, bf16[256,256]{1,0:T(8,128)(2,1)S(1)}, u32[]{:S(2)}, u32[]{:S(2)}) collective-permute-start(bf16[256,256]{1,0:T(8,128)(2,1)} %get-tuple-element.65), channel_id=1, source_target_pairs={{0,1},{1,2},{2,3},{3,4},{4,5},{5,6},{6,7},{7,0},{8,9},{9,10},{10,1... | collective-permute-start | bytes 393224 | tf_op jit(solution)/shard_map/ppermute | solution.py:343
  85.3 7.7 %collective-permute-start.12 = (bf16[2,256,256]{2,1,0:T(8,128)(2,1)S(1)}, bf16[2,256,256]{2,1,0:T(8,128)(2,1)S(1)}, u32[]{:S(2)}, u32[]{:S(2)}) collective-permute-start(bf16[2,256,256]{2,1,0:T(8,128)(2,1)S(1)} %add_convert_fusion.4), channel_id=1, source_target_pairs={{0,7},{1,0},{2,1},{3,2},{4,3},{5,4},{6,5},{7,6},{8,15},{9,8},{10,9... | collective-permute-start | bytes 786440 | tf_op jit(solution)/shard_map/ppermute | solution.py:343
  87.8 9.0 %collective-permute-start.11 = (bf16[2,256,256]{2,1,0:T(8,128)(2,1)S(1)}, bf16[2,256,256]{2,1,0:T(8,128)(2,1)S(1)}, u32[]{:S(2)}, u32[]{:S(2)}) collective-permute-start(bf16[2,256,256]{2,1,0:T(8,128)(2,1)S(1)} %add_convert_fusion.5), channel_id=1, source_target_pairs={{0,1},{1,2},{2,3},{3,4},{4,5},{5,6},{6,7},{7,0},{8,9},{9,10},{10,1... | collective-permute-start | bytes 786440 | tf_op jit(solution)/shard_map/ppermute | solution.py:343
  93.9 7.7 %collective-permute-start.14 = (bf16[2,256,256]{2,1,0:T(8,128)(2,1)S(1)}, bf16[2,256,256]{2,1,0:T(8,128)(2,1)S(1)}, u32[]{:S(2)}, u32[]{:S(2)}) collective-permute-start(bf16[2,256,256]{2,1,0:T(8,128)(2,1)S(1)} %add_convert_fusion.2), channel_id=1, source_target_pairs={{0,7},{1,0},{2,1},{3,2},{4,3},{5,4},{6,5},{7,6},{8,15},{9,8},{10,9... | collective-permute-start | bytes 786440 | tf_op jit(solution)/shard_map/ppermute | solution.py:343
  97.8 8.1 %collective-permute-start.13 = (bf16[2,256,256]{2,1,0:T(8,128)(2,1)S(1)}, bf16[2,256,256]{2,1,0:T(8,128)(2,1)S(1)}, u32[]{:S(2)}, u32[]{:S(2)}) collective-permute-start(bf16[2,256,256]{2,1,0:T(8,128)(2,1)S(1)} %add_convert_fusion.3), channel_id=1, source_target_pairs={{0,1},{1,2},{2,3},{3,4},{4,5},{5,6},{6,7},{7,0},{8,9},{9,10},{10,1... | collective-permute-start | bytes 786440 | tf_op jit(solution)/shard_map/ppermute | solution.py:343
  102.7 7.2 %collective-permute-start.16 = (bf16[2,256,256]{2,1,0:T(8,128)(2,1)S(1)}, bf16[2,256,256]{2,1,0:T(8,128)(2,1)S(1)}, u32[]{:S(2)}, u32[]{:S(2)}) collective-permute-start(bf16[2,256,256]{2,1,0:T(8,128)(2,1)S(1)} %add_convert_fusion), channel_id=1, source_target_pairs={{0,7},{1,0},{2,1},{3,2},{4,3},{5,4},{6,5},{7,6},{8,15},{9,8},{10,9... | collective-permute-start | bytes 786440 | tf_op jit(solution)/shard_map/ppermute | solution.py:343
  107.0 7.7 %collective-permute-start.15 = (bf16[2,256,256]{2,1,0:T(8,128)(2,1)S(1)}, bf16[2,256,256]{2,1,0:T(8,128)(2,1)S(1)}, u32[]{:S(2)}, u32[]{:S(2)}) collective-permute-start(bf16[2,256,256]{2,1,0:T(8,128)(2,1)S(1)} %add_convert_fusion.1), channel_id=1, source_target_pairs={{0,1},{1,2},{2,3},{3,4},{4,5},{5,6},{6,7},{7,0},{8,9},{9,10},{10,1... | collective-permute-start | bytes 786440 | tf_op jit(solution)/shard_map/ppermute | solution.py:343
  115.7 5.1 %collective-permute-start.17 = (bf16[256,256]{1,0:T(8,128)(2,1)S(1)}, bf16[256,256]{1,0:T(8,128)(2,1)S(1)}, u32[]{:S(2)}, u32[]{:S(2)}) collective-permute-start(bf16[256,256]{1,0:T(8,128)(2,1)S(1)} %fusion.2), channel_id=1, source_target_pairs={{0,8},{1,9},{2,10},{3,11},{4,12},{5,13},{6,14},{7,15},{8,0},{9,1},... | collective-permute-start | bytes 393224 | tf_op jit(solution)/shard_map/ppermute | solution.py:348
